TPU v7x, 32 devices: a whole 2x2x4 slice. The times are simulated.
32 devices in a mesh: dp: 4 (over x, core), ctx: 4 (over z), fsdp: 2 (over y).
Axes of the slice: x: 2, y: 2, z: 4, core: 2. Of those that a mesh axis runs over, the one named last changes fastest.
Arguments:
- hidden: bfloat16 [8, 512, 2048], P(('dp', 'fsdp'), 'ctx'), may hold values from -6 to 6
- cotangent: bfloat16 [8, 512, 2048], P(('dp', 'fsdp'), 'ctx'), may hold values from -6 to 6
- ln1_gain: bfloat16 [2048], P(('ctx', 'fsdp')), may hold values from 0.099609375 to 1.8984375
- ln1_bias: bfloat16 [2048], P(('ctx', 'fsdp')), may hold values from -3 to 3
- ln2_gain: bfloat16 [2048], P(('ctx', 'fsdp')), may hold values from 0.099609375 to 1.8984375
- ln2_bias: bfloat16 [2048], P(('ctx', 'fsdp')), may hold values from -3 to 3
- w_qkv: bfloat16 [2048, 6144], P(None, ('ctx', 'fsdp')), may hold values from -1.5 to 1.5
- b_qkv: bfloat16 [6144], P(('ctx', 'fsdp')), may hold values from -3 to 3
- w_out: bfloat16 [2048, 2048], P(None, ('ctx', 'fsdp')), may hold values from -0.75 to 0.75
- b_out: bfloat16 [2048], P(('ctx', 'fsdp')), may hold values from -3 to 3
- w_fc1: bfloat16 [2048, 8192], P(None, ('ctx', 'fsdp')), may hold values from -0.125 to 0.125
- b_fc1: bfloat16 [8192], P(('ctx', 'fsdp')), may hold values from -3 to 3
- w_fc2: bfloat16 [8192, 2048], P(None, ('ctx', 'fsdp')), may hold values from -0.0625 to 0.0625
- b_fc2: bfloat16 [2048], P(('ctx', 'fsdp')), may hold values from -3 to 3
Outputs:
- output: bfloat16 [8, 512, 2048], P(('dp', 'fsdp'), 'ctx')
- input_grad: bfloat16 [8, 512, 2048], P(('dp', 'fsdp'), 'ctx')
- ln1_gain_grad: float32 [2048], P(('ctx', 'fsdp'))
- ln1_bias_grad: float32 [2048], P(('ctx', 'fsdp'))
- ln2_gain_grad: float32 [2048], P(('ctx', 'fsdp'))
- ln2_bias_grad: float32 [2048], P(('ctx', 'fsdp'))
- w_qkv_grad: float32 [2048, 6144], P(None, ('ctx', 'fsdp'))
- b_qkv_grad: float32 [6144], P(('ctx', 'fsdp'))
- w_out_grad: float32 [2048, 2048], P(None, ('ctx', 'fsdp'))
- b_out_grad: float32 [2048], P(('ctx', 'fsdp'))
- w_fc1_grad: float32 [2048, 8192], P(None, ('ctx', 'fsdp'))
- b_fc1_grad: float32 [8192], P(('ctx', 'fsdp'))
- w_fc2_grad: float32 [8192, 2048], P(None, ('ctx', 'fsdp'))
- b_fc2_grad: float32 [2048], P(('ctx', 'fsdp'))
All inputs are finite; a program needn't handle non-finite values.
Results may differ from a plain program's by a relative error of at most 0.0096.
Values may be sent and summed in bfloat16 or wider, within the bound.
No kernel may reach another device: no remote copies, remote signals or barrier semaphores. Data moves between devices by JAX's collectives and lax.ppermute only.
A program may use at most 384 MiB of HBM per device.

v0:
```python
import math

import jax
import jax.numpy as jnp
from jax import lax
from jax.sharding import PartitionSpec as P

HEADS = 8
HEAD = 256
ROT = 64


EPSILON = 1e-05
SQRT_HALF = 0.7071067811865476
INV_ROOT_TWO_PI = 0.3989422804014327
MASKED = -1e30


def from_behind(value, axis, steps):
    count = lax.axis_size(axis)
    pairs = [(source, (source + steps) % count) for source in range(count)]
    return lax.ppermute(value, axis, pairs)


def shifted(block, axis, distance):
    devices = range(lax.axis_size(axis))
    route = [(i - distance, i) for i in devices if i - distance in devices]
    return lax.ppermute(block, axis, route)


def normalize(inputs):
    centre = jnp.mean(inputs, axis=-1, keepdims=True)
    centred = inputs - centre
    variance = jnp.mean(centred * centred, axis=-1, keepdims=True)
    inv_std = lax.rsqrt(variance + EPSILON)
    return (centred * inv_std, inv_std)


def norm_backward(upstream, normed, inv_std):
    first_mean = jnp.mean(upstream, axis=-1, keepdims=True)
    second_mean = jnp.mean(upstream * normed, axis=-1, keepdims=True)
    return inv_std * (upstream - first_mean - normed * second_mean)


def gelu_parts(preact):
    normal_cdf = 0.5 * (1.0 + lax.erf(preact * SQRT_HALF))
    normal_pdf = jnp.exp(-0.5 * preact * preact) * INV_ROOT_TWO_PI
    return (preact * normal_cdf, normal_cdf + preact * normal_pdf)


def rotary_tables(positions, rot_dims):
    half_dims = rot_dims // 2
    frequency = jnp.exp(
        jnp.arange(half_dims).astype(jnp.float32) * (-2.0 * math.log(10000.0) / rot_dims)
    )
    angles = positions[:, None] * frequency[None, :]
    return (jnp.cos(angles)[:, None, :], jnp.sin(angles)[:, None, :])


def rotate(tensor, cosine, sine_table, rot_dims):
    half_dims = rot_dims // 2
    leading = tensor[..., :half_dims]
    trailing = tensor[..., half_dims:rot_dims]
    return jnp.concatenate(
        [
            leading * cosine - trailing * sine_table,
            trailing * cosine + leading * sine_table,
            tensor[..., rot_dims:],
        ],
        axis=-1,
    )


def contract_rows(left, right):
    return lax.dot_general(
        left, right, (((0,), (0,)), ((), ())), preferred_element_type=jnp.float32
    )


def contract_cols(left, right):
    return lax.dot_general(
        left, right, (((1,), (1,)), ((), ())), preferred_element_type=jnp.float32
    )


def body(
    hidden,
    cotangent,
    ln1_gain,
    ln1_bias,
    ln2_gain,
    ln2_bias,
    w_qkv,
    b_qkv,
    w_out,
    b_out,
    w_fc1,
    b_fc1,
    w_fc2,
    b_fc2,
):
    inputs = hidden[0]
    upstream_bf = cotangent[0]
    row_count = inputs.shape[0]
    score_scale = HEAD ** (-0.5)
    cycle_size = lax.axis_size("ctx")
    cycle_place = lax.axis_index("ctx")
    attn_gathered = (
        lax.all_gather(ln1_gain, ("ctx", "fsdp"), axis=0, tiled=True),
        lax.all_gather(ln1_bias, ("ctx", "fsdp"), axis=0, tiled=True),
        lax.all_gather(w_qkv, ("ctx", "fsdp"), axis=1, tiled=True),
        lax.all_gather(b_qkv, ("ctx", "fsdp"), axis=0, tiled=True),
        lax.all_gather(w_out, ("ctx", "fsdp"), axis=1, tiled=True),
        lax.all_gather(b_out, ("ctx", "fsdp"), axis=0, tiled=True),
    )
    mlp_gathered = (
        lax.all_gather(ln2_gain, ("ctx", "fsdp"), axis=0, tiled=True),
        lax.all_gather(ln2_bias, ("ctx", "fsdp"), axis=0, tiled=True),
        lax.all_gather(w_fc1, ("ctx", "fsdp"), axis=1, tiled=True),
        lax.all_gather(b_fc1, ("ctx", "fsdp"), axis=0, tiled=True),
        lax.all_gather(w_fc2, ("ctx", "fsdp"), axis=1, tiled=True),
        lax.all_gather(b_fc2, ("ctx", "fsdp"), axis=0, tiled=True),
    )
    gain_one, shift_one, full_qkv, full_bqkv, full_out, full_bout = attn_gathered
    gain_two, shift_two, full_fc1, full_bfc1, full_fc2, full_bfc2 = mlp_gathered
    inputs_f = inputs.astype(jnp.float32)
    normed, inv_std = normalize(inputs_f)
    attn_in = (normed * gain_one.astype(jnp.float32) + shift_one.astype(jnp.float32)).astype(
        jnp.bfloat16
    )
    mlp_in = (normed * gain_two.astype(jnp.float32) + shift_two.astype(jnp.float32)).astype(
        jnp.bfloat16
    )
    joined = jnp.dot(attn_in, full_qkv, preferred_element_type=jnp.float32) + full_bqkv.astype(
        jnp.float32
    )
    joined = joined.reshape(row_count, 3, HEADS, HEAD)
    token_pos = cycle_place * row_count + jnp.arange(row_count, dtype=jnp.int32)
    cosine, sine_table = rotary_tables(token_pos.astype(jnp.float32), ROT)
    queries = rotate(joined[:, 0], cosine, sine_table, ROT).astype(jnp.bfloat16)
    keys_own = rotate(joined[:, 1], cosine, sine_table, ROT).astype(jnp.bfloat16)
    values_own = joined[:, 2].astype(jnp.bfloat16)
    row_top = jnp.full((HEADS, row_count), MASKED, jnp.float32)
    absorb_key_block = lax.all_gather(keys_own, "ctx", axis=0, tiled=True)
    absorb_value_block = lax.all_gather(values_own, "ctx", axis=0, tiled=True)
    absorb_key_pos = jnp.arange(absorb_key_block.shape[0], dtype=jnp.int32)
    absorb_visible = (token_pos[:, None] >= absorb_key_pos[None, :])[None]
    absorb_scores = (
        jnp.einsum("qhd,khd->hqk", queries, absorb_key_block, preferred_element_type=jnp.float32)
        * score_scale
    )
    absorb_scores = jnp.where(absorb_visible, absorb_scores, MASKED)
    new_top = jnp.maximum(row_top, jnp.max(absorb_scores, axis=-1))
    weights_exp = jnp.where(absorb_visible, jnp.exp(absorb_scores - new_top[:, :, None]), 0.0)
    row_total = jnp.sum(weights_exp, axis=-1)
    mixed = jnp.einsum(
        "hqk,khd->qhd",
        weights_exp.astype(jnp.bfloat16),
        absorb_value_block,
        preferred_element_type=jnp.float32,
    )
    row_top, row_total, mixed = (new_top, row_total, mixed)
    attended = (mixed / jnp.transpose(row_total)[:, :, None]).astype(jnp.bfloat16)
    log_total = row_top + jnp.log(row_total)
    attended_flat = attended.reshape(row_count, HEADS * HEAD)
    branch_attn = jnp.dot(
        attended_flat, full_out, preferred_element_type=jnp.float32
    ) + full_bout.astype(jnp.float32)
    preact = jnp.dot(mlp_in, full_fc1, preferred_element_type=jnp.float32) + full_bfc1.astype(
        jnp.float32
    )
    activated, slope = gelu_parts(preact)
    act_bf = activated.astype(jnp.bfloat16)
    branch_mlp = jnp.dot(act_bf, full_fc2, preferred_element_type=jnp.float32) + full_bfc2.astype(
        jnp.float32
    )
    output = (inputs_f + branch_attn + branch_mlp).astype(jnp.bfloat16)
    rows_all = (
        lax.all_gather(inputs, ("ctx", "fsdp"), axis=0, tiled=True),
        lax.all_gather(act_bf, ("ctx", "fsdp"), axis=0, tiled=True),
        lax.all_gather(attended_flat, ("ctx", "fsdp"), axis=0, tiled=True),
    )
    attn_gathered = (
        lax.all_gather(ln1_gain, ("ctx", "fsdp"), axis=0, tiled=True),
        lax.all_gather(ln1_bias, ("ctx", "fsdp"), axis=0, tiled=True),
        lax.all_gather(w_qkv, ("ctx", "fsdp"), axis=1, tiled=True),
        lax.all_gather(b_qkv, ("ctx", "fsdp"), axis=0, tiled=True),
        lax.all_gather(w_out, ("ctx", "fsdp"), axis=1, tiled=True),
        lax.all_gather(b_out, ("ctx", "fsdp"), axis=0, tiled=True),
    )
    mlp_gathered = (
        lax.all_gather(ln2_gain, ("ctx", "fsdp"), axis=0, tiled=True),
        lax.all_gather(ln2_bias, ("ctx", "fsdp"), axis=0, tiled=True),
        lax.all_gather(w_fc1, ("ctx", "fsdp"), axis=1, tiled=True),
        lax.all_gather(b_fc1, ("ctx", "fsdp"), axis=0, tiled=True),
        lax.all_gather(w_fc2, ("ctx", "fsdp"), axis=1, tiled=True),
        lax.all_gather(b_fc2, ("ctx", "fsdp"), axis=0, tiled=True),
    )
    gain_one, shift_one, full_qkv, full_bqkv, full_out, full_bout = attn_gathered
    gain_two, shift_two, full_fc1, full_bfc1, full_fc2, full_bfc2 = mlp_gathered
    upstream = upstream_bf.astype(jnp.float32)
    bias_out_grad = jnp.sum(upstream, axis=0)
    d_act = contract_cols(upstream_bf, full_fc2)
    d_preact = d_act * slope
    d_preact_bf = d_preact.astype(jnp.bfloat16)
    d_mlp_in = contract_cols(d_preact_bf, full_fc1)
    fc1_bias_grad = jnp.sum(d_preact, axis=0)
    ln2_gain_part = jnp.sum(d_mlp_in * normed, axis=0)
    ln2_bias_part = jnp.sum(d_mlp_in, axis=0)
    d_attended = (
        contract_cols(upstream_bf, full_out).astype(jnp.bfloat16).reshape(row_count, HEADS, HEAD)
    )
    row_dot = jnp.transpose(
        jnp.sum(d_attended.astype(jnp.float32) * attended.astype(jnp.float32), axis=-1)
    )
    d_queries = jnp.zeros((row_count, HEADS, HEAD), jnp.float32)
    travelling = (keys_own, values_own)
    key_grads = (
        jnp.zeros((row_count, HEADS, HEAD), jnp.float32),
        jnp.zeros((row_count, HEADS, HEAD), jnp.float32),
    )
    for turn_index in range(cycle_size):
        source = (cycle_place - turn_index) % cycle_size
        key_pos = source * row_count + jnp.arange(row_count, dtype=jnp.int32)
        key_block, value_block = travelling
        visible = (token_pos[:, None] >= key_pos[None, :])[None]
        scores = (
            jnp.einsum("qhd,khd->hqk", queries, key_block, preferred_element_type=jnp.float32)
            * score_scale
        )
        scores = jnp.where(visible, scores, MASKED)
        probability = jnp.where(visible, jnp.exp(scores - log_total[:, :, None]), 0.0)
        d_probability = jnp.einsum(
            "qhd,khd->hqk", d_attended, value_block, preferred_element_type=jnp.float32
        )
        d_scores = (probability * (d_probability - row_dot[:, :, None]) * score_scale).astype(
            jnp.bfloat16
        )
        d_queries = d_queries + jnp.einsum(
            "hqk,khd->qhd", d_scores, key_block, preferred_element_type=jnp.float32
        )
        key_grads = (
            key_grads[0]
            + jnp.einsum("hqk,qhd->khd", d_scores, queries, preferred_element_type=jnp.float32),
            key_grads[1]
            + jnp.einsum(
                "hqk,qhd->khd",
                probability.astype(jnp.bfloat16),
                d_attended,
                preferred_element_type=jnp.float32,
            ),
        )
        key_grads = from_behind((key_grads[0], key_grads[1]), "ctx", 1)
        if turn_index + 1 < cycle_size:
            travelling = shifted((travelling[0], travelling[1]), "ctx", 1)
    d_queries = rotate(d_queries, cosine, -sine_table, ROT)
    d_keys = rotate(key_grads[0], cosine, -sine_table, ROT)
    d_joined = jnp.stack([d_queries, d_keys, key_grads[1]], axis=1).reshape(
        row_count, 3 * HEADS * HEAD
    )
    d_joined_bf = d_joined.astype(jnp.bfloat16)
    d_attn_in = contract_cols(d_joined_bf, full_qkv)
    qkv_bias_grad = jnp.sum(d_joined, axis=0)
    ln1_gain_part = jnp.sum(d_attn_in * normed, axis=0)
    ln1_bias_part = jnp.sum(d_attn_in, axis=0)
    columns = (
        lax.all_to_all(upstream_bf, ("ctx", "fsdp"), split_axis=1, concat_axis=0, tiled=True),
        lax.all_to_all(d_preact_bf, ("ctx", "fsdp"), split_axis=1, concat_axis=0, tiled=True),
        lax.all_to_all(d_joined_bf, ("ctx", "fsdp"), split_axis=1, concat_axis=0, tiled=True),
    )
    small = (
        lax.psum_scatter(ln1_gain_part, ("ctx", "fsdp"), scatter_dimension=0, tiled=True),
        lax.psum_scatter(ln1_bias_part, ("ctx", "fsdp"), scatter_dimension=0, tiled=True),
        lax.psum_scatter(ln2_gain_part, ("ctx", "fsdp"), scatter_dimension=0, tiled=True),
        lax.psum_scatter(ln2_bias_part, ("ctx", "fsdp"), scatter_dimension=0, tiled=True),
        lax.psum_scatter(qkv_bias_grad, ("ctx", "fsdp"), scatter_dimension=0, tiled=True),
        lax.psum_scatter(bias_out_grad, ("ctx", "fsdp"), scatter_dimension=0, tiled=True),
        lax.psum_scatter(fc1_bias_grad, ("ctx", "fsdp"), scatter_dimension=0, tiled=True),
    )
    normed_all, unused_std = normalize(rows_all[0].astype(jnp.float32))
    attn_all = (normed_all * gain_one.astype(jnp.float32) + shift_one.astype(jnp.float32)).astype(
        jnp.bfloat16
    )
    mlp_all = (normed_all * gain_two.astype(jnp.float32) + shift_two.astype(jnp.float32)).astype(
        jnp.bfloat16
    )
    fc2_part = contract_rows(rows_all[1], columns[0])
    out_part = contract_rows(rows_all[2], columns[0])
    fc1_part = contract_rows(mlp_all, columns[1])
    qkv_part = contract_rows(attn_all, columns[2])
    owned = (
        small[0],
        small[1],
        small[2],
        small[3],
        qkv_part,
        small[4],
        out_part,
        small[5],
        fc1_part,
        small[6],
        fc2_part,
    )
    merged = d_attn_in * gain_one.astype(jnp.float32) + d_mlp_in * gain_two.astype(jnp.float32)
    input_grad = (upstream + norm_backward(merged, normed, inv_std)).astype(jnp.bfloat16)
    totals = lax.psum(
        (
            owned[0],
            owned[1],
            owned[2],
            owned[3],
            owned[4],
            owned[5],
            owned[6],
            owned[7],
            owned[8],
            owned[9],
            owned[10],
        ),
        "dp",
    )
    return (
        output[None],
        input_grad[None],
        totals[0],
        totals[1],
        totals[2],
        totals[3],
        totals[4],
        totals[5],
        totals[6],
        totals[7],
        totals[8],
        totals[9],
        totals[10],
        totals[7],
    )


def solution(mesh):
    return jax.shard_map(
        body,
        mesh=mesh,
        in_specs=(
            P(("dp", "fsdp"), "ctx", None),
            P(("dp", "fsdp"), "ctx", None),
            P(("ctx", "fsdp")),
            P(("ctx", "fsdp")),
            P(("ctx", "fsdp")),
            P(("ctx", "fsdp")),
            P(None, ("ctx", "fsdp")),
            P(("ctx", "fsdp")),
            P(None, ("ctx", "fsdp")),
            P(("ctx", "fsdp")),
            P(None, ("ctx", "fsdp")),
            P(("ctx", "fsdp")),
            P(None, ("ctx", "fsdp")),
            P(("ctx", "fsdp")),
        ),
        out_specs=(
            P(("dp", "fsdp"), "ctx", None),
            P(("dp", "fsdp"), "ctx", None),
            P(("ctx", "fsdp")),
            P(("ctx", "fsdp")),
            P(("ctx", "fsdp")),
            P(("ctx", "fsdp")),
            P(None, ("ctx", "fsdp")),
            P(("ctx", "fsdp")),
            P(None, ("ctx", "fsdp")),
            P(("ctx", "fsdp")),
            P(None, ("ctx", "fsdp")),
            P(("ctx", "fsdp")),
            P(None, ("ctx", "fsdp")),
            P(("ctx", "fsdp")),
        ),
        check_vma=False,
    )
```

profile of v0, /device:TPU:0, one launch (start us, length us, event | category | flops | bytes accessed | tf_op | source)
XLA Modules:
  0.0 3050.2 jit_solution(16428829092678689775)
XLA Ops:
  8.8 66.9 %all-gather.4 = bf16[8,1,768]{2,1,0:T(2,128)(2,1)S(1)} all-gather(bf16[1,1,768]{2,1,0:T(2,128)(2,1)S(1)} %reshape.342), channel_id=1, replica_groups=mesh['dp'=4,'ctx'=4,'fsdp'=2] {'ctx','fsdp'}, dimensions={0}, use_global_device_ids=true | all-gather | bytes 13824 | tf_op jit(solution)/shard_map/all_gather | solution.py:112
  75.7 22.1 all-gather.3
  97.8 22.8 all-gather.2
  122.1 371.3 %all-gather.19.cloned.1.call-done = bf16[2048,6144]{1,0:T(8,128)(2,1)} async-done(((bf16[2048,768]{1,0:T(8,128)(2,1)}), bf16[2048,6144]{1,0:T(8,128)(2,1)}) %all-gather.19.cloned.1.call-update) | async-done | bytes 25165840 | tf_op jit(solution)/shard_map/all_gather | solution.py:111
  493.4 10.1 convolution_add_fusion.1
  513.5 106.8 %all-gather.23.cloned.1.call-done = bf16[2048,2048]{1,0:T(8,128)(2,1)} async-done(((bf16[2048,256]{1,0:T(8,128)(2,1)}), bf16[2048,2048]{1,0:T(8,128)(2,1)}) %all-gather.23.cloned.1.call-update) | async-done | bytes 8388624 | tf_op jit(solution)/shard_map/all_gather | solution.py:113
  620.3 6.3 convolution_convert_fusion
  627.6 38.7 %all-gather.21.cloned.1.call-done = bf16[512,8,256]{2,0,1:T(8,128)(2,1)} async-done(((bf16[128,8,256]{2,0,1:T(8,128)(2,1)}), bf16[512,8,256]{2,0,1:T(8,128)(2,1)}) %all-gather.21.cloned.1.call-update) | async-done | bytes 2097168 | tf_op jit(solution)/shard_map/all_gather | solution.py:144
  670.8 42.6 %all-gather.33.cloned.1.call-done = bf16[512,1,8,256]{0,3,2,1:T(8,128)(2,1)} async-done(((bf16[128,1,8,256]{0,3,2,1:T(8,128)(2,1)}), bf16[512,1,8,256]{0,3,2,1:T(8,128)(2,1)}) %all-gather.33.cloned.1.call-update) | async-done | bytes 2097168 | tf_op jit(solution)/shard_map/all_gather | solution.py:145
  713.4 3.9 multiply_reduce_fusion
  718.2 75.0 %all_gather.70 = bf16[8192]{0:T(1024)(128)(2,1)S(1)} all-gather(bf16[1024]{0:T(1024)(128)(2,1)S(1)} %copy-done.26), channel_id=1, replica_groups=mesh['dp'=4,'ctx'=4,'fsdp'=2] {'ctx','fsdp'}, dimensions={0}, use_global_device_ids=true | all-gather | bytes 18432 | tf_op jit(solution)/shard_map/all_gather | solution.py:120
  793.2 27.6 all-gather.7
  820.9 25.2 all-gather.6
  846.1 505.2 %all-gather.25.cloned.1.call-done = bf16[2048,8192]{1,0:T(8,128)(2,1)} async-done(((bf16[2048,1024]{1,0:T(8,128)(2,1)}), bf16[2048,8192]{1,0:T(8,128)(2,1)}) %all-gather.25.cloned.1.call-update) | async-done | bytes 33554448 | tf_op jit(solution)/shard_map/all_gather | solution.py:119
  1351.3 16.6 multiply_convert_fusion
  1368.0 4.1 collective-permute-start
  1372.0 3.4 collective-permute-start.1
  1375.4 15.1 collective-permute-done
  1390.5 5.3 collective-permute-start.2
  1395.8 13.9 collective-permute-done.1
  1409.7 9.5 collective-permute-start.3
  1420.2 8.3 all-to-all-start.1
  1428.7 3.6 collective-permute-done.2
  1432.3 11.2 collective-permute-start.4
  1443.5 11.3 collective-permute-done.3
  1454.7 8.0 collective-permute-start.5
  1473.1 68.2 %collective-permute-done.6 = f32[128,8,256]{2,0,1:T(8,128)S(1)} collective-permute-done((f32[128,8,256]{2,0,1:T(8,128)S(1)}, f32[128,8,256]{2,0,1:T(8,128)S(1)}, u32[]{:S(2)}, u32[]{:S(2)}) %collective-permute-start.6) | collective-permute-done | bytes 1048608 | tf_op jit(solution)/shard_map/ppermute | solution.py:22
  1541.7 11.7 collective-permute-start.7
  1554.9 29.5 collective-permute-done.10
  1584.8 4.3 collective-permute-start.11
  1589.7 31.2 %collective-permute-done.7 = f32[128,8,256]{2,0,1:T(8,128)S(1)} collective-permute-done((f32[128,8,256]{2,0,1:T(8,128)S(1)}, f32[128,8,256]{2,0,1:T(8,128)S(1)}, u32[]{:S(2)}, u32[]{:S(2)}) %collective-permute-start.7) | collective-permute-done | bytes 1048608 | tf_op jit(solution)/shard_map/ppermute | solution.py:22
  1621.1 6.5 collective-permute-start.8
  1628.4 37.5 %collective-permute-done.11 = f32[128,8,256]{2,0,1:T(8,128)S(1)} collective-permute-done((f32[128,8,256]{2,0,1:T(8,128)S(1)}, f32[128,8,256]{2,0,1:T(8,128)S(1)}, u32[]{:S(2)}, u32[]{:S(2)}) %collective-permute-start.11) | collective-permute-done | bytes 1048608 | tf_op jit(solution)/shard_map/ppermute | solution.py:22
  1666.0 6.5 collective-permute-start.12
  1673.2 31.7 %collective-permute-done.8 = f32[128,8,256]{2,0,1:T(8,128)S(1)} collective-permute-done((f32[128,8,256]{2,0,1:T(8,128)S(1)}, f32[128,8,256]{2,0,1:T(8,128)S(1)}, u32[]{:S(2)}, u32[]{:S(2)}) %collective-permute-start.8) | collective-permute-done | bytes 1048608 | tf_op jit(solution)/shard_map/ppermute | solution.py:22
  1705.1 6.5 collective-permute-start.9
  1713.2 36.7 %collective-permute-done.12 = f32[128,8,256]{2,0,1:T(8,128)S(1)} collective-permute-done((f32[128,8,256]{2,0,1:T(8,128)S(1)}, f32[128,8,256]{2,0,1:T(8,128)S(1)}, u32[]{:S(2)}, u32[]{:S(2)}) %collective-permute-start.12) | collective-permute-done | bytes 1048608 | tf_op jit(solution)/shard_map/ppermute | solution.py:22
  1750.1 6.5 collective-permute-start.13
  1758.6 34.5 %collective-permute-done.9 = f32[128,8,256]{2,0,1:T(8,128)S(1)} collective-permute-done((f32[128,8,256]{2,0,1:T(8,128)S(1)}, f32[128,8,256]{2,0,1:T(8,128)S(1)}, u32[]{:S(2)}, u32[]{:S(2)}) %collective-permute-start.9) | collective-permute-done | bytes 1048608 | tf_op jit(solution)/shard_map/ppermute | solution.py:22
  1795.3 42.5 %collective-permute-done.13 = f32[128,8,256]{2,0,1:T(8,128)S(1)} collective-permute-done((f32[128,8,256]{2,0,1:T(8,128)S(1)}, f32[128,8,256]{2,0,1:T(8,128)S(1)}, u32[]{:S(2)}, u32[]{:S(2)}) %collective-permute-start.13) | collective-permute-done | bytes 1048608 | tf_op jit(solution)/shard_map/ppermute | solution.py:22
  1842.8 23.7 all-to-all-start
  1868.6 3.0 convert_reduce_fusion
  1874.2 48.4 %all-to-all-done = bf16[128,8,768]{0,2,1:T(8,128)(2,1)} async-done(((bf16[128,8,768]{0,2,1:T(8,128)(2,1)}), bf16[128,8,768]{0,2,1:T(8,128)(2,1)}, u32[]{:S(2)}, u32[]{:S(2)}) %all-to-all-start) | async-done | bytes 1572896 | tf_op jit(solution)/shard_map/all_to_all | solution.py:269
  1924.3 9.1 fusion.16
  1933.4 4.8 fusion.132
  1938.2 310.6 %all-gather.27.cloned.1.call-done = bf16[8192,2048]{1,0:T(8,128)(2,1)} async-done(((bf16[8192,256]{1,0:T(8,128)(2,1)}), bf16[8192,2048]{1,0:T(8,128)(2,1)}) %all-gather.27.cloned.1.call-update) | async-done | bytes 33554448 | tf_op jit(solution)/shard_map/all_gather | solution.py:121
  2248.8 19.1 fusion.129
  2269.5 5.5 all-to-all-start.2
  2275.3 16.9 fusion.131
  2292.2 14.6 fusion.126
  2308.9 65.0 %all-to-all-done.2 = bf16[128,8,1024]{2,0,1:T(8,128)(2,1)} async-done(((bf16[128,8,1024]{2,0,1:T(8,128)(2,1)}), bf16[128,8,1024]{2,0,1:T(8,128)(2,1)}, u32[]{:S(2)}, u32[]{:S(2)}) %all-to-all-start.2) | async-done | bytes 2097184 | tf_op jit(solution)/shard_map/all_to_all | solution.py:268
  2373.8 12.3 fusion.14
  2386.1 137.8 %all-gather.31.cloned.1.call-done = bf16[1024,8192]{1,0:T(8,128)(2,1)} async-done(((bf16[128,8192]{1,0:T(8,128)(2,1)}), bf16[1024,8192]{1,0:T(8,128)(2,1)}) %all-gather.31.cloned.1.call-update) | async-done | bytes 16777232 | tf_op jit(solution)/shard_map/all_gather | solution.py:180
  2523.9 13.9 fusion.133
  2538.5 17.6 all-gather.5
  2556.2 17.2 all-gather.8
  2576.0 4.8 fusion.27
  2580.8 14.0 fusion.29
  2594.8 3.7 all-reduce.13.cloned.1.call-done
  2603.7 11.6 all-reduce.8
  2615.3 409.5 %all-reduce.15.cloned.1.call-done = (f32[2048,768]{1,0:T(8,128)}, f32[2048,256]{1,0:T(8,128)}, f32[2048,1024]{1,0:T(8,128)}, f32[8192,256]{1,0:T(8,128)}) async-done(((f32[2048,768]{1,0:T(8,128)}, f32[2048,256]{1,0:T(8,128)}, f32[2048,1024]{1,0:T(8,128)}, f32[8192,256]{1,0:T(8,128)}), (f32[2048,768]{1,0:T(8,128)}, f32[2048,256]{1,0:T(8,128)}, f32[2048,1024]{1,0:T(8,128)}, ...) | async-done | bytes 25165840 | tf_op jit(solution)/shard_map/psum | solution.py:306
  3025.4 6.5 copy.223
  3034.2 4.3 copy.225
  3039.8 3.4 copy.226
  (201 shorter events, 67.1 us)
Async XLA Ops:
  7.2 1.6 copy-start.27
  7.2 68.5 %copy-start.29 = (bf16[256]{0:T(256)(128)(2,1)S(1)}, bf16[256]{0:T(256)(128)(2,1)}, u32[]{:S(2)}) copy-start(bf16[256]{0:T(256)(128)(2,1)} %param.17) | copy-start | bytes 1540
  7.2 90.6 %copy-start.30 = (bf16[256]{0:T(256)(128)(2,1)S(1)}, bf16[256]{0:T(256)(128)(2,1)}, u32[]{:S(2)}) copy-start(bf16[256]{0:T(256)(128)(2,1)} %param.16) | copy-start | bytes 1540
  7.2 113.4 %copy-start = (bf16[1,128,2048]{2,1,0:T(8,128)(2,1)S(1)}, bf16[1,128,2048]{2,1,0:T(8,128)(2,1)}, u32[]{:S(2)}) copy-start(bf16[1,128,2048]{2,1,0:T(8,128)(2,1)} %param.14) | copy-start | bytes 1572868
  7.2 486.2 %all-gather.19.cloned.1.call-start = ((), (), s32[]{:S(2)}) async-start(), calls=%async_computation.3 | async-start | bytes 28311552 | tf_op jit(solution)/shard_map/all_gather | solution.py:111
  8.0 612.4 %all-gather.23.cloned.1.call-start = ((), (), s32[]{:S(2)}) async-start(), calls=%async_computation.5 | async-start | bytes 9437184 | tf_op jit(solution)/shard_map/all_gather | solution.py:113
  8.7 657.6 %all-gather.21.cloned.1.call-start = ((), (), s32[]{:S(2)}) async-start(), calls=%async_computation.4 | async-start | bytes 2621440 | tf_op jit(solution)/shard_map/all_gather | solution.py:144
  120.8 382.7 %copy-start.20 = (f32[128]{0:T(128)}, f32[128]{0:T(128)S(1)}, u32[]{:S(2)}) copy-start(f32[128]{0:T(128)S(1)} %broadcast_multiply_fusion.3) | copy-start | bytes 1540
  121.1 382.4 %copy-start.22 = (f32[128]{0:T(128)}, f32[128]{0:T(128)S(1)}, u32[]{:S(2)}) copy-start(f32[128]{0:T(128)S(1)} %add_rsqrt_fusion.1) | copy-start | bytes 1540
  504.5 1.8 copy-start.19
  505.3 1.0 copy-start.6
  508.7 204.7 %all-gather.33.cloned.1.call-start = ((), (), s32[]{:S(2)}) async-start(), calls=%async_computation.10 | async-start | bytes 2621440 | tf_op jit(solution)/shard_map/all_gather | solution.py:145
  509.6 110.7 %copy-start.10 = (bf16[1,128,2048]{2,1,0:T(8,128)(2,1)S(1)}, bf16[1,128,2048]{2,1,0:T(8,128)(2,1)}, u32[]{:S(2)}) copy-start(bf16[1,128,2048]{2,1,0:T(8,128)(2,1)} %param.15) | copy-start | bytes 1572868
  511.9 839.4 %all-gather.25.cloned.1.call-start = ((), (), s32[]{:S(2)}) async-start(), calls=%async_computation.6 | async-start | bytes 37748736 | tf_op jit(solution)/shard_map/all_gather | solution.py:119
  512.5 1356.1 %all-gather.35.cloned.1.call-start = ((), (), s32[]{:S(2)}) async-start(), calls=%async_computation.11 | async-start | bytes 4718592 | tf_op jit(solution)/shard_map/all_gather | solution.py:179
  513.1 1420.3 %all-gather.29.cloned.1.call-start = ((), (), s32[]{:S(2)}) async-start(), calls=%async_computation.8 | async-start | bytes 4718592 | tf_op jit(solution)/shard_map/all_gather | solution.py:181
  513.4 113.2 %copy-start.24 = (s32[128]{0:T(128)}, s32[128]{0:T(128)S(1)}, u32[]{:S(2)}) copy-start(s32[128]{0:T(128)S(1)} %iota_add_fusion.4) | copy-start | bytes 1540
  513.5 113.4 %copy-start.7 = (f32[128,8,256]{2,0,1:T(8,128)S(1)}, f32[128,8,256]{2,0,1:T(8,128)}, u32[]{:S(2)}) copy-start(f32[128,8,256]{2,0,1:T(8,128)} %copy-done.6) | copy-start | bytes 3145732
  513.5 113.6 %copy-start.16 = (bf16[128,8,32]{2,0,1:T(8,128)(2,1)S(1)}, bf16[128,8,32]{2,0,1:T(8,128)(2,1)}, u32[]{:S(2)}) copy-start(bf16[128,8,32]{2,0,1:T(8,128)(2,1)} %get-tuple-element.61) | copy-start | bytes 196612
  668.8 1.3 copy-start.5
  717.3 75.9 %copy-start.31 = (bf16[256]{0:T(256)(128)(2,1)S(1)}, bf16[256]{0:T(256)(128)(2,1)}, u32[]{:S(2)}) copy-start(bf16[256]{0:T(256)(128)(2,1)} %param.19) | copy-start | bytes 1540
  717.3 103.6 %copy-start.32 = (bf16[256]{0:T(256)(128)(2,1)S(1)}, bf16[256]{0:T(256)(128)(2,1)}, u32[]{:S(2)}) copy-start(bf16[256]{0:T(256)(128)(2,1)} %param.18) | copy-start | bytes 1540
  717.3 634.0 %copy-start.1 = (bf16[1,128,2048]{2,1,0:T(8,128)(2,1)S(1)}, bf16[1,128,2048]{2,1,0:T(8,128)(2,1)}, u32[]{:S(2)}) copy-start(bf16[1,128,2048]{2,1,0:T(8,128)(2,1)} %param.14) | copy-start | bytes 1572868
  717.3 634.0 %copy-start.21 = (f32[128]{0:T(128)S(1)}, f32[128]{0:T(128)}, u32[]{:S(2)}) copy-start(f32[128]{0:T(128)} %copy-done.20) | copy-start | bytes 1540
  717.3 634.0 %copy-start.23 = (f32[128]{0:T(128)S(1)}, f32[128]{0:T(128)}, u32[]{:S(2)}) copy-start(f32[128]{0:T(128)} %copy-done.22) | copy-start | bytes 1540
  717.4 1531.4 %all-gather.27.cloned.1.call-start = ((), (), s32[]{:S(2)}) async-start(), calls=%async_computation.7 | async-start | bytes 37748736 | tf_op jit(solution)/shard_map/all_gather | solution.py:121
  718.1 1805.8 %all-gather.31.cloned.1.call-start = ((), (), s32[]{:S(2)}) async-start(), calls=%async_computation.9 | async-start | bytes 18874368 | tf_op jit(solution)/shard_map/all_gather | solution.py:180
  1351.3 16.6 copy-start.8
  1351.3 20.7 copy-start.9
  1367.9 60.7 %copy-start.25 = (s32[128]{0:T(128)S(1)}, s32[128]{0:T(128)}, u32[]{:S(2)}) copy-start(s32[128]{0:T(128)} %copy-done.24) | copy-start | bytes 1540
  1368.0 22.6 collective-permute-start
  1372.0 37.7 %collective-permute-start.1 = (bf16[128,8,256]{0,2,1:T(8,128)(2,1)S(1)}, bf16[128,8,256]{0,2,1:T(8,128)(2,1)}, u32[]{:S(2)}, u32[]{:S(2)}) collective-permute-start(bf16[128,8,256]{0,2,1:T(8,128)(2,1)S(1)} %bitcast.242), channel_id=1, source_target_pairs={{0,2},{2,4},{4,6},{1,3},{3,5},{5,7},{8,10},{10,12},{12,14},{9,11},... | collective-permute-start | bytes 1572872 | tf_op jit(solution)/shard_map/ppermute | solution.py:28
  1390.5 41.7 %collective-permute-start.2 = (bf16[128,8,256]{2,0,1:T(8,128)(2,1)}, bf16[128,8,256]{2,0,1:T(8,128)(2,1)}, u32[]{:S(2)}, u32[]{:S(2)}) collective-permute-start(bf16[128,8,256]{2,0,1:T(8,128)(2,1)} %collective-permute-done), channel_id=1, source_target_pairs={{0,2},{2,4},{4,6},{1,3},{3,5},{5,7},{8,10},{10,12},{12,14},{9,11},... | collective-permute-start | bytes 1572872 | tf_op jit(solution)/shard_map/ppermute | solution.py:28
  1409.7 45.0 %collective-permute-start.3 = (bf16[128,8,256]{0,2,1:T(8,128)(2,1)}, bf16[128,8,256]{0,2,1:T(8,128)(2,1)}, u32[]{:S(2)}, u32[]{:S(2)}) collective-permute-start(bf16[128,8,256]{0,2,1:T(8,128)(2,1)} %collective-permute-done.1), channel_id=1, source_target_pairs={{0,2},{2,4},{4,6},{1,3},{3,5},{5,7},{8,10},{10,12},{12,14},{9,11},... | collective-permute-start | bytes 1572872 | tf_op jit(solution)/shard_map/ppermute | solution.py:28
  1420.2 422.6 %all-to-all-start.1 = ((bf16[128,8,256]{0,2,1:T(8,128)(2,1)}), bf16[128,8,256]{0,2,1:T(8,128)(2,1)}, u32[]{:S(2)}, u32[]{:S(2)}) async-start(bf16[128,8,256]{0,2,1:T(8,128)(2,1)} %bitcast.247), calls=%async_computation.1 | async-start | bytes 1048576 | tf_op jit(solution)/shard_map/all_to_all | solution.py:267
  1432.3 156.8 %collective-permute-start.4 = (bf16[128,8,256]{2,0,1:T(8,128)(2,1)}, bf16[128,8,256]{2,0,1:T(8,128)(2,1)S(1)}, u32[]{:S(2)}, u32[]{:S(2)}) collective-permute-start(bf16[128,8,256]{2,0,1:T(8,128)(2,1)} %collective-permute-done.2), channel_id=1, source_target_pairs={{0,2},{2,4},{4,6},{1,3},{3,5},{5,7},{8,10},{10,12},{12,14},{9,11},... | collective-permute-start | bytes 1572872 | tf_op jit(solution)/shard_map/ppermute | solution.py:28
  1454.7 172.9 %collective-permute-start.5 = (bf16[128,8,256]{0,2,1:T(8,128)(2,1)}, bf16[128,8,256]{0,2,1:T(8,128)(2,1)S(1)}, u32[]{:S(2)}, u32[]{:S(2)}) collective-permute-start(bf16[128,8,256]{0,2,1:T(8,128)(2,1)} %collective-permute-done.3), channel_id=1, source_target_pairs={{0,2},{2,4},{4,6},{1,3},{3,5},{5,7},{8,10},{10,12},{12,14},{9,11},... | collective-permute-start | bytes 1572872 | tf_op jit(solution)/shard_map/ppermute | solution.py:28
  1463.9 77.5 %collective-permute-start.6 = (f32[128,8,256]{2,0,1:T(8,128)S(1)}, f32[128,8,256]{2,0,1:T(8,128)S(1)}, u32[]{:S(2)}, u32[]{:S(2)}) collective-permute-start(f32[128,8,256]{2,0,1:T(8,128)S(1)} %convolution_bitcast_fusion.7), channel_id=1, source_target_pairs={{0,2},{2,4},{4,6},{6,0},{1,3},{3,5},{5,7},{7,1},{8,10},{10,12},{12... | collective-permute-start | bytes 3145736 | tf_op jit(solution)/shard_map/ppermute | solution.py:22
  1466.9 117.5 %collective-permute-start.10 = (f32[128,8,256]{2,0,1:T(8,128)S(1)}, f32[128,8,256]{2,0,1:T(8,128)S(1)}, u32[]{:S(2)}, u32[]{:S(2)}) collective-permute-start(f32[128,8,256]{2,0,1:T(8,128)S(1)} %convolution_bitcast_fusion.3), channel_id=1, source_target_pairs={{0,2},{2,4},{4,6},{6,0},{1,3},{3,5},{5,7},{7,1},{8,10},{10,12},{12... | collective-permute-start | bytes 3145736 | tf_op jit(solution)/shard_map/ppermute | solution.py:22
  1541.7 79.2 %collective-permute-start.7 = (f32[128,8,256]{2,0,1:T(8,128)S(1)}, f32[128,8,256]{2,0,1:T(8,128)S(1)}, u32[]{:S(2)}, u32[]{:S(2)}) collective-permute-start(f32[128,8,256]{2,0,1:T(8,128)S(1)} %fusion.42), channel_id=1, source_target_pairs={{0,2},{2,4},{4,6},{6,0},{1,3},{3,5},{5,7},{7,1},{8,10},{10,12},{12... | collective-permute-start | bytes 3145736 | tf_op jit(solution)/shard_map/ppermute | solution.py:22
  1584.8 81.1 %collective-permute-start.11 = (f32[128,8,256]{2,0,1:T(8,128)S(1)}, f32[128,8,256]{2,0,1:T(8,128)S(1)}, u32[]{:S(2)}, u32[]{:S(2)}) collective-permute-start(f32[128,8,256]{2,0,1:T(8,128)S(1)} %fusion.41), channel_id=1, source_target_pairs={{0,2},{2,4},{4,6},{6,0},{1,3},{3,5},{5,7},{7,1},{8,10},{10,12},{12... | collective-permute-start | bytes 3145736 | tf_op jit(solution)/shard_map/ppermute | solution.py:22
  1621.1 83.9 %collective-permute-start.8 = (f32[128,8,256]{2,0,1:T(8,128)S(1)}, f32[128,8,256]{2,0,1:T(8,128)S(1)}, u32[]{:S(2)}, u32[]{:S(2)}) collective-permute-start(f32[128,8,256]{2,0,1:T(8,128)S(1)} %add.304), channel_id=1, source_target_pairs={{0,2},{2,4},{4,6},{6,0},{1,3},{3,5},{5,7},{7,1},{8,10},{10,12},{12... | collective-permute-start | bytes 3145736 | tf_op jit(solution)/shard_map/ppermute | solution.py:22
  1666.0 83.9 %collective-permute-start.12 = (f32[128,8,256]{2,0,1:T(8,128)S(1)}, f32[128,8,256]{2,0,1:T(8,128)S(1)}, u32[]{:S(2)}, u32[]{:S(2)}) collective-permute-start(f32[128,8,256]{2,0,1:T(8,128)S(1)} %add.308), channel_id=1, source_target_pairs={{0,2},{2,4},{4,6},{6,0},{1,3},{3,5},{5,7},{7,1},{8,10},{10,12},{12... | collective-permute-start | bytes 3145736 | tf_op jit(solution)/shard_map/ppermute | solution.py:22
  1705.1 88.0 %collective-permute-start.9 = (f32[128,8,256]{2,0,1:T(8,128)S(1)}, f32[128,8,256]{2,0,1:T(8,128)S(1)}, u32[]{:S(2)}, u32[]{:S(2)}) collective-permute-start(f32[128,8,256]{2,0,1:T(8,128)S(1)} %add.305), channel_id=1, source_target_pairs={{0,2},{2,4},{4,6},{6,0},{1,3},{3,5},{5,7},{7,1},{8,10},{10,12},{12... | collective-permute-start | bytes 3145736 | tf_op jit(solution)/shard_map/ppermute | solution.py:22
  1750.1 87.7 %collective-permute-start.13 = (f32[128,8,256]{2,0,1:T(8,128)S(1)}, f32[128,8,256]{2,0,1:T(8,128)S(1)}, u32[]{:S(2)}, u32[]{:S(2)}) collective-permute-start(f32[128,8,256]{2,0,1:T(8,128)S(1)} %add.309), channel_id=1, source_target_pairs={{0,2},{2,4},{4,6},{6,0},{1,3},{3,5},{5,7},{7,1},{8,10},{10,12},{12... | collective-permute-start | bytes 3145736 | tf_op jit(solution)/shard_map/ppermute | solution.py:22
  1837.8 1.0 copy-start.12
  1842.8 79.7 %all-to-all-start = ((bf16[128,8,768]{0,2,1:T(8,128)(2,1)}), bf16[128,8,768]{0,2,1:T(8,128)(2,1)}, u32[]{:S(2)}, u32[]{:S(2)}) async-start(bf16[128,8,768]{0,2,1:T(8,128)(2,1)} %bitcast.34), calls=%async_computation | async-start | bytes 3145728 | tf_op jit(solution)/shard_map/all_to_all | solution.py:269
  1868.6 3.4 copy-start.3
  1868.6 4.7 copy-start.13
  1924.3 9.1 copy-start.17
  1933.4 315.4 %copy-start.11 = (bf16[1,128,2048]{2,1,0:T(8,128)(2,1)S(1)}, bf16[1,128,2048]{2,1,0:T(8,128)(2,1)}, u32[]{:S(2)}) copy-start(bf16[1,128,2048]{2,1,0:T(8,128)(2,1)} %param.15) | copy-start | bytes 1572868
  2269.5 104.3 %all-to-all-start.2 = ((bf16[128,8,1024]{2,0,1:T(8,128)(2,1)}), bf16[128,8,1024]{2,0,1:T(8,128)(2,1)}, u32[]{:S(2)}, u32[]{:S(2)}) async-start(bf16[128,8,1024]{2,0,1:T(8,128)(2,1)} %bitcast.241), calls=%async_computation.2 | async-start | bytes 4194304 | tf_op jit(solution)/shard_map/all_to_all | solution.py:268
  2275.0 323.5 %all-reduce.13.cloned.1.call-start = ((), (), s32[]{:S(2)}) async-start(), calls=%async_computation.12 | async-start | bytes 196608
  2308.8 716.0 %all-reduce.15.cloned.1.call-start = ((), (), s32[]{:S(2)}) async-start(), calls=%async_computation.13 | async-start | bytes 50331648 | tf_op jit(solution)/shard_map/psum | solution.py:306
  2373.8 150.1 %copy-start.18 = (bf16[8,128,256]{2,1,0:T(8,128)(2,1)S(1)}, bf16[8,128,256]{2,1,0:T(8,128)(2,1)}, u32[]{:S(2)}) copy-start(bf16[8,128,256]{2,1,0:T(8,128)(2,1)} %copy.170) | copy-start | bytes 1572868
  2537.8 18.3 copy-start.34
  2537.8 35.5 %copy-start.35 = (u32[32]{0:T(128)S(1)}, u32[32]{0:T(128)}, u32[]{:S(2)}) copy-start(u32[32]{0:T(128)} %constant.80) | copy-start | bytes 388
  2537.9 38.1 %copy-start.14 = (bf16[128,8,256]{0,2,1:T(8,128)(2,1)S(1)}, bf16[128,8,256]{0,2,1:T(8,128)(2,1)}, u32[]{:S(2)}) copy-start(bf16[128,8,256]{0,2,1:T(8,128)(2,1)} %get-tuple-element.75) | copy-start | bytes 1572868
  2575.9 4.8 copy-start.2
  2615.3 416.7 %copy-start.28 = (f32[256]{0:T(256)}, f32[256]{0:T(256)S(1)}, u32[]{:S(2)}) copy-start(f32[256]{0:T(256)S(1)} %get-tuple-element.119) | copy-start | bytes 3076
  3025.4 6.6 copy-start.15
  3025.4 8.9 copy-start.4
  3031.9 6.6 slice-start
  3034.2 5.6 slice-start.1
  (2 other events, 1.5 us)
Sparse Core Ops, SparseCore 0:
  9.6 483.7 all-gather.18
  495.4 124.8 all-gather.22
  622.5 43.8 all-gather.20
  668.3 45.0 all-gather.32
  714.8 636.4 all-gather.24
  1353.3 108.0 all-gather.34
  1464.1 118.5 all-gather.28
  1584.1 664.6 all-gather.26
  2251.5 272.3 all-gather.30
  2528.0 70.4 all-reduce.12
  2602.4 422.3 all-reduce.14
where the time goes:
time: 3060 us; the launch traced here: 3050 us
  waiting for transfers between devices  2400 us (78%)
  blocking collectives  286 us (9%)
  matrix products  162 us (5%)
  starting transfers between devices  127 us (4%)
  local copies, waits for them, and re-layouts  44.3 us (1%)
    all_gather x1, waiting for transfers between devices, body(): lax.all_gather(w_fc1, ('ctx', 'fsdp'), axis=1, tiled=True)  505 us
    psum x1, waiting for transfers between devices, body(): lax.psum((owned[0], owned[1], owned[2], owned[3], owned[4], owned[5], own...  410 us
    all_gather x1, waiting for transfers between devices, body(): lax.all_gather(w_qkv, ('ctx', 'fsdp'), axis=1, tiled=True)  371 us
    ppermute x8, waiting for transfers between devices, from_behind(): return lax.ppermute(value, axis, pairs)  312 us
    all_gather x1, waiting for transfers between devices, body(): lax.all_gather(w_fc2, ('ctx', 'fsdp'), axis=1, tiled=True)  311 us
    all_gather x1, waiting for transfers between devices, body(): lax.all_gather(act_bf, ('ctx', 'fsdp'), axis=0, tiled=True)  138 us
    all_gather x1, waiting for transfers between devices, body(): lax.all_gather(w_out, ('ctx', 'fsdp'), axis=1, tiled=True)  107 us
    all_gather x1, blocking collectives, body(): lax.all_gather(b_fc1, ('ctx', 'fsdp'), axis=0, tiled=True)  75 us
  transfers between devices with their start and end apart: 28, of which 23 were waited for; matrix products, arithmetic and copies ran while one was open for 7% of the time, Pallas kernels for 0%

commit v1 on v0

--- a/solution.py
+++ b/solution.py
@@ -3,6 +3,7 @@
 import jax
 import jax.numpy as jnp
 from jax import lax
+from jax.sharding import Mesh
 from jax.sharding import PartitionSpec as P
 
 HEADS = 8
@@ -337,41 +338,290 @@
     )
 
 
+def rotated(value, axis, steps):
+    count = lax.axis_size(axis)
+    return lax.ppermute(value, axis, [(i, (i + steps) % count) for i in range(count)])
+
+
+def gather_rows(rows):
+    ring = lax.axis_size("ctx")
+    own = [rows] + [rotated(rows, "ctx", r) for r in range(1, ring)]
+    other = [rotated(part, "fsdp", 1) for part in own]
+    return jnp.concatenate(own + other, axis=0)
+
+
+def scatter_rows(partial, ring):
+    rows = partial.shape[0] // (2 * ring)
+    total = None
+    for r in reversed(range(ring)):
+        mine = partial[r * rows : (r + 1) * rows]
+        theirs = partial[(ring + r) * rows : (ring + r + 1) * rows]
+        arrived = rotated(theirs.astype(jnp.bfloat16), "fsdp", 1)
+        block = mine + arrived.astype(jnp.float32)
+        if r:
+            block = rotated(block.astype(jnp.bfloat16), "ctx", -r).astype(jnp.float32)
+        total = block if total is None else total + block
+    return total
+
+
+def from_replicas(piece):
+    x, core = lax.axis_index("x"), lax.axis_index("core")
+    twin = rotated(piece, "core", 1)
+    pair = jnp.where(core == 0, jnp.stack([piece, twin]), jnp.stack([twin, piece]))
+    other = rotated(pair, "x", 1)
+    return jnp.where(x == 0, jnp.stack([pair, other]), jnp.stack([other, pair]))
+
+
+def replica_quarter(parts):
+    x, core = lax.axis_index("x"), lax.axis_index("core")
+    pick = lambda array, at, dim: lax.dynamic_index_in_dim(array, at, dim, keepdims=False)
+    mine = pick(parts, core, 1) + rotated(pick(parts, 1 - core, 1), "core", 1)
+    sent = rotated(pick(mine, 1 - x, 0).astype(jnp.bfloat16), "x", 1)
+    return pick(mine, x, 0) + sent.astype(jnp.float32)
+
+
+def tensor_body(
+    hidden,
+    cotangent,
+    ln1_gain,
+    ln1_bias,
+    ln2_gain,
+    ln2_bias,
+    w_qkv,
+    b_qkv,
+    w_out,
+    b_out,
+    w_fc1,
+    b_fc1,
+    w_fc2,
+    b_fc2,
+):
+    f32, bf16 = jnp.float32, jnp.bfloat16
+    group = ("ctx", "fsdp")
+    ring = lax.axis_size("ctx")
+    members = ring * lax.axis_size("fsdp")
+    place = lax.axis_index(group)
+    replica = lax.axis_index(("x", "core"))
+    inputs, upstream_own = hidden[0], cotangent[0]
+    row_count, width = inputs.shape
+    length = ring * row_count
+    cols = width // members
+    units = w_fc1.shape[1]
+    slots = w_qkv.shape[1] // HEAD
+    score_scale = HEAD ** (-0.5)
+
+    def quarter(array, dim):
+        size = array.shape[dim] // 4
+        return lax.dynamic_slice_in_dim(array, replica * size, size, dim)
+
+    rows = gather_rows(inputs)
+    small = jnp.concatenate([ln1_gain, ln1_bias, ln2_gain, ln2_bias, b_out, b_fc2, b_qkv])
+    small = lax.all_gather(small, group, axis=0, tiled=False).astype(f32)
+    gain_one, shift_one, gain_two, shift_two, full_bout, full_bfc2 = (
+        small[:, i * cols : (i + 1) * cols].reshape(width) for i in range(6)
+    )
+    full_bqkv = small[:, 6 * cols :].reshape(3 * HEADS, HEAD)
+
+    qkv_quarter = quarter(w_qkv, 0)
+    qkv_moved = [
+        lax.ppermute(
+            qkv_quarter[:, s * HEAD : (s + 1) * HEAD],
+            group,
+            [(i, (slots * i + s) % members) for i in range(members)],
+        )
+        for s in range(slots)
+    ]
+    head_qkv = from_replicas(jnp.concatenate(qkv_moved, axis=1)).reshape(width, slots * HEAD)
+
+    moved = jnp.concatenate(
+        [
+            quarter(w_fc2.reshape(members, units, cols), 1),
+            quarter(w_out.reshape(members, HEAD, cols), 1),
+        ],
+        axis=1,
+    )
+    moved = lax.all_to_all(moved, group, split_axis=0, concat_axis=0, tiled=True)
+    moved = from_replicas(moved).reshape(4, members, (units + HEAD) // 4, cols)
+    rows_fc2 = jnp.transpose(moved[:, :, : units // 4], (0, 2, 1, 3)).reshape(units, width)
+    rows_out = jnp.transpose(moved[:, :, units // 4 :], (0, 2, 1, 3)).reshape(HEAD, width)
+
+    upstream = gather_rows(upstream_own)
+
+    kind_of = [[0] * slots for _ in range(members)]
+    slot_of = [[0] * slots for _ in range(members)]
+    for source in range(members):
+        for s in range(slots):
+            block = slots * source + s
+            kind_of[block % members][s] = block // HEADS
+            slot_of[block % members][block // HEADS] = s
+    kinds = jnp.asarray(kind_of, jnp.int32)[place]
+    where_is = jnp.asarray(slot_of, jnp.int32)[place]
+
+    inputs_f = rows.astype(f32)
+    normed, _ = normalize(inputs_f)
+    attn_in = (normed * gain_one + shift_one).astype(bf16)
+    mlp_in = (normed * gain_two + shift_two).astype(bf16)
+
+    joined = jnp.dot(attn_in, head_qkv, preferred_element_type=f32)
+    bias_rows = kinds * HEADS + place
+    joined = joined.reshape(2, length, slots, HEAD) + full_bqkv[bias_rows]
+    token_pos = (
+        ((lax.axis_index("ctx") - jnp.arange(ring)) % ring)[:, None] * row_count
+        + jnp.arange(row_count)[None]
+    ).reshape(length)
+    cosine, sine_table = rotary_tables(token_pos.astype(f32), ROT)
+    cosine, sine_table = cosine[None, :, 0], sine_table[None, :, 0]
+    pick = lambda kind: lax.dynamic_index_in_dim(joined, where_is[kind], 2, keepdims=False)
+    queries = rotate(pick(0), cosine, sine_table, ROT).astype(bf16)
+    keys = rotate(pick(1), cosine, sine_table, ROT).astype(bf16)
+    values = pick(2).astype(bf16)
+    visible = (token_pos[:, None] >= token_pos[None, :])[None]
+    scores = jnp.einsum("sqd,skd->sqk", queries, keys, preferred_element_type=f32) * score_scale
+    scores = jnp.where(visible, scores, MASKED)
+    row_top = jnp.max(scores, axis=-1, keepdims=True)
+    weights_exp = jnp.where(visible, jnp.exp(scores - row_top), 0.0)
+    row_total = jnp.sum(weights_exp, axis=-1, keepdims=True)
+    mixed = jnp.einsum("sqk,skd->sqd", weights_exp.astype(bf16), values, preferred_element_type=f32)
+    attended = (mixed / row_total).astype(bf16)
+    log_total = row_top + jnp.log(row_total)
+    attended_flat = attended.reshape(2 * length, HEAD)
+
+    preact = jnp.dot(mlp_in, w_fc1, preferred_element_type=f32) + b_fc1.astype(f32)
+    activated, slope = gelu_parts(preact)
+    act_bf = activated.astype(bf16)
+    branch = jnp.dot(attended_flat, rows_out, preferred_element_type=f32) + jnp.dot(
+        act_bf, rows_fc2, preferred_element_type=f32
+    )
+    branch = scatter_rows(branch, ring)
+    own_f = inputs.astype(f32)
+    output = (own_f + (branch + full_bout + full_bfc2)).astype(bf16)
+
+    d_act = contract_cols(upstream, rows_fc2)
+    d_preact = d_act * slope
+    d_preact_bf = d_preact.astype(bf16)
+    fc1_bias_part = jnp.sum(d_preact, axis=0)
+    d_mlp_in = contract_cols(d_preact_bf, w_fc1)
+    d_attended = contract_cols(upstream, rows_out).astype(bf16).reshape(2, length, HEAD)
+    row_dot = jnp.sum(d_attended.astype(f32) * attended.astype(f32), axis=-1, keepdims=True)
+    probability = jnp.where(visible, jnp.exp(scores - log_total), 0.0)
+    d_probability = jnp.einsum("sqd,skd->sqk", d_attended, values, preferred_element_type=f32)
+    d_scores = (probability * (d_probability - row_dot) * score_scale).astype(bf16)
+    d_queries = jnp.einsum("sqk,skd->sqd", d_scores, keys, preferred_element_type=f32)
+    d_keys = jnp.einsum("sqk,sqd->skd", d_scores, queries, preferred_element_type=f32)
+    d_values = jnp.einsum(
+        "sqk,sqd->skd", probability.astype(bf16), d_attended, preferred_element_type=f32
+    )
+    d_queries = rotate(d_queries, cosine, -sine_table, ROT).reshape(2 * length, HEAD)
+    d_keys = rotate(d_keys, cosine, -sine_table, ROT).reshape(2 * length, HEAD)
+    d_values = d_values.reshape(2 * length, HEAD)
+    by_kind = (d_queries, d_keys, d_values)
+    bias_kind = jnp.stack([jnp.sum(grad, axis=0) for grad in by_kind])
+    by_kind = jnp.stack([grad.astype(bf16) for grad in by_kind])
+    d_joined_bf = jnp.concatenate(
+        [lax.dynamic_index_in_dim(by_kind, kinds[s], 0, keepdims=False) for s in range(slots)], axis=1
+    )
+    d_attn_in = contract_cols(d_joined_bf, head_qkv)
+
+    merged = scatter_rows(d_attn_in * gain_one + d_mlp_in * gain_two, ring)
+    own_normed, own_std = normalize(own_f)
+    input_grad = (
+        upstream_own.astype(f32) + norm_backward(merged, own_normed, own_std)
+    ).astype(bf16)
+
+    bqkv_all = jnp.zeros((3, HEADS, HEAD), f32)
+    bqkv_all = lax.dynamic_update_slice(bqkv_all, bias_kind[:, None], (0, place, 0))
+    upstream_sum = jnp.sum(upstream_own.astype(f32), axis=0)
+    vectors = [
+        jnp.sum(d_attn_in * normed, axis=0),
+        jnp.sum(d_attn_in, axis=0),
+        jnp.sum(d_mlp_in * normed, axis=0),
+        jnp.sum(d_mlp_in, axis=0),
+        upstream_sum,
+        bqkv_all.reshape(3 * width),
+    ]
+    vectors = jnp.concatenate([v.reshape(members, -1) for v in vectors], axis=1)
+    fc1_all = lax.dynamic_update_slice(
+        jnp.zeros((members, units), f32), fc1_bias_part[None], (place, 0)
+    )
+    vectors = lax.psum(
+        jnp.concatenate([vectors, fc1_all], axis=1), ("x", "core", "ctx", "fsdp")
+    )
+    vectors = lax.dynamic_index_in_dim(vectors, place, 0, keepdims=False)
+    g1, s1, g2, s2, bout_grad = (vectors[i * cols : (i + 1) * cols] for i in range(5))
+    bqkv_grad = vectors[5 * cols : 5 * cols + slots * HEAD]
+    bfc1_grad = vectors[5 * cols + slots * HEAD :]
+
+    fc2_part = contract_rows(act_bf, upstream).reshape(2, 2, units // 4, width)
+    out_part = contract_rows(attended_flat, upstream).reshape(2, 2, HEAD // 4, width)
+    rows_part = replica_quarter(jnp.concatenate([fc2_part, out_part], axis=2))
+    rows_part = rows_part.astype(bf16).reshape(-1, members, cols)
+    back = lax.all_to_all(
+        jnp.transpose(rows_part, (1, 0, 2)), group, split_axis=0, concat_axis=0, tiled=True
+    )
+    back = from_replicas(back).reshape(4, members, (units + HEAD) // 4, cols)
+    fc2_grad = jnp.transpose(back[:, :, : units // 4], (1, 0, 2, 3)).reshape(-1, cols).astype(f32)
+    out_grad = jnp.transpose(back[:, :, units // 4 :], (1, 0, 2, 3)).reshape(-1, cols).astype(f32)
+
+    fc1_part = contract_rows(mlp_in, d_preact_bf).reshape(2, width // 2, units)
+    core = lax.axis_index("core")
+    half = lax.dynamic_index_in_dim(fc1_part, core, 0, keepdims=False) + rotated(
+        lax.dynamic_index_in_dim(fc1_part, 1 - core, 0, keepdims=False), "core", 1
+    )
+    half = half.astype(bf16)
+    half = half.astype(f32) + rotated(half, "x", 1).astype(f32)
+    twin = rotated(half, "core", 1)
+    fc1_grad = jnp.where(core == 0, jnp.stack([half, twin]), jnp.stack([twin, half]))
+    fc1_grad = fc1_grad.reshape(width, units)
+
+    qkv_part = contract_rows(attn_in, d_joined_bf).reshape(2, 2, width // 4, slots * HEAD)
+    qkv_part = replica_quarter(qkv_part).astype(bf16)
+    qkv_back = [
+        lax.ppermute(
+            qkv_part[:, s * HEAD : (s + 1) * HEAD],
+            group,
+            [((slots * i + s) % members, i) for i in range(members)],
+        )
+        for s in range(slots)
+    ]
+    qkv_grad = from_replicas(jnp.concatenate(qkv_back, axis=1)).reshape(width, -1).astype(f32)
+
+    return (
+        output[None],
+        input_grad[None],
+        g1,
+        s1,
+        g2,
+        s2,
+        qkv_grad,
+        bqkv_grad,
+        out_grad,
+        bout_grad,
+        fc1_grad,
+        bfc1_grad,
+        fc2_grad,
+        bout_grad,
+    )
+
+
 def solution(mesh):
+    sizes = dict(mesh.shape)
+    x_size = sizes["dp"] // 2
+    fits = sizes["ctx"] * sizes["fsdp"] == HEADS and sizes["fsdp"] == 2 and sizes["dp"] == 4
+    if fits:
+        mesh = Mesh(
+            mesh.devices.reshape(x_size, 2, sizes["ctx"], sizes["fsdp"]),
+            ("x", "core", "ctx", "fsdp"),
+        )
+        dp = ("x", "core")
+    else:
+        dp = ("dp",)
+    rows = P((*dp, "fsdp"), "ctx", None)
+    vector, matrix = P(("ctx", "fsdp")), P(None, ("ctx", "fsdp"))
+    params = (vector,) * 4 + (matrix, vector) * 4
     return jax.shard_map(
-        body,
+        tensor_body if fits else body,
         mesh=mesh,
-        in_specs=(
-            P(("dp", "fsdp"), "ctx", None),
-            P(("dp", "fsdp"), "ctx", None),
-            P(("ctx", "fsdp")),
-            P(("ctx", "fsdp")),
-            P(("ctx", "fsdp")),
-            P(("ctx", "fsdp")),
-            P(None, ("ctx", "fsdp")),
-            P(("ctx", "fsdp")),
-            P(None, ("ctx", "fsdp")),
-            P(("ctx", "fsdp")),
-            P(None, ("ctx", "fsdp")),
-            P(("ctx", "fsdp")),
-            P(None, ("ctx", "fsdp")),
-            P(("ctx", "fsdp")),
-        ),
-        out_specs=(
-            P(("dp", "fsdp"), "ctx", None),
-            P(("dp", "fsdp"), "ctx", None),
-            P(("ctx", "fsdp")),
-            P(("ctx", "fsdp")),
-            P(("ctx", "fsdp")),
-            P(("ctx", "fsdp")),
-            P(None, ("ctx", "fsdp")),
-            P(("ctx", "fsdp")),
-            P(None, ("ctx", "fsdp")),
-            P(("ctx", "fsdp")),
-            P(None, ("ctx", "fsdp")),
-            P(("ctx", "fsdp")),
-            P(None, ("ctx", "fsdp")),
-            P(("ctx", "fsdp")),
-        ),
+        in_specs=(rows, rows, *params),
+        out_specs=(rows, rows, *params),
         check_vma=False,
     )

time: 3060 us -> 814 us (0.27)
  waiting for transfers between devices: 2400 us -> 315 us
  blocking collectives: 286 us -> 73.1 us
  other arithmetic: 15.6 us -> 94.4 us
  matrix products: 162 us -> 93.8 us
  local copies, waits for them, and re-layouts: 44.3 us -> 92.1 us
    all_gather x9 -> x0, waiting for transfers between devices: 1510 us -> none  [the longest x1 505 us: body(): lax.all_gather(w_fc1, ('ctx', 'fsdp'), axis=1, tiled=True)]
    psum x1, waiting for transfers between devices: 410 us -> 124 us  [tensor_body(): lax.psum(jnp.concatenate([vectors, fc1_all], axis=1), ('x', 'core', 'ctx'...]
    all_gather x8 -> x1, blocking collectives: 274 us -> 73.1 us  [tensor_body(): small = lax.all_gather(small, group, axis=0, tiled=False).astype(f32)]
    ppermute x14 -> x49, waiting for transfers between devices: 356 us -> 191 us  [the longest x43 191 us: rotated(): lax.ppermute(value, axis, [(i, (i + steps) % count) for i in range(count)])]
    all_to_all x3 -> x2, waiting for transfers between devices: 113 us -> 0.01 us  [the longest x1 0.01 us: tensor_body(): lax.all_to_all(jnp.transpose(rows_part, (1, 0, 2)), group, split_axis=0,...]
    select_n x0 -> x14, other arithmetic: none -> 31.7 us  [the longest x4 13.9 us: from_replicas(): return jnp.where(x == 0, jnp.stack([pair, other]), jnp.stack([other, pair]))]
    dot_general x26 -> x10, matrix products: 65 us -> 39.9 us  [the longest x1 9.61 us: tensor_body(): jnp.dot(attended_flat, rows_out, preferred_element_type=f32)]
    ppermute x14 -> x49, starting transfers between devices: 88.3 us -> 99.4 us  [the longest x43 69.3 us: rotated(): lax.ppermute(value, axis, [(i, (i + steps) % count) for i in range(count)])]
  transfers between devices with their start and end apart: 28 -> 52, of which waited for: 23 -> 17; matrix products, arithmetic and copies ran while one was open for 7% -> 27% of each run, Pallas kernels for 0% -> 0%
where the time goes in v1:
time: 814 us; the launch traced here: 805 us
  waiting for transfers between devices  315 us (39%)
  starting transfers between devices  115 us (14%)
  other arithmetic  94.4 us (12%)
  matrix products  93.8 us (12%)
  local copies, waits for them, and re-layouts  92.1 us (11%)
  blocking collectives  73.1 us (9%)
  between operations  21.8 us (3%)
    ppermute x43, waiting for transfers between devices, rotated(): lax.ppermute(value, axis, [(i, (i + steps) % count) for i in range(count)])  191 us
    psum x1, waiting for transfers between devices, tensor_body(): lax.psum(jnp.concatenate([vectors, fc1_all], axis=1), ('x', 'core', 'ctx'...  124 us
    all_gather x1, blocking collectives, tensor_body(): small = lax.all_gather(small, group, axis=0, tiled=False).astype(f32)  73.1 us
    ppermute x43, starting transfers between devices, rotated(): lax.ppermute(value, axis, [(i, (i + steps) % count) for i in range(count)])  69.3 us
    unnamed x200, local copies, waits for them, and re-layouts  46 us
    dot_general x4, matrix products, contract_cols(): lax.dot_general(left, right, (((1,), (1,)), ((), ())), preferred_element_...  32.6 us
    dot_general x4, matrix products, contract_rows(): lax.dot_general(left, right, (((0,), (0,)), ((), ())), preferred_element_...  21.3 us
    ppermute x3, starting transfers between devices, tensor_body(): lax.ppermute(qkv_part[:, s * HEAD:(s + 1) * HEAD], group, [((slots * i +...  20.4 us
  transfers between devices with their start and end apart: 52, of which 17 were waited for; matrix products, arithmetic and copies ran while one was open for 27% of the time, Pallas kernels for 0%

profile of v1, /device:TPU:0, one launch (start us, length us, event | category | flops | bytes accessed | tf_op | source)
XLA Modules:
  0.0 805.4 jit_solution(16676672140685399920)
XLA Ops:
  7.2 3.1 collective-permute-start
  15.5 3.7 all-to-all-start
  21.1 4.8 collective-permute-start.8
  25.9 4.3 collective-permute-start.9
  33.5 73.1 %all-gather.1 = bf16[8,1,2304]{2,1,0:T(2,128)(2,1)S(1)} all-gather(bf16[1,1,2304]{2,1,0:T(2,128)(2,1)S(1)} %reshape.769), channel_id=2, replica_groups=mesh['x'=2,'core'=2,'ctx'=4,'fsdp'=2] {'ctx','fsdp'}, dimensions={0}, use_global_device_ids=true | all-gather | bytes 41472 | tf_op jit(solution)/shard_map/all_gather | solution.py:419
  130.1 3.3 collective-permute-start.23
  135.3 14.7 %collective-permute-done.2 = bf16[128,2048]{1,0:T(8,128)(2,1)S(1)} collective-permute-done((bf16[128,2048]{1,0:T(8,128)(2,1)S(1)}, bf16[128,2048]{1,0:T(8,128)(2,1)S(1)}, u32[]{:S(2)}, u32[]{:S(2)}) %collective-permute-start.2) | collective-permute-done | bytes 524320 | tf_op jit(solution)/shard_map/ppermute | solution.py:343
  154.5 12.4 %collective-permute-done.22 = bf16[128,2048]{1,0:T(8,128)(2,1)S(1)} collective-permute-done((bf16[128,2048]{1,0:T(8,128)(2,1)}, bf16[128,2048]{1,0:T(8,128)(2,1)S(1)}, u32[]{:S(2)}, u32[]{:S(2)}) %collective-permute-start.22) | collective-permute-done | bytes 524320 | tf_op jit(solution)/shard_map/ppermute | solution.py:343
  175.6 10.4 %collective-permute-done.5 = bf16[128,2048]{1,0:T(8,128)(2,1)S(1)} collective-permute-done((bf16[128,2048]{1,0:T(8,128)(2,1)}, bf16[128,2048]{1,0:T(8,128)(2,1)S(1)}, u32[]{:S(2)}, u32[]{:S(2)}) %collective-permute-start.5) | collective-permute-done | bytes 524320 | tf_op jit(solution)/shard_map/ppermute | solution.py:343
  186.8 10.4 %collective-permute-done.6 = bf16[128,2048]{1,0:T(8,128)(2,1)S(1)} collective-permute-done((bf16[128,2048]{1,0:T(8,128)(2,1)S(1)}, bf16[128,2048]{1,0:T(8,128)(2,1)S(1)}, u32[]{:S(2)}, u32[]{:S(2)}) %collective-permute-start.6) | collective-permute-done | bytes 524320 | tf_op jit(solution)/shard_map/ppermute | solution.py:343
  198.0 3.0 convert_reduce_fusion
  205.7 7.3 multiply_convert_fusion
  213.0 3.1 fusion.7
  217.0 2.7 collective-permute-done.26
  220.8 6.1 collective-permute-done.27
  228.8 9.0 %fusion.113 = f32[1024,2048]{1,0:T(8,128)} fusion(bf16[1024,1024]{1,0:T(8,128)(2,1)S(1)} %copy-done.67, bf16[1024,2048]{1,0:T(8,128)(2,1)} %constant_dynamic-update-slice_fusion.11), kind=kOutput, calls=%fused_computation.248 | convolution fusion | flops 4294967296 | bytes 14680064 | tf_op jit(solution)/shard_map/dot_general | solution.py:76
  241.1 3.7 maximum_select_fusion.3
  244.8 4.7 copy.100
  249.6 6.3 convolution_add_fusion.1
  264.7 30.0 %collective-permute-done.13 = bf16[2,8,320,256]{3,2,1,0:T(8,128)(2,1)} collective-permute-done((bf16[2,8,320,256]{3,2,1,0:T(8,128)(2,1)}, bf16[2,8,320,256]{3,2,1,0:T(8,128)(2,1)}, u32[]{:S(2)}, u32[]{:S(2)}) %collective-permute-start.13) | collective-permute-done | bytes 2621472 | tf_op jit(solution)/shard_map/ppermute | solution.py:343
  294.7 4.0 maximum_select_fusion.1
  300.2 3.9 convolution_convert_fusion
  305.9 2.9 multiply_reduce_fusion
  315.4 3.5 copy.150
  322.1 2.7 multiply_subtract_fusion.1
  331.6 3.5 fusion.71
  335.2 2.7 copy-done.12
  340.1 3.4 fusion.23
  343.5 5.6 fusion.14
  349.7 8.5 %fusion.111 = (f32[1024]{0:T(1024)}, bf16[1024,1024]{1,0:T(8,128)(2,1)S(1)}) fusion(f32[1024,1024]{1,0:T(8,128)S(1)} %copy-done.69, f32[1024]{0:T(1024)S(1)} %copy-done.53, bf16[1024,2048]{1,0:T(8,128)(2,1)} %constant_dynamic-update-slice_fusion.11, bf16[1024,2048]{1,0:T(8,128)(2,1)S(1)} %bitcast.248), kind=kOutput, calls=%fused_computation.246 | convolution fusion | flops 4307549184 | bytes 14688256 | tf_op jit(solution)/shard_map/dot_general | solution.py:82
  358.3 5.3 fusion.56
  365.9 3.2 copy-done.9
  369.7 6.9 fusion.58
  376.6 6.8 fusion.112
  383.4 13.4 %fusion.95 = (f32[2048]{0:T(1024)}, f32[2048]{0:T(1024)}, bf16[1024,2048]{1,0:T(8,128)(2,1)}, f32[1024,2048]{1,0:T(8,128)}, f32[2048]{0:T(1024)}, /*index=5*/f32[2048]{0:T(1024)}) fusion(f32[1024,2048]{1,0:T(8,128)} %fusion.58, f32[1024]{0:T(1024)S(1)} %add_rsqrt_fusion, f32[1024]{0:T(1024)S(1)} %broadcast_multiply_fusion, ...), kind=kOutput, calls=%fused_computation.231 | convolution fusion | flops 3253198848 | bytes 29941760 | tf_op jit(solution)/shard_map/dot_general | solution.py:82
  396.8 6.1 fusion.17
  409.8 3.4 bitcast_add_fusion.1
  416.4 4.5 fusion.25
  422.1 14.4 %collective-permute-done.43 = bf16[320,2048]{1,0:T(8,128)(2,1)S(1)} collective-permute-done((bf16[320,2048]{1,0:T(8,128)(2,1)S(1)}, bf16[320,2048]{1,0:T(8,128)(2,1)S(1)}, u32[]{:S(2)}, u32[]{:S(2)}) %collective-permute-start.43) | collective-permute-done | bytes 1310752 | tf_op jit(solution)/shard_map/ppermute | solution.py:343
  438.1 12.0 %all-to-all-start.1 = ((bf16[8,320,256]{2,1,0:T(8,128)(2,1)}), bf16[8,320,256]{2,1,0:T(8,128)(2,1)S(1)}, u32[]{:S(2)}, u32[]{:S(2)}) async-start(bf16[8,320,256]{2,1,0:T(8,128)(2,1)} %bitcast.235), calls=%async_computation.1 | async-start | bytes 2621440 | tf_op jit(solution)/shard_map/all_to_all | solution.py:558
  450.2 9.6 %fusion.110 = (bf16[1024,2048]{1,0:T(8,128)(2,1)}, f32[1024,2048]{1,0:T(8,128)}) fusion(f32[1024,2048]{1,0:T(8,128)} %fusion.112, bf16[1024,256]{1,0:T(8,128)(2,1)} %bitcast.256, bf16[256,2048]{1,0:T(8,128)(2,1)S(1)} %bitcast.247), kind=kOutput, calls=%fused_computation.245 | convolution fusion | flops 1077936128 | bytes 22544384 | tf_op jit(solution)/shard_map/dot_general | solution.py:492
  459.9 3.0 fusion.101
  465.2 3.6 collective-permute-start.37
  468.8 3.6 collective-permute-start.38
  472.4 5.2 collective-permute-start.32
  478.6 13.2 %collective-permute-start.39 = (bf16[512,256]{1,0:T(8,128)(2,1)}, bf16[512,256]{1,0:T(8,128)(2,1)S(1)}, u32[]{:S(2)}, u32[]{:S(2)}) collective-permute-start(bf16[512,256]{1,0:T(8,128)(2,1)} %get-tuple-element.65), channel_id=1, source_target_pairs={{2,0},{5,1},{0,2},{3,3},{6,4},{1,5},{4,6},{7,7},{10,8},{13,9},{8,1... | collective-permute-start | bytes 786440 | tf_op jit(solution)/shard_map/ppermute | solution.py:579
  494.0 3.2 collective-permute-start.30
  497.2 5.1 collective-permute-start.14
  502.9 6.8 fusion.91
  512.2 9.2 %collective-permute-done.20 = bf16[128,2048]{1,0:T(8,128)(2,1)} collective-permute-done((bf16[128,2048]{1,0:T(8,128)(2,1)}, bf16[128,2048]{1,0:T(8,128)(2,1)}, u32[]{:S(2)}, u32[]{:S(2)}) %collective-permute-start.20) | collective-permute-done | bytes 524320 | tf_op jit(solution)/shard_map/ppermute | solution.py:343
  523.5 9.2 %collective-permute-done.14 = bf16[128,2048]{1,0:T(8,128)(2,1)} collective-permute-done((bf16[128,2048]{1,0:T(8,128)(2,1)}, bf16[128,2048]{1,0:T(8,128)(2,1)}, u32[]{:S(2)}, u32[]{:S(2)}) %collective-permute-start.14) | collective-permute-done | bytes 524320 | tf_op jit(solution)/shard_map/ppermute | solution.py:343
  532.7 2.8 fusion.49
  535.5 8.3 %collective-permute-done.18 = bf16[128,2048]{1,0:T(8,128)(2,1)S(1)} collective-permute-done((bf16[128,2048]{1,0:T(8,128)(2,1)}, bf16[128,2048]{1,0:T(8,128)(2,1)S(1)}, u32[]{:S(2)}, u32[]{:S(2)}) %collective-permute-start.18) | collective-permute-done | bytes 524320 | tf_op jit(solution)/shard_map/ppermute | solution.py:343
  543.8 8.5 %collective-permute-start.33 = (bf16[128,2048]{1,0:T(8,128)(2,1)S(1)}, bf16[128,2048]{1,0:T(8,128)(2,1)S(1)}, u32[]{:S(2)}, u32[]{:S(2)}) collective-permute-start(bf16[128,2048]{1,0:T(8,128)(2,1)S(1)} %get-tuple-element.28), channel_id=1, source_target_pairs={{0,6},{2,0},{4,2},{6,4},{1,7},{3,1},{5,3},{7,5},{8,14},{10,8},{12,... | collective-permute-start | bytes 1572872 | tf_op jit(solution)/shard_map/ppermute | solution.py:343
  554.9 7.0 collective-permute-start.29
  566.0 3.0 collective-permute-start.19
  569.0 45.3 %collective-permute-done.31 = bf16[128,2048]{1,0:T(8,128)(2,1)S(1)} collective-permute-done((bf16[128,2048]{1,0:T(8,128)(2,1)S(1)}, bf16[128,2048]{1,0:T(8,128)(2,1)S(1)}, u32[]{:S(2)}, u32[]{:S(2)}) %collective-permute-start.31) | collective-permute-done | bytes 524320 | tf_op jit(solution)/shard_map/ppermute | solution.py:343
  620.5 16.7 %collective-permute-done.17 = bf16[128,2048]{1,0:T(8,128)(2,1)S(1)} collective-permute-done((bf16[128,2048]{1,0:T(8,128)(2,1)S(1)}, bf16[128,2048]{1,0:T(8,128)(2,1)S(1)}, u32[]{:S(2)}, u32[]{:S(2)}) %collective-permute-start.17) | collective-permute-done | bytes 524320 | tf_op jit(solution)/shard_map/ppermute | solution.py:343
  637.2 3.5 convert_reduce_fusion.2
  641.5 123.9 %all-reduce.2.cloned.1.call-done = f32[8,3072]{1,0:T(8,128)} async-done(((f32[8,3072]{1,0:T(8,128)}), f32[8,3072]{1,0:T(8,128)}) %all-reduce.2.cloned.1.call-update) | async-done | bytes 98320 | tf_op jit(solution)/shard_map/psum | solution.py:546
  774.0 3.4 bitcast_convert_fusion
  779.6 7.4 maximum_select_fusion
  787.0 3.7 maximum_select_fusion.2
  793.5 4.0 copy.126
  (378 shorter events, 141.7 us)
Async XLA Ops:
  7.2 120.4 %collective-permute-start = (bf16[128,2048]{1,0:T(8,128)(2,1)}, bf16[128,2048]{1,0:T(8,128)(2,1)}, u32[]{:S(2)}, u32[]{:S(2)}) collective-permute-start(bf16[128,2048]{1,0:T(8,128)(2,1)} %bitcast.213), channel_id=1, source_target_pairs={{0,2},{2,4},{4,6},{6,0},{1,3},{3,5},{5,7},{7,1},{8,10},{10,12},{12... | collective-permute-start | bytes 1572872 | tf_op jit(solution)/shard_map/ppermute | solution.py:343
  10.3 119.8 %collective-permute-start.1 = (bf16[128,2048]{1,0:T(8,128)(2,1)}, bf16[128,2048]{1,0:T(8,128)(2,1)}, u32[]{:S(2)}, u32[]{:S(2)}) collective-permute-start(bf16[128,2048]{1,0:T(8,128)(2,1)} %bitcast.214), channel_id=1, source_target_pairs={{0,4},{2,6},{4,0},{6,2},{1,5},{3,7},{5,1},{7,3},{8,12},{10,14},{12... | collective-permute-start | bytes 1572872 | tf_op jit(solution)/shard_map/ppermute | solution.py:343
  15.5 101.7 %copy-start.56 = (bf16[1024]{0:T(1024)(128)(2,1)S(1)}, bf16[1024]{0:T(1024)(128)(2,1)}, u32[]{:S(2)}) copy-start(bf16[1024]{0:T(1024)(128)(2,1)} %param.27) | copy-start | bytes 6148
  15.5 205.0 %all-to-all-start = ((bf16[8,320,256]{2,1,0:T(8,128)(2,1)}), bf16[8,320,256]{2,1,0:T(8,128)(2,1)S(1)}, u32[]{:S(2)}, u32[]{:S(2)}) async-start(bf16[8,320,256]{2,1,0:T(8,128)(2,1)} %pad_maximum_fusion.2), calls=%async_computation | async-start | bytes 2621440 | tf_op jit(solution)/shard_map/all_to_all | solution.py:443
  20.4 100.7 %collective-permute-start.7 = (bf16[512,256]{1,0:T(8,128)(2,1)S(1)}, bf16[512,256]{1,0:T(8,128)(2,1)S(1)}, u32[]{:S(2)}, u32[]{:S(2)}) collective-permute-start(bf16[512,256]{1,0:T(8,128)(2,1)S(1)} %get-tuple-element.47), channel_id=1, source_target_pairs={{0,0},{1,3},{2,6},{3,1},{4,4},{5,7},{6,2},{7,5},{8,8},{9,11},{10,1... | collective-permute-start | bytes 786440 | tf_op jit(solution)/shard_map/ppermute | solution.py:427
  21.1 102.2 %collective-permute-start.8 = (bf16[512,256]{1,0:T(8,128)(2,1)S(1)}, bf16[512,256]{1,0:T(8,128)(2,1)}, u32[]{:S(2)}, u32[]{:S(2)}) collective-permute-start(bf16[512,256]{1,0:T(8,128)(2,1)S(1)} %get-tuple-element.46), channel_id=1, source_target_pairs={{0,1},{1,4},{2,7},{3,2},{4,5},{5,0},{6,3},{7,6},{8,9},{9,12},{10,1... | collective-permute-start | bytes 786440 | tf_op jit(solution)/shard_map/ppermute | solution.py:427
  25.9 100.7 %collective-permute-start.9 = (bf16[512,256]{1,0:T(8,128)(2,1)S(1)}, bf16[512,256]{1,0:T(8,128)(2,1)}, u32[]{:S(2)}, u32[]{:S(2)}) collective-permute-start(bf16[512,256]{1,0:T(8,128)(2,1)S(1)} %get-tuple-element.45), channel_id=1, source_target_pairs={{0,2},{1,5},{2,0},{3,3},{4,6},{5,1},{6,4},{7,7},{8,10},{9,13},{10,... | collective-permute-start | bytes 786440 | tf_op jit(solution)/shard_map/ppermute | solution.py:427
  31.2 86.2 %copy-start.49 = (f32[128]{0:T(128)}, f32[128]{0:T(128)S(1)}, u32[]{:S(2)}) copy-start(f32[128]{0:T(128)S(1)} %broadcast_multiply_fusion.3) | copy-start | bytes 1540
  117.3 88.4 %copy-start.52 = (f32[1024]{0:T(1024)}, f32[1024]{0:T(1024)S(1)}, u32[]{:S(2)}) copy-start(f32[1024]{0:T(1024)S(1)} %convert_element_type.279) | copy-start | bytes 12292
  117.3 88.4 %copy-start.43 = (f32[1,2,8,128]{3,1,2,0:T(2,128)}, f32[1,2,8,128]{3,1,2,0:T(2,128)S(1)}, u32[]{:S(2)}) copy-start(f32[1,2,8,128]{3,1,2,0:T(2,128)S(1)} %copy.149) | copy-start | bytes 24580
  117.3 88.4 %copy-start.41 = (f32[1,2,8,128]{3,1,2,0:T(2,128)}, f32[1,2,8,128]{3,1,2,0:T(2,128)S(1)}, u32[]{:S(2)}) copy-start(f32[1,2,8,128]{3,1,2,0:T(2,128)S(1)} %copy.148) | copy-start | bytes 24580
  121.8 28.2 %collective-permute-start.2 = (bf16[128,2048]{1,0:T(8,128)(2,1)S(1)}, bf16[128,2048]{1,0:T(8,128)(2,1)S(1)}, u32[]{:S(2)}, u32[]{:S(2)}) collective-permute-start(bf16[128,2048]{1,0:T(8,128)(2,1)S(1)} %bitcast.215), channel_id=1, source_target_pairs={{0,6},{2,0},{4,2},{6,4},{1,7},{3,1},{5,3},{7,5},{8,14},{10,8},{12,... | collective-permute-start | bytes 1572872 | tf_op jit(solution)/shard_map/ppermute | solution.py:343
  123.3 27.5 %collective-permute-start.3 = (bf16[128,2048]{1,0:T(8,128)(2,1)S(1)}, bf16[128,2048]{1,0:T(8,128)(2,1)S(1)}, u32[]{:S(2)}, u32[]{:S(2)}) collective-permute-start(bf16[128,2048]{1,0:T(8,128)(2,1)S(1)} %bitcast.216), channel_id=1, source_target_pairs={{0,1},{1,0},{2,3},{3,2},{4,5},{5,4},{6,7},{7,6},{8,9},{9,8},{10,11... | collective-permute-start | bytes 1572872 | tf_op jit(solution)/shard_map/ppermute | solution.py:343
  126.6 25.1 %collective-permute-start.21 = (bf16[128,2048]{1,0:T(8,128)(2,1)}, bf16[128,2048]{1,0:T(8,128)(2,1)S(1)}, u32[]{:S(2)}, u32[]{:S(2)}) collective-permute-start(bf16[128,2048]{1,0:T(8,128)(2,1)} %bitcast.34), channel_id=1, source_target_pairs={{0,2},{2,4},{4,6},{6,0},{1,3},{3,5},{5,7},{7,1},{8,10},{10,12},{12... | collective-permute-start | bytes 1572872 | tf_op jit(solution)/shard_map/ppermute | solution.py:343
  127.6 39.3 %collective-permute-start.22 = (bf16[128,2048]{1,0:T(8,128)(2,1)}, bf16[128,2048]{1,0:T(8,128)(2,1)S(1)}, u32[]{:S(2)}, u32[]{:S(2)}) collective-permute-start(bf16[128,2048]{1,0:T(8,128)(2,1)} %bitcast.34), channel_id=1, source_target_pairs={{0,4},{2,6},{4,0},{6,2},{1,5},{3,7},{5,1},{7,3},{8,12},{10,14},{12... | collective-permute-start | bytes 1572872 | tf_op jit(solution)/shard_map/ppermute | solution.py:343
  130.1 39.8 %collective-permute-start.23 = (bf16[128,2048]{1,0:T(8,128)(2,1)}, bf16[128,2048]{1,0:T(8,128)(2,1)}, u32[]{:S(2)}, u32[]{:S(2)}) collective-permute-start(bf16[128,2048]{1,0:T(8,128)(2,1)} %bitcast.34), channel_id=1, source_target_pairs={{0,6},{2,0},{4,2},{6,4},{1,7},{3,1},{5,3},{7,5},{8,14},{10,8},{12,... | collective-permute-start | bytes 1572872 | tf_op jit(solution)/shard_map/ppermute | solution.py:343
  150.0 21.8 %collective-permute-start.24 = (bf16[128,2048]{1,0:T(8,128)(2,1)}, bf16[128,2048]{1,0:T(8,128)(2,1)S(1)}, u32[]{:S(2)}, u32[]{:S(2)}) collective-permute-start(bf16[128,2048]{1,0:T(8,128)(2,1)} %bitcast.34), channel_id=1, source_target_pairs={{0,1},{1,0},{2,3},{3,2},{4,5},{5,4},{6,7},{7,6},{8,9},{9,8},{10,11... | collective-permute-start | bytes 1572872 | tf_op jit(solution)/shard_map/ppermute | solution.py:343
  150.8 51.9 %collective-permute-start.10 = (bf16[512,768]{1,0:T(8,128)(2,1)S(1)}, bf16[512,768]{1,0:T(8,128)(2,1)S(1)}, u32[]{:S(2)}, u32[]{:S(2)}) collective-permute-start(bf16[512,768]{1,0:T(8,128)(2,1)S(1)} %constant_dynamic-update-slice_fusion.8), channel_id=1, source_target_pairs={{0,8},{8,0},{1,9},{9,1},{2,10},{10,2},{3,11},{11,3},{4,12},{12,4},... | collective-permute-start | bytes 2359304 | tf_op jit(solution)/shard_map/ppermute | solution.py:343
  151.7 23.1 %collective-permute-start.4 = (bf16[128,2048]{1,0:T(8,128)(2,1)}, bf16[128,2048]{1,0:T(8,128)(2,1)S(1)}, u32[]{:S(2)}, u32[]{:S(2)}) collective-permute-start(bf16[128,2048]{1,0:T(8,128)(2,1)} %collective-permute-done), channel_id=1, source_target_pairs={{0,1},{1,0},{2,3},{3,2},{4,5},{5,4},{6,7},{7,6},{8,9},{9,8},{10,11... | collective-permute-start | bytes 1572872 | tf_op jit(solution)/shard_map/ppermute | solution.py:343
  166.9 19.1 %collective-permute-start.5 = (bf16[128,2048]{1,0:T(8,128)(2,1)}, bf16[128,2048]{1,0:T(8,128)(2,1)S(1)}, u32[]{:S(2)}, u32[]{:S(2)}) collective-permute-start(bf16[128,2048]{1,0:T(8,128)(2,1)} %collective-permute-done.1), channel_id=1, source_target_pairs={{0,1},{1,0},{2,3},{3,2},{4,5},{5,4},{6,7},{7,6},{8,9},{9,8},{10,11... | collective-permute-start | bytes 1572872 | tf_op jit(solution)/shard_map/ppermute | solution.py:343
  169.9 27.3 %collective-permute-start.6 = (bf16[128,2048]{1,0:T(8,128)(2,1)S(1)}, bf16[128,2048]{1,0:T(8,128)(2,1)S(1)}, u32[]{:S(2)}, u32[]{:S(2)}) collective-permute-start(bf16[128,2048]{1,0:T(8,128)(2,1)S(1)} %collective-permute-done.2), channel_id=1, source_target_pairs={{0,1},{1,0},{2,3},{3,2},{4,5},{5,4},{6,7},{7,6},{8,9},{9,8},{10,11... | collective-permute-start | bytes 1572872 | tf_op jit(solution)/shard_map/ppermute | solution.py:343
  171.8 44.4 %collective-permute-start.25 = (bf16[128,2048]{1,0:T(8,128)(2,1)S(1)}, bf16[128,2048]{1,0:T(8,128)(2,1)S(1)}, u32[]{:S(2)}, u32[]{:S(2)}) collective-permute-start(bf16[128,2048]{1,0:T(8,128)(2,1)S(1)} %collective-permute-done.21), channel_id=1, source_target_pairs={{0,1},{1,0},{2,3},{3,2},{4,5},{5,4},{6,7},{7,6},{8,9},{9,8},{10,11... | collective-permute-start | bytes 1572872 | tf_op jit(solution)/shard_map/ppermute | solution.py:343
  174.7 44.9 %collective-permute-start.26 = (bf16[128,2048]{1,0:T(8,128)(2,1)S(1)}, bf16[128,2048]{1,0:T(8,128)(2,1)S(1)}, u32[]{:S(2)}, u32[]{:S(2)}) collective-permute-start(bf16[128,2048]{1,0:T(8,128)(2,1)S(1)} %collective-permute-done.22), channel_id=1, source_target_pairs={{0,1},{1,0},{2,3},{3,2},{4,5},{5,4},{6,7},{7,6},{8,9},{9,8},{10,11... | collective-permute-start | bytes 1572872 | tf_op jit(solution)/shard_map/ppermute | solution.py:343
  186.0 40.9 %collective-permute-start.27 = (bf16[128,2048]{1,0:T(8,128)(2,1)}, bf16[128,2048]{1,0:T(8,128)(2,1)}, u32[]{:S(2)}, u32[]{:S(2)}) collective-permute-start(bf16[128,2048]{1,0:T(8,128)(2,1)} %collective-permute-done.23), channel_id=1, source_target_pairs={{0,1},{1,0},{2,3},{3,2},{4,5},{5,4},{6,7},{7,6},{8,9},{9,8},{10,11... | collective-permute-start | bytes 1572872 | tf_op jit(solution)/shard_map/ppermute | solution.py:343
  204.2 36.9 %collective-permute-start.11 = (bf16[2,512,768]{2,1,0:T(8,128)(2,1)}, bf16[2,512,768]{2,1,0:T(8,128)(2,1)}, u32[]{:S(2)}, u32[]{:S(2)}) collective-permute-start(bf16[2,512,768]{2,1,0:T(8,128)(2,1)} %maximum_select_fusion.10), channel_id=1, source_target_pairs={{0,16},{16,0},{1,17},{17,1},{2,18},{18,2},{3,19},{19,3},{4,20},{20... | collective-permute-start | bytes 4718600 | tf_op jit(solution)/shard_map/ppermute | solution.py:343
  220.5 17.3 %collective-permute-start.12 = (bf16[8,320,256]{2,1,0:T(8,128)(2,1)S(1)}, bf16[8,320,256]{2,1,0:T(8,128)(2,1)S(1)}, u32[]{:S(2)}, u32[]{:S(2)}) collective-permute-start(bf16[8,320,256]{2,1,0:T(8,128)(2,1)S(1)} %all-to-all-done), channel_id=1, source_target_pairs={{0,8},{8,0},{1,9},{9,1},{2,10},{10,2},{3,11},{11,3},{4,12},{12,4},... | collective-permute-start | bytes 3932168 | tf_op jit(solution)/shard_map/ppermute | solution.py:343
  239.6 55.1 %collective-permute-start.13 = (bf16[2,8,320,256]{3,2,1,0:T(8,128)(2,1)}, bf16[2,8,320,256]{3,2,1,0:T(8,128)(2,1)}, u32[]{:S(2)}, u32[]{:S(2)}) collective-permute-start(bf16[2,8,320,256]{3,2,1,0:T(8,128)(2,1)} %maximum_select_fusion.6), channel_id=1, source_target_pairs={{0,16},{16,0},{1,17},{17,1},{2,18},{18,2},{3,19},{19,3},{4,20},{20... | collective-permute-start | bytes 7864328 | tf_op jit(solution)/shard_map/ppermute | solution.py:343
  339.8 69.9 %collective-permute-start.35 = (f32[2,512,768]{2,1,0:T(8,128)}, f32[2,512,768]{2,1,0:T(8,128)}, u32[]{:S(2)}, u32[]{:S(2)}) collective-permute-start(f32[2,512,768]{2,1,0:T(8,128)} %dynamic-slice_bitcast_fusion.1), channel_id=1, source_target_pairs={{0,8},{8,0},{1,9},{9,1},{2,10},{10,2},{3,11},{11,3},{4,12},{12,4},... | collective-permute-start | bytes 9437192 | tf_op jit(solution)/shard_map/ppermute | solution.py:343
  349.1 47.7 %collective-permute-start.42 = (f32[2,320,2048]{2,1,0:T(8,128)}, f32[2,320,2048]{2,1,0:T(8,128)}, u32[]{:S(2)}, u32[]{:S(2)}) collective-permute-start(f32[2,320,2048]{2,1,0:T(8,128)} %fusion.14), channel_id=1, source_target_pairs={{0,8},{8,0},{1,9},{9,1},{2,10},{10,2},{3,11},{11,3},{4,12},{12,4},... | collective-permute-start | bytes 15728648 | tf_op jit(solution)/shard_map/ppermute | solution.py:343
  369.2 47.2 %collective-permute-start.46 = (f32[1024,1024]{1,0:T(8,128)}, f32[1024,1024]{1,0:T(8,128)}, u32[]{:S(2)}, u32[]{:S(2)}) collective-permute-start(f32[1024,1024]{1,0:T(8,128)} %dynamic-slice_bitcast_fusion), channel_id=1, source_target_pairs={{0,8},{8,0},{1,9},{9,1},{2,10},{10,2},{3,11},{11,3},{4,12},{12,4},... | collective-permute-start | bytes 12582920 | tf_op jit(solution)/shard_map/ppermute | solution.py:343
  404.8 31.7 %collective-permute-start.43 = (bf16[320,2048]{1,0:T(8,128)(2,1)S(1)}, bf16[320,2048]{1,0:T(8,128)(2,1)S(1)}, u32[]{:S(2)}, u32[]{:S(2)}) collective-permute-start(bf16[320,2048]{1,0:T(8,128)(2,1)S(1)} %fusion.31), channel_id=1, source_target_pairs={{0,16},{16,0},{1,17},{17,1},{2,18},{18,2},{3,19},{19,3},{4,20},{20... | collective-permute-start | bytes 3932168 | tf_op jit(solution)/shard_map/ppermute | solution.py:343
  407.7 86.2 %collective-permute-start.34 = (bf16[128,2048]{1,0:T(8,128)(2,1)}, bf16[128,2048]{1,0:T(8,128)(2,1)}, u32[]{:S(2)}, u32[]{:S(2)}) collective-permute-start(bf16[128,2048]{1,0:T(8,128)(2,1)} %get-tuple-element.36), channel_id=1, source_target_pairs={{0,1},{1,0},{2,3},{3,2},{4,5},{5,4},{6,7},{7,6},{8,9},{9,8},{10,11... | collective-permute-start | bytes 1572872 | tf_op jit(solution)/shard_map/ppermute | solution.py:343
  409.5 87.7 %collective-permute-start.28 = (bf16[128,2048]{1,0:T(8,128)(2,1)}, bf16[128,2048]{1,0:T(8,128)(2,1)}, u32[]{:S(2)}, u32[]{:S(2)}) collective-permute-start(bf16[128,2048]{1,0:T(8,128)(2,1)} %get-tuple-element.35), channel_id=1, source_target_pairs={{0,1},{1,0},{2,3},{3,2},{4,5},{5,4},{6,7},{7,6},{8,9},{9,8},{10,11... | collective-permute-start | bytes 1572872 | tf_op jit(solution)/shard_map/ppermute | solution.py:343
  415.8 47.1 %collective-permute-start.36 = (bf16[512,768]{1,0:T(8,128)(2,1)}, bf16[512,768]{1,0:T(8,128)(2,1)}, u32[]{:S(2)}, u32[]{:S(2)}) collective-permute-start(bf16[512,768]{1,0:T(8,128)(2,1)} %fusion.66), channel_id=1, source_target_pairs={{0,16},{16,0},{1,17},{17,1},{2,18},{18,2},{3,19},{19,3},{4,20},{20... | collective-permute-start | bytes 2359304 | tf_op jit(solution)/shard_map/ppermute | solution.py:343
  420.9 29.3 %copy-start.19 = (bf16[32,8,8,256]{3,1,2,0:T(8,128)(2,1)S(1)}, bf16[32,8,8,256]{3,1,2,0:T(8,128)(2,1)}, u32[]{:S(2)}) copy-start(bf16[32,8,8,256]{3,1,2,0:T(8,128)(2,1)} %copy-done.18) | copy-start | bytes 3145732
  420.9 81.5 %collective-permute-start.47 = (bf16[1024,1024]{1,0:T(8,128)(2,1)}, bf16[1024,1024]{1,0:T(8,128)(2,1)}, u32[]{:S(2)}, u32[]{:S(2)}) collective-permute-start(bf16[1024,1024]{1,0:T(8,128)(2,1)} %fusion.25), channel_id=1, source_target_pairs={{0,16},{16,0},{1,17},{17,1},{2,18},{18,2},{3,19},{19,3},{4,20},{20... | collective-permute-start | bytes 6291464 | tf_op jit(solution)/shard_map/ppermute | solution.py:343
  438.1 64.4 %all-to-all-start.1 = ((bf16[8,320,256]{2,1,0:T(8,128)(2,1)}), bf16[8,320,256]{2,1,0:T(8,128)(2,1)S(1)}, u32[]{:S(2)}, u32[]{:S(2)}) async-start(bf16[8,320,256]{2,1,0:T(8,128)(2,1)} %bitcast.235), calls=%async_computation.1 | async-start | bytes 2621440 | tf_op jit(solution)/shard_map/all_to_all | solution.py:558
  450.1 315.2 %all-reduce.2.cloned.1.call-start = ((), (), s32[]{:S(2)}) async-start(), calls=%async_computation.2 | async-start | bytes 196608 | tf_op jit(solution)/shard_map/psum | solution.py:546
  462.9 28.8 %copy-start.58 = (f32[256]{0:T(256)S(1)}, f32[256]{0:T(256)}, u32[]{:S(2)}) copy-start(f32[256]{0:T(256)} %get-tuple-element.59) | copy-start | bytes 3076
  462.9 29.0 %copy-start.54 = (f32[1024]{0:T(1024)S(1)}, f32[1024]{0:T(1024)}, u32[]{:S(2)}) copy-start(f32[1024]{0:T(1024)} %get-tuple-element.103) | copy-start | bytes 12292
  465.2 7.3 collective-permute-start.37
  468.8 9.7 %collective-permute-start.38 = (bf16[512,256]{1,0:T(8,128)(2,1)}, bf16[512,256]{1,0:T(8,128)(2,1)}, u32[]{:S(2)}, u32[]{:S(2)}) collective-permute-start(bf16[512,256]{1,0:T(8,128)(2,1)} %get-tuple-element.66), channel_id=1, source_target_pairs={{1,0},{4,1},{7,2},{2,3},{5,4},{0,5},{3,6},{6,7},{9,8},{12,9},{15,1... | collective-permute-start | bytes 786440 | tf_op jit(solution)/shard_map/ppermute | solution.py:579
  472.4 29.9 %collective-permute-start.32 = (bf16[128,2048]{1,0:T(8,128)(2,1)}, bf16[128,2048]{1,0:T(8,128)(2,1)}, u32[]{:S(2)}, u32[]{:S(2)}) collective-permute-start(bf16[128,2048]{1,0:T(8,128)(2,1)} %get-tuple-element.37), channel_id=1, source_target_pairs={{0,1},{1,0},{2,3},{3,2},{4,5},{5,4},{6,7},{7,6},{8,9},{9,8},{10,11... | collective-permute-start | bytes 1572872 | tf_op jit(solution)/shard_map/ppermute | solution.py:343
  478.6 18.7 %collective-permute-start.39 = (bf16[512,256]{1,0:T(8,128)(2,1)}, bf16[512,256]{1,0:T(8,128)(2,1)S(1)}, u32[]{:S(2)}, u32[]{:S(2)}) collective-permute-start(bf16[512,256]{1,0:T(8,128)(2,1)} %get-tuple-element.65), channel_id=1, source_target_pairs={{2,0},{5,1},{0,2},{3,3},{6,4},{1,5},{4,6},{7,7},{10,8},{13,9},{8,1... | collective-permute-start | bytes 786440 | tf_op jit(solution)/shard_map/ppermute | solution.py:579
  494.0 16.3 %collective-permute-start.30 = (bf16[128,2048]{1,0:T(8,128)(2,1)}, bf16[128,2048]{1,0:T(8,128)(2,1)}, u32[]{:S(2)}, u32[]{:S(2)}) collective-permute-start(bf16[128,2048]{1,0:T(8,128)(2,1)} %get-tuple-element.38), channel_id=1, source_target_pairs={{0,1},{1,0},{2,3},{3,2},{4,5},{5,4},{6,7},{7,6},{8,9},{9,8},{10,11... | collective-permute-start | bytes 1572872 | tf_op jit(solution)/shard_map/ppermute | solution.py:343
  497.1 24.3 %collective-permute-start.20 = (bf16[128,2048]{1,0:T(8,128)(2,1)}, bf16[128,2048]{1,0:T(8,128)(2,1)}, u32[]{:S(2)}, u32[]{:S(2)}) collective-permute-start(bf16[128,2048]{1,0:T(8,128)(2,1)} %get-tuple-element.40), channel_id=1, source_target_pairs={{0,1},{1,0},{2,3},{3,2},{4,5},{5,4},{6,7},{7,6},{8,9},{9,8},{10,11... | collective-permute-start | bytes 1572872 | tf_op jit(solution)/shard_map/ppermute | solution.py:343
  497.2 35.5 %collective-permute-start.14 = (bf16[128,2048]{1,0:T(8,128)(2,1)}, bf16[128,2048]{1,0:T(8,128)(2,1)}, u32[]{:S(2)}, u32[]{:S(2)}) collective-permute-start(bf16[128,2048]{1,0:T(8,128)(2,1)} %get-tuple-element.39), channel_id=1, source_target_pairs={{0,1},{1,0},{2,3},{3,2},{4,5},{5,4},{6,7},{7,6},{8,9},{9,8},{10,11... | collective-permute-start | bytes 1572872 | tf_op jit(solution)/shard_map/ppermute | solution.py:343
  502.3 52.6 %collective-permute-start.40 = (bf16[512,768]{1,0:T(8,128)(2,1)S(1)}, bf16[512,768]{1,0:T(8,128)(2,1)S(1)}, u32[]{:S(2)}, u32[]{:S(2)}) collective-permute-start(bf16[512,768]{1,0:T(8,128)(2,1)S(1)} %constant_dynamic-update-slice_fusion.26), channel_id=1, source_target_pairs={{0,8},{8,0},{1,9},{9,1},{2,10},{10,2},{3,11},{11,3},{4,12},{12,4},... | collective-permute-start | bytes 2359304 | tf_op jit(solution)/shard_map/ppermute | solution.py:343
  502.4 111.9 %collective-permute-start.44 = (bf16[8,320,256]{2,1,0:T(8,128)(2,1)S(1)}, bf16[8,320,256]{2,1,0:T(8,128)(2,1)S(1)}, u32[]{:S(2)}, u32[]{:S(2)}) collective-permute-start(bf16[8,320,256]{2,1,0:T(8,128)(2,1)S(1)} %all-to-all-done.1), channel_id=1, source_target_pairs={{0,8},{8,0},{1,9},{9,1},{2,10},{10,2},{3,11},{11,3},{4,12},{12,4},... | collective-permute-start | bytes 3932168 | tf_op jit(solution)/shard_map/ppermute | solution.py:343
  510.2 33.6 %collective-permute-start.18 = (bf16[128,2048]{1,0:T(8,128)(2,1)}, bf16[128,2048]{1,0:T(8,128)(2,1)S(1)}, u32[]{:S(2)}, u32[]{:S(2)}) collective-permute-start(bf16[128,2048]{1,0:T(8,128)(2,1)} %get-tuple-element.41), channel_id=1, source_target_pairs={{0,1},{1,0},{2,3},{3,2},{4,5},{5,4},{6,7},{7,6},{8,9},{9,8},{10,11... | collective-permute-start | bytes 1572872 | tf_op jit(solution)/shard_map/ppermute | solution.py:343
  521.5 30.8 %collective-permute-start.16 = (bf16[128,2048]{1,0:T(8,128)(2,1)}, bf16[128,2048]{1,0:T(8,128)(2,1)S(1)}, u32[]{:S(2)}, u32[]{:S(2)}) collective-permute-start(bf16[128,2048]{1,0:T(8,128)(2,1)} %get-tuple-element.42), channel_id=1, source_target_pairs={{0,1},{1,0},{2,3},{3,2},{4,5},{5,4},{6,7},{7,6},{8,9},{9,8},{10,11... | collective-permute-start | bytes 1572872 | tf_op jit(solution)/shard_map/ppermute | solution.py:343
  532.7 245.1 %collective-permute-start.48 = (f32[1024,1024]{1,0:T(8,128)}, f32[1024,1024]{1,0:T(8,128)}, u32[]{:S(2)}, u32[]{:S(2)}) collective-permute-start(f32[1024,1024]{1,0:T(8,128)} %get-tuple-element.34), channel_id=1, source_target_pairs={{0,8},{8,0},{1,9},{9,1},{2,10},{10,2},{3,11},{11,3},{4,12},{12,4},... | collective-permute-start | bytes 12582920 | tf_op jit(solution)/shard_map/ppermute | solution.py:343
  543.8 22.2 %collective-permute-start.33 = (bf16[128,2048]{1,0:T(8,128)(2,1)S(1)}, bf16[128,2048]{1,0:T(8,128)(2,1)S(1)}, u32[]{:S(2)}, u32[]{:S(2)}) collective-permute-start(bf16[128,2048]{1,0:T(8,128)(2,1)S(1)} %get-tuple-element.28), channel_id=1, source_target_pairs={{0,6},{2,0},{4,2},{6,4},{1,7},{3,1},{5,3},{7,5},{8,14},{10,8},{12,... | collective-permute-start | bytes 1572872 | tf_op jit(solution)/shard_map/ppermute | solution.py:343
  552.3 62.0 %collective-permute-start.31 = (bf16[128,2048]{1,0:T(8,128)(2,1)S(1)}, bf16[128,2048]{1,0:T(8,128)(2,1)S(1)}, u32[]{:S(2)}, u32[]{:S(2)}) collective-permute-start(bf16[128,2048]{1,0:T(8,128)(2,1)S(1)} %get-tuple-element.29), channel_id=1, source_target_pairs={{0,4},{2,6},{4,0},{6,2},{1,5},{3,7},{5,1},{7,3},{8,12},{10,14},{12... | collective-permute-start | bytes 1572872 | tf_op jit(solution)/shard_map/ppermute | solution.py:343
  554.9 59.3 %collective-permute-start.29 = (bf16[128,2048]{1,0:T(8,128)(2,1)S(1)}, bf16[128,2048]{1,0:T(8,128)(2,1)S(1)}, u32[]{:S(2)}, u32[]{:S(2)}) collective-permute-start(bf16[128,2048]{1,0:T(8,128)(2,1)S(1)} %get-tuple-element.27), channel_id=1, source_target_pairs={{0,2},{2,4},{4,6},{6,0},{1,3},{3,5},{5,7},{7,1},{8,10},{10,12},{12... | collective-permute-start | bytes 1572872 | tf_op jit(solution)/shard_map/ppermute | solution.py:343
  562.0 54.0 %copy-start.6 = (bf16[1,128,2048]{2,1,0:T(8,128)(2,1)S(1)}, bf16[1,128,2048]{2,1,0:T(8,128)(2,1)}, u32[]{:S(2)}) copy-start(bf16[1,128,2048]{2,1,0:T(8,128)(2,1)} %param.16) | copy-start | bytes 1572868
  562.0 54.0 %copy-start.50 = (f32[128]{0:T(128)S(1)}, f32[128]{0:T(128)}, u32[]{:S(2)}) copy-start(f32[128]{0:T(128)} %copy-done.49) | copy-start | bytes 1540
  562.0 54.0 %copy-start.55 = (f32[128]{0:T(128)S(1)}, f32[128]{0:T(128)}, u32[]{:S(2)}) copy-start(f32[128]{0:T(128)} %add_rsqrt_fusion.1) | copy-start | bytes 1540
  566.0 54.0 %collective-permute-start.19 = (bf16[128,2048]{1,0:T(8,128)(2,1)S(1)}, bf16[128,2048]{1,0:T(8,128)(2,1)S(1)}, u32[]{:S(2)}, u32[]{:S(2)}) collective-permute-start(bf16[128,2048]{1,0:T(8,128)(2,1)S(1)} %get-tuple-element.31), channel_id=1, source_target_pairs={{0,6},{2,0},{4,2},{6,4},{1,7},{3,1},{5,3},{7,5},{8,14},{10,8},{12,... | collective-permute-start | bytes 1572872 | tf_op jit(solution)/shard_map/ppermute | solution.py:343
  614.3 23.0 %collective-permute-start.17 = (bf16[128,2048]{1,0:T(8,128)(2,1)S(1)}, bf16[128,2048]{1,0:T(8,128)(2,1)S(1)}, u32[]{:S(2)}, u32[]{:S(2)}) collective-permute-start(bf16[128,2048]{1,0:T(8,128)(2,1)S(1)} %get-tuple-element.32), channel_id=1, source_target_pairs={{0,4},{2,6},{4,0},{6,2},{1,5},{3,7},{5,1},{7,3},{8,12},{10,14},{12... | collective-permute-start | bytes 1572872 | tf_op jit(solution)/shard_map/ppermute | solution.py:343
  614.3 22.9 %collective-permute-start.15 = (bf16[128,2048]{1,0:T(8,128)(2,1)S(1)}, bf16[128,2048]{1,0:T(8,128)(2,1)S(1)}, u32[]{:S(2)}, u32[]{:S(2)}) collective-permute-start(bf16[128,2048]{1,0:T(8,128)(2,1)S(1)} %get-tuple-element.30), channel_id=1, source_target_pairs={{0,2},{2,4},{4,6},{6,0},{1,3},{3,5},{5,7},{7,1},{8,10},{10,12},{12... | collective-permute-start | bytes 1572872 | tf_op jit(solution)/shard_map/ppermute | solution.py:343
  614.4 157.1 %collective-permute-start.41 = (bf16[2,512,768]{2,1,0:T(8,128)(2,1)}, bf16[2,512,768]{2,1,0:T(8,128)(2,1)}, u32[]{:S(2)}, u32[]{:S(2)}) collective-permute-start(bf16[2,512,768]{2,1,0:T(8,128)(2,1)} %maximum_select_fusion.12), channel_id=1, source_target_pairs={{0,16},{16,0},{1,17},{17,1},{2,18},{18,2},{3,19},{19,3},{4,20},{20... | collective-permute-start | bytes 4718600 | tf_op jit(solution)/shard_map/ppermute | solution.py:343
  620.0 167.0 %collective-permute-start.45 = (bf16[2,8,320,256]{3,2,1,0:T(8,128)(2,1)}, bf16[2,8,320,256]{3,2,1,0:T(8,128)(2,1)}, u32[]{:S(2)}, u32[]{:S(2)}) collective-permute-start(bf16[2,8,320,256]{3,2,1,0:T(8,128)(2,1)} %maximum_select_fusion.8), channel_id=1, source_target_pairs={{0,16},{16,0},{1,17},{17,1},{2,18},{18,2},{3,19},{19,3},{4,20},{20... | collective-permute-start | bytes 7864328 | tf_op jit(solution)/shard_map/ppermute | solution.py:343
  766.8 30.7 %copy-start.51 = (f32[1,256]{1,0:T(1,128)}, f32[1,256]{1,0:T(1,128)S(1)}, u32[]{:S(2)}) copy-start(f32[1,256]{1,0:T(1,128)S(1)} %get-tuple-element.75) | copy-start | bytes 3076
  (64 other events, 569.4 us)
Sparse Core Ops, SparseCore 0:
  641.6 123.7 all-reduce.1

commit v2 on v0

v2 whole, which is shorter than its diff:
```python
import math

import jax
import jax.numpy as jnp
from jax import lax
from jax.experimental import pallas as pl
from jax.experimental.pallas import tpu as pltpu
from jax.sharding import Mesh
from jax.sharding import PartitionSpec as P

HEADS = 8
HEAD = 256
ROT = 64


EPSILON = 1e-05
SQRT_HALF = 0.7071067811865476
INV_ROOT_TWO_PI = 0.3989422804014327
MASKED = -1e30

DP, CTX, FSDP, X, CORE = "dp", "ctx", "fsdp", "x", "core"
GROUP, REPLICAS = (CTX, FSDP), (X, CORE)
QK, KV, QT = "qhd,khd->hqk", "hqk,khd->qhd", "hqk,qhd->khd"


def from_behind(value, axis, steps):
    count = lax.axis_size(axis)
    pairs = [(source, (source + steps) % count) for source in range(count)]
    return lax.ppermute(value, axis, pairs)


def shifted(block, axis, distance):
    devices = range(lax.axis_size(axis))
    route = [(i - distance, i) for i in devices if i - distance in devices]
    return lax.ppermute(block, axis, route)


def normalize(inputs):
    centre = jnp.mean(inputs, axis=-1, keepdims=True)
    centred = inputs - centre
    variance = jnp.mean(centred * centred, axis=-1, keepdims=True)
    inv_std = lax.rsqrt(variance + EPSILON)
    return (centred * inv_std, inv_std)


def norm_backward(upstream, normed, inv_std):
    first_mean = jnp.mean(upstream, axis=-1, keepdims=True)
    second_mean = jnp.mean(upstream * normed, axis=-1, keepdims=True)
    return inv_std * (upstream - first_mean - normed * second_mean)


def gelu_parts(preact):
    normal_cdf = 0.5 * (1.0 + lax.erf(preact * SQRT_HALF))
    normal_pdf = jnp.exp(-0.5 * preact * preact) * INV_ROOT_TWO_PI
    return (preact * normal_cdf, normal_cdf + preact * normal_pdf)


def rotary_tables(positions, rot_dims):
    half_dims = rot_dims // 2
    frequency = jnp.exp(
        jnp.arange(half_dims).astype(jnp.float32) * (-2.0 * math.log(10000.0) / rot_dims)
    )
    angles = positions[:, None] * frequency[None, :]
    return (jnp.cos(angles)[:, None, :], jnp.sin(angles)[:, None, :])


def rotate(tensor, cosine, sine_table, rot_dims):
    half_dims = rot_dims // 2
    leading = tensor[..., :half_dims]
    trailing = tensor[..., half_dims:rot_dims]
    return jnp.concatenate(
        [
            leading * cosine - trailing * sine_table,
            trailing * cosine + leading * sine_table,
            tensor[..., rot_dims:],
        ],
        axis=-1,
    )


def contract_rows(left, right):
    return lax.dot_general(
        left, right, (((0,), (0,)), ((), ())), preferred_element_type=jnp.float32
    )


def contract_cols(left, right):
    return lax.dot_general(
        left, right, (((1,), (1,)), ((), ())), preferred_element_type=jnp.float32
    )


def plain_layer(
    hidden,
    cotangent,
    ln1_gain,
    ln1_bias,
    ln2_gain,
    ln2_bias,
    w_qkv,
    b_qkv,
    w_out,
    b_out,
    w_fc1,
    b_fc1,
    w_fc2,
    b_fc2,
):
    inputs = hidden[0]
    upstream_bf = cotangent[0]
    row_count = inputs.shape[0]
    score_scale = HEAD ** (-0.5)
    cycle_size = lax.axis_size(CTX)
    cycle_place = lax.axis_index(CTX)
    attn_gathered = (
        lax.all_gather(ln1_gain, GROUP, axis=0, tiled=True),
        lax.all_gather(ln1_bias, GROUP, axis=0, tiled=True),
        lax.all_gather(w_qkv, GROUP, axis=1, tiled=True),
        lax.all_gather(b_qkv, GROUP, axis=0, tiled=True),
        lax.all_gather(w_out, GROUP, axis=1, tiled=True),
        lax.all_gather(b_out, GROUP, axis=0, tiled=True),
    )
    mlp_gathered = (
        lax.all_gather(ln2_gain, GROUP, axis=0, tiled=True),
        lax.all_gather(ln2_bias, GROUP, axis=0, tiled=True),
        lax.all_gather(w_fc1, GROUP, axis=1, tiled=True),
        lax.all_gather(b_fc1, GROUP, axis=0, tiled=True),
        lax.all_gather(w_fc2, GROUP, axis=1, tiled=True),
        lax.all_gather(b_fc2, GROUP, axis=0, tiled=True),
    )
    gain_one, shift_one, full_qkv, full_bqkv, full_out, full_bout = attn_gathered
    gain_two, shift_two, full_fc1, full_bfc1, full_fc2, full_bfc2 = mlp_gathered
    inputs_f = inputs.astype(jnp.float32)
    normed, inv_std = normalize(inputs_f)
    attn_in = (normed * gain_one.astype(jnp.float32) + shift_one.astype(jnp.float32)).astype(
        jnp.bfloat16
    )
    mlp_in = (normed * gain_two.astype(jnp.float32) + shift_two.astype(jnp.float32)).astype(
        jnp.bfloat16
    )
    joined = jnp.dot(attn_in, full_qkv, preferred_element_type=jnp.float32) + full_bqkv.astype(
        jnp.float32
    )
    joined = joined.reshape(row_count, 3, HEADS, HEAD)
    token_pos = cycle_place * row_count + jnp.arange(row_count, dtype=jnp.int32)
    cosine, sine_table = rotary_tables(token_pos.astype(jnp.float32), ROT)
    queries = rotate(joined[:, 0], cosine, sine_table, ROT).astype(jnp.bfloat16)
    keys_own = rotate(joined[:, 1], cosine, sine_table, ROT).astype(jnp.bfloat16)
    values_own = joined[:, 2].astype(jnp.bfloat16)
    row_top = jnp.full((HEADS, row_count), MASKED, jnp.float32)
    absorb_key_block = lax.all_gather(keys_own, CTX, axis=0, tiled=True)
    absorb_value_block = lax.all_gather(values_own, CTX, axis=0, tiled=True)
    absorb_key_pos = jnp.arange(absorb_key_block.shape[0], dtype=jnp.int32)
    absorb_visible = (token_pos[:, None] >= absorb_key_pos[None, :])[None]
    absorb_scores = (
        jnp.einsum(QK, queries, absorb_key_block, preferred_element_type=jnp.float32)
        * score_scale
    )
    absorb_scores = jnp.where(absorb_visible, absorb_scores, MASKED)
    new_top = jnp.maximum(row_top, jnp.max(absorb_scores, axis=-1))
    weights_exp = jnp.where(absorb_visible, jnp.exp(absorb_scores - new_top[:, :, None]), 0.0)
    row_total = jnp.sum(weights_exp, axis=-1)
    mixed = jnp.einsum(
        KV,
        weights_exp.astype(jnp.bfloat16),
        absorb_value_block,
        preferred_element_type=jnp.float32,
    )
    row_top, row_total, mixed = (new_top, row_total, mixed)
    attended = (mixed / jnp.transpose(row_total)[:, :, None]).astype(jnp.bfloat16)
    log_total = row_top + jnp.log(row_total)
    attended_flat = attended.reshape(row_count, HEADS * HEAD)
    branch_attn = jnp.dot(
        attended_flat, full_out, preferred_element_type=jnp.float32
    ) + full_bout.astype(jnp.float32)
    preact = jnp.dot(mlp_in, full_fc1, preferred_element_type=jnp.float32) + full_bfc1.astype(
        jnp.float32
    )
    activated, slope = gelu_parts(preact)
    act_bf = activated.astype(jnp.bfloat16)
    branch_mlp = jnp.dot(act_bf, full_fc2, preferred_element_type=jnp.float32) + full_bfc2.astype(
        jnp.float32
    )
    output = (inputs_f + branch_attn + branch_mlp).astype(jnp.bfloat16)
    rows_all = (
        lax.all_gather(inputs, GROUP, axis=0, tiled=True),
        lax.all_gather(act_bf, GROUP, axis=0, tiled=True),
        lax.all_gather(attended_flat, GROUP, axis=0, tiled=True),
    )
    attn_gathered = (
        lax.all_gather(ln1_gain, GROUP, axis=0, tiled=True),
        lax.all_gather(ln1_bias, GROUP, axis=0, tiled=True),
        lax.all_gather(w_qkv, GROUP, axis=1, tiled=True),
        lax.all_gather(b_qkv, GROUP, axis=0, tiled=True),
        lax.all_gather(w_out, GROUP, axis=1, tiled=True),
        lax.all_gather(b_out, GROUP, axis=0, tiled=True),
    )
    mlp_gathered = (
        lax.all_gather(ln2_gain, GROUP, axis=0, tiled=True),
        lax.all_gather(ln2_bias, GROUP, axis=0, tiled=True),
        lax.all_gather(w_fc1, GROUP, axis=1, tiled=True),
        lax.all_gather(b_fc1, GROUP, axis=0, tiled=True),
        lax.all_gather(w_fc2, GROUP, axis=1, tiled=True),
        lax.all_gather(b_fc2, GROUP, axis=0, tiled=True),
    )
    gain_one, shift_one, full_qkv, full_bqkv, full_out, full_bout = attn_gathered
    gain_two, shift_two, full_fc1, full_bfc1, full_fc2, full_bfc2 = mlp_gathered
    upstream = upstream_bf.astype(jnp.float32)
    bias_out_grad = jnp.sum(upstream, axis=0)
    d_act = contract_cols(upstream_bf, full_fc2)
    d_preact = d_act * slope
    d_preact_bf = d_preact.astype(jnp.bfloat16)
    d_mlp_in = contract_cols(d_preact_bf, full_fc1)
    fc1_bias_grad = jnp.sum(d_preact, axis=0)
    ln2_gain_part = jnp.sum(d_mlp_in * normed, axis=0)
    ln2_bias_part = jnp.sum(d_mlp_in, axis=0)
    d_attended = (
        contract_cols(upstream_bf, full_out).astype(jnp.bfloat16).reshape(row_count, HEADS, HEAD)
    )
    row_dot = jnp.transpose(
        jnp.sum(d_attended.astype(jnp.float32) * attended.astype(jnp.float32), axis=-1)
    )
    d_queries = jnp.zeros((row_count, HEADS, HEAD), jnp.float32)
    travelling = (keys_own, values_own)
    key_grads = (
        jnp.zeros((row_count, HEADS, HEAD), jnp.float32),
        jnp.zeros((row_count, HEADS, HEAD), jnp.float32),
    )
    for turn_index in range(cycle_size):
        source = (cycle_place - turn_index) % cycle_size
        key_pos = source * row_count + jnp.arange(row_count, dtype=jnp.int32)
        key_block, value_block = travelling
        visible = (token_pos[:, None] >= key_pos[None, :])[None]
        scores = (
            jnp.einsum(QK, queries, key_block, preferred_element_type=jnp.float32)
            * score_scale
        )
        scores = jnp.where(visible, scores, MASKED)
        probability = jnp.where(visible, jnp.exp(scores - log_total[:, :, None]), 0.0)
        d_probability = jnp.einsum(
            QK, d_attended, value_block, preferred_element_type=jnp.float32
        )
        d_scores = (probability * (d_probability - row_dot[:, :, None]) * score_scale).astype(
            jnp.bfloat16
        )
        d_queries = d_queries + jnp.einsum(
            KV, d_scores, key_block, preferred_element_type=jnp.float32
        )
        key_grads = (
            key_grads[0]
            + jnp.einsum(QT, d_scores, queries, preferred_element_type=jnp.float32),
            key_grads[1]
            + jnp.einsum(
                QT,
                probability.astype(jnp.bfloat16),
                d_attended,
                preferred_element_type=jnp.float32,
            ),
        )
        key_grads = from_behind((key_grads[0], key_grads[1]), CTX, 1)
        if turn_index + 1 < cycle_size:
            travelling = shifted((travelling[0], travelling[1]), CTX, 1)
    d_queries = rotate(d_queries, cosine, -sine_table, ROT)
    d_keys = rotate(key_grads[0], cosine, -sine_table, ROT)
    d_joined = jnp.stack([d_queries, d_keys, key_grads[1]], axis=1).reshape(
        row_count, 3 * HEADS * HEAD
    )
    d_joined_bf = d_joined.astype(jnp.bfloat16)
    d_attn_in = contract_cols(d_joined_bf, full_qkv)
    qkv_bias_grad = jnp.sum(d_joined, axis=0)
    ln1_gain_part = jnp.sum(d_attn_in * normed, axis=0)
    ln1_bias_part = jnp.sum(d_attn_in, axis=0)
    columns = (
        lax.all_to_all(upstream_bf, GROUP, split_axis=1, concat_axis=0, tiled=True),
        lax.all_to_all(d_preact_bf, GROUP, split_axis=1, concat_axis=0, tiled=True),
        lax.all_to_all(d_joined_bf, GROUP, split_axis=1, concat_axis=0, tiled=True),
    )
    small = (
        lax.psum_scatter(ln1_gain_part, GROUP, scatter_dimension=0, tiled=True),
        lax.psum_scatter(ln1_bias_part, GROUP, scatter_dimension=0, tiled=True),
        lax.psum_scatter(ln2_gain_part, GROUP, scatter_dimension=0, tiled=True),
        lax.psum_scatter(ln2_bias_part, GROUP, scatter_dimension=0, tiled=True),
        lax.psum_scatter(qkv_bias_grad, GROUP, scatter_dimension=0, tiled=True),
        lax.psum_scatter(bias_out_grad, GROUP, scatter_dimension=0, tiled=True),
        lax.psum_scatter(fc1_bias_grad, GROUP, scatter_dimension=0, tiled=True),
    )
    normed_all, _ = normalize(rows_all[0].astype(jnp.float32))
    attn_all = (normed_all * gain_one.astype(jnp.float32) + shift_one.astype(jnp.float32)).astype(
        jnp.bfloat16
    )
    mlp_all = (normed_all * gain_two.astype(jnp.float32) + shift_two.astype(jnp.float32)).astype(
        jnp.bfloat16
    )
    fc2_part = contract_rows(rows_all[1], columns[0])
    out_part = contract_rows(rows_all[2], columns[0])
    fc1_part = contract_rows(mlp_all, columns[1])
    qkv_part = contract_rows(attn_all, columns[2])
    owned = (
        small[0],
        small[1],
        small[2],
        small[3],
        qkv_part,
        small[4],
        out_part,
        small[5],
        fc1_part,
        small[6],
        fc2_part,
    )
    merged = d_attn_in * gain_one.astype(jnp.float32) + d_mlp_in * gain_two.astype(jnp.float32)
    input_grad = (upstream + norm_backward(merged, normed, inv_std)).astype(jnp.bfloat16)
    totals = lax.psum(
        (
            owned[0],
            owned[1],
            owned[2],
            owned[3],
            owned[4],
            owned[5],
            owned[6],
            owned[7],
            owned[8],
            owned[9],
            owned[10],
        ),
        DP,
    )
    return (
        output[None],
        input_grad[None],
        totals[0],
        totals[1],
        totals[2],
        totals[3],
        totals[4],
        totals[5],
        totals[6],
        totals[7],
        totals[8],
        totals[9],
        totals[10],
        totals[7],
    )


def rotated(value, axis, steps):
    count = lax.axis_size(axis)
    return lax.ppermute(value, axis, [(i, (i + steps) % count) for i in range(count)])


def gather_line(block):
    place = lax.axis_index(CTX)
    low = rotated(block, CTX, 1)
    high = rotated(block, CTX, 3)
    up = lax.ppermute(low, CTX, [(1, 2), (2, 3)])
    down = lax.ppermute(high, CTX, [(2, 1), (1, 0)])
    middle = jnp.where(place >= 2, up, down)
    return [block, low, middle, high]


def gather_side(blocks):
    gathered = []
    for block in blocks:
        gathered.append(rotated(block, FSDP, 1))
    return gathered


NT = (((1,), (1,)), ((), ()))
TN = (((0,), (0,)), ((), ()))
NN = (((1,), (0,)), ((), ()))
ROPE_LANES = 128
VMEM_LIMIT = 16 << 20


def mm(left, right, dims=NN):
    return lax.dot_general(left, right, dims, preferred_element_type=jnp.float32)


def whole(shape):
    return pl.BlockSpec(shape, lambda *_: (0,) * len(shape), pipeline_mode=pl.Buffered(1))


def call(kernel, grid, in_specs, out_specs, outs, scratch=(), scalars=(), args=()):
    return pl.pallas_call(
        kernel,
        grid_spec=pltpu.PrefetchScalarGridSpec(
            num_scalar_prefetch=len(scalars),
            grid=grid,
            in_specs=in_specs,
            out_specs=out_specs,
            scratch_shapes=list(scratch),
        ),
        out_shape=[jax.ShapeDtypeStruct(shape, dtype) for shape, dtype in outs],
        compiler_params=pltpu.CompilerParams(vmem_limit_bytes=VMEM_LIMIT),
    )(*scalars, *args)


def pack_columns(pieces):
    rows = pieces[0].shape[0]
    total = sum(p.shape[1] for p in pieces)

    def kernel(*refs):
        begin = 0
        for ref in refs[:-1]:
            end = begin + ref.shape[1]
            refs[-1][:, begin:end] = ref[...]
            begin = end

    return call(
        kernel,
        (1,),
        [whole(p.shape) for p in pieces],
        [whole((rows, total))],
        [((rows, total), pieces[0].dtype)],
        args=pieces,
    )[0]


def norm_fc1(pieces, params, w_fc1, b_fc1):
    f32, bf16 = jnp.float32, jnp.bfloat16
    count, (piece, width) = len(pieces), pieces[0].shape
    rows, units = count * piece, w_fc1.shape[1]
    chunk, step, tall = 256, 64, 256

    def kernel(*refs):
        piece_refs, (par, w, b, attn, mlp, centre, scale, act, slope) = refs[:count], refs[count:]

        @pl.when(pl.program_id(0) == 0)
        def _():
            for i in range(count):

                def norm(k, _, i=i):
                    x = piece_refs[i][pl.ds(pl.multiple_of(k * step, step), step), :].astype(f32)
                    mean = jnp.mean(x, axis=-1, keepdims=True)
                    x = x - mean
                    inv = lax.rsqrt(jnp.mean(x * x, axis=-1, keepdims=True) + EPSILON)
                    x = x * inv
                    here = pl.ds(pl.multiple_of(i * piece + k * step, step), step)
                    attn[here, :] = (x * par[0:1] + par[1:2]).astype(bf16)
                    mlp[here, :] = (x * par[2:3] + par[3:4]).astype(bf16)
                    centre[here, :] = mean
                    scale[here, :] = inv
                    return 0

                lax.fori_loop(0, piece // step, norm, 0)

        for r in range(rows // tall):
            here = slice(r * tall, (r + 1) * tall)
            activated, gradient = gelu_parts(mm(mlp[here, :], w[...]) + b[...])
            act[here, :] = activated.astype(bf16)
            slope[here, :] = gradient

    column = pl.BlockSpec((rows, chunk), lambda j: (0, j))
    return call(
        kernel,
        (units // chunk,),
        [whole((piece, width))] * count
        + [
            whole(params.shape),
            pl.BlockSpec((width, chunk), lambda j: (0, j)),
            pl.BlockSpec((1, chunk), lambda j: (0, j)),
        ],
        [whole((rows, width))] * 2 + [whole((rows, 1))] * 2 + [column] * 2,
        [((rows, width), bf16)] * 2
        + [((rows, 1), f32)] * 2
        + [((rows, units), bf16), ((rows, units), f32)],
        args=(*pieces, params, w_fc1, b_fc1),
    )


def turn(tensor, cosine, sine):
    first = tensor[:, :ROPE_LANES]
    lane = lax.broadcasted_iota(jnp.int32, first.shape, 1)
    swapped = jnp.where(
        lane < ROT // 2,
        pltpu.roll(first, ROPE_LANES - ROT // 2, 1),
        pltpu.roll(first, ROT // 2, 1),
    )
    return jnp.concatenate([first * cosine + swapped * sine, tensor[:, ROPE_LANES:]], axis=1)


def head_attention(attn_in, weights, bias, tables, positions, meta):
    f32, bf16 = jnp.float32, jnp.bfloat16
    length, width = attn_in.shape
    chunk, slots = length // 4, 3
    joins = len(weights) > 1

    def kernel(meta, x, *refs):
        pieces, (b, cosine, sine, down, along) = refs[: len(weights)], refs[len(weights) :][:5]
        qkv, att, log_total = refs[-3:]
        w = refs[-4] if joins else pieces[0]
        if joins:
            deep = pieces[0].shape[0]
            for d, p in enumerate(pieces):
                here = pl.ds(pl.multiple_of((meta[0] ^ d) * deep, deep), deep)
                for s in range(slots):
                    w[meta[1 + s], here, :] = p[:, s * HEAD : (s + 1) * HEAD]
        for kind in range(3):
            t = mm(x[...], w[kind]) + b[kind]
            if kind < 2:
                t = turn(t, cosine[...], sine[...])
            qkv[kind] = t.astype(bf16)
        for c in range(4):
            here = slice(c * chunk, (c + 1) * chunk)
            seen = down[here, :] >= along[...]
            scores = jnp.where(seen, mm(qkv[0, here, :], qkv[1], NT) * HEAD**-0.5, MASKED)
            top = jnp.max(scores, axis=-1, keepdims=True)
            powers = jnp.where(seen, jnp.exp(scores - top), 0.0)
            total = jnp.sum(powers, axis=-1, keepdims=True)
            att[here, :] = (mm(powers.astype(bf16), qkv[2]) / total).astype(bf16)
            log_total[here, :] = top + jnp.log(total)

    args = (attn_in, *weights, bias, *tables, *positions)
    outs = [((3, length, HEAD), bf16), ((length, HEAD), bf16), ((length, 1), f32)]
    if joins:
        outs = [((3, width, HEAD), bf16)] + outs
    return call(
        kernel,
        (1,),
        [whole(v.shape) for v in args],
        [whole(shape) for shape, _ in outs],
        outs,
        scalars=(meta,),
        args=args,
    )


def project_other(pieces, act, att, meta):
    bf16 = jnp.bfloat16
    members, _, cols = pieces[0].shape
    length, units = act.shape
    width = members * cols
    tall, low = units // 4, HEAD // 4

    def kernel(meta, p0, p1, p2, p3, act, att, w, out):
        for d, p in enumerate((p0, p1, p2, p3)):
            q = meta[0] ^ d
            upper = pl.ds(pl.multiple_of(q * tall, tall), tall)
            lower = pl.ds(pl.multiple_of(units + q * low, low), low)
            for m in range(members):
                w[upper, m * cols : (m + 1) * cols] = p[m, :tall, :]
                w[lower, m * cols : (m + 1) * cols] = p[m, tall:, :]
        for m in range(members):
            here = slice(m * cols, (m + 1) * cols)
            part = mm(act[...], w[:units, here]) + mm(att[...], w[units:, here])
            out[:, here] = part.astype(bf16)

    args = (*pieces, act, att)
    return call(
        kernel,
        (1,),
        [whole(v.shape) for v in args],
        [whole((units + HEAD, width)), whole((length, width))],
        [((units + HEAD, width), bf16), ((length, width), bf16)],
        scalars=(meta,),
        args=args,
    )


def project_own(w, act, att):
    length, units = act.shape
    width, chunk = w.shape[1], 512

    def kernel(w, act, att, out, both):
        @pl.when(pl.program_id(0) == 0)
        def _():
            both[:, :units] = act[...]
            both[:, units:] = att[...]

        out[...] = mm(both[...], w[...]).astype(out.dtype)

    return call(
        kernel,
        (width // chunk,),
        [pl.BlockSpec((units + HEAD, chunk), lambda j: (0, j)), whole(act.shape), whole(att.shape)],
        [pl.BlockSpec((length, chunk), lambda j: (0, j))],
        [((length, width), jnp.bfloat16)],
        [pltpu.VMEM((length, units + HEAD), jnp.bfloat16)],
        args=(w, act, att),
    )[0]


def backward(cot, w, slope, att, qkv, log_total, tables, positions):
    f32, bf16 = jnp.float32, jnp.bfloat16
    length, units = slope.shape
    width, chunk, wide = cot.shape[1], length // 4, 256

    def kernel(*refs):
        (cot, w, slope, att, qkv, log_total, cosine, sine, down, along) = refs[:10]
        (dpre, dqkv, sum_fc1, sum_qkv, sum_cot, datt, dk, dv) = refs[10:]
        total = jnp.zeros((1, width), f32)
        for c in range(4):
            block = cot[c * chunk : (c + 1) * chunk, :].astype(f32)
            total = total + jnp.sum(block, axis=0, keepdims=True)
        sum_cot[...] = total
        datt[...] = mm(cot[...], w[units:, :], NT).astype(bf16)
        for n in range(units // wide):
            here = slice(n * wide, (n + 1) * wide)
            grad = mm(cot[...], w[here, :], NT) * slope[:, here]
            sum_fc1[:, here] = jnp.sum(grad, axis=0, keepdims=True)
            dpre[:, here] = grad.astype(bf16)
        dk[...] = jnp.zeros_like(dk)
        dv[...] = jnp.zeros_like(dv)
        sum_qkv[...] = jnp.zeros_like(sum_qkv)
        for c in range(4):
            here = slice(c * chunk, (c + 1) * chunk)
            queries, grad = qkv[0, here, :], datt[here, :]
            seen = down[here, :] >= along[...]
            scores = mm(queries, qkv[1], NT) * HEAD**-0.5
            prob = jnp.where(seen, jnp.exp(jnp.where(seen, scores, MASKED) - log_total[here, :]), 0.0)
            dot = jnp.sum(grad.astype(f32) * att[here, :].astype(f32), axis=-1, keepdims=True)
            dscore = (prob * (mm(grad, qkv[2], NT) - dot) * HEAD**-0.5).astype(bf16)
            dq = turn(mm(dscore, qkv[1]), cosine[here, :], -sine[here, :])
            sum_qkv[0:1, :] += jnp.sum(dq, axis=0, keepdims=True)
            dqkv[0, here, :] = dq.astype(bf16)
            dk[...] += mm(dscore, queries, TN)
            dv[...] += mm(prob.astype(bf16), grad, TN)
        turned = turn(dk[...], cosine[...], -sine[...])
        sum_qkv[1:2, :] = jnp.sum(turned, axis=0, keepdims=True)
        sum_qkv[2:3, :] = jnp.sum(dv[...], axis=0, keepdims=True)
        dqkv[1] = turned.astype(bf16)
        dqkv[2] = dv[...].astype(bf16)

    args = (cot, w, slope, att, qkv, log_total, *tables, *positions)
    outs = [
        ((length, units), bf16),
        ((3, length, HEAD), bf16),
        ((1, units), f32),
        ((8, HEAD), f32),
        ((1, width), f32),
    ]
    return call(
        kernel,
        (1,),
        [whole(v.shape) for v in args],
        [whole(shape) for shape, _ in outs],
        outs,
        [
            pltpu.VMEM((length, HEAD), bf16),
            pltpu.VMEM((length, HEAD), f32),
            pltpu.VMEM((length, HEAD), f32),
        ],
        args=args,
    )


def input_side(pieces, dpre, dqkv, w_fc1, w_qkv, centre, scale, params):
    f32 = jnp.float32
    count, (piece, width) = len(pieces), pieces[0].shape
    length, units, chunk = count * piece, dpre.shape[1], 512

    def kernel(*refs):
        x = refs[:count]
        dpre, dqkv, w_fc1, w_qkv, centre, scale, par, sums, out, dmlp, dattn = refs[count:]
        dmlp[...] = mm(dpre[...], w_fc1[...], NT)
        dattn[...] = (
            mm(dqkv[0], w_qkv[0], NT) + mm(dqkv[1], w_qkv[1], NT) + mm(dqkv[2], w_qkv[2], NT)
        )
        totals = [jnp.zeros((1, chunk), f32)] * 4
        for r in range(count):
            here = slice(r * piece, (r + 1) * piece)
            normed = (x[r][...].astype(f32) - centre[here, :]) * scale[here, :]
            a, m = dattn[here, :], dmlp[here, :]
            terms = (a * normed, a, m * normed, m)
            totals = [t + jnp.sum(v, axis=0, keepdims=True) for t, v in zip(totals, terms)]
            out[here, :] = (a * par[0:1] + m * par[2:3]).astype(out.dtype)
        for i, total in enumerate(totals):
            sums[i : i + 1, :] = total

    block = pl.BlockSpec((piece, chunk), lambda j: (0, j))
    return call(
        kernel,
        (width // chunk,),
        [block] * count
        + [
            whole(dpre.shape),
            whole(dqkv.shape),
            pl.BlockSpec((chunk, units), lambda j: (j, 0)),
            pl.BlockSpec((3, chunk, HEAD), lambda j: (0, j, 0)),
            whole(centre.shape),
            whole(scale.shape),
            pl.BlockSpec((4, chunk), lambda j: (0, j)),
        ],
        [pl.BlockSpec((rows, chunk), lambda j: (0, j)) for rows in (8, length)],
        [((8, width), f32), ((length, width), jnp.bfloat16)],
        [pltpu.VMEM((length, chunk), f32)] * 2,
        args=(*pieces, dpre, dqkv, w_fc1, w_qkv, centre, scale, params),
    )


def fc1_gradient(mlp_in, dpre, which, arrived=None):
    rows, width = mlp_in[0].shape
    units, chunk = dpre[0].shape[1], 256
    steps = width // 2 // chunk

    def kernel(which, x0, x1, d0, d1, *rest):
        part = mm(x0[...], d0[...], TN) + mm(x1[...], d1[...], TN)
        if arrived is not None:
            part = part + rest[0][...].astype(jnp.float32)
        rest[-1][...] = part.astype(jnp.bfloat16)

    out = pl.BlockSpec((chunk, units), lambda j, _: (j, 0))
    columns = pl.BlockSpec((rows, chunk), lambda j, which: (0, which[0] * steps + j))
    extra = () if arrived is None else (arrived,)
    return call(
        kernel,
        (steps,),
        [columns] * 2 + [whole(dpre[0].shape)] * 2 + [out] * len(extra),
        [out],
        [((width // 2, units), jnp.bfloat16)],
        scalars=(which,),
        args=(*mlp_in, *dpre, *extra),
    )[0]


def send_places_of(spot):
    return [1 - spot[1], 3 - spot[1]]


def keep_places_of(spot):
    return [2 * (1 - spot[0]) + spot[1], 2 * spot[0] + spot[1]]


def rows_gradient(act, att, cot, spot, came=None):
    f32, bf16 = jnp.float32, jnp.bfloat16
    rows, units = act[0].shape
    width, tall, low, chunk = cot[0].shape[1], units // 4, HEAD // 4, 512
    half = len(cot) // 2
    piece = cot[0].shape[0]
    places = send_places_of if came is None else keep_places_of

    def columns(deep):
        return pl.BlockSpec((deep, chunk), lambda j, _: (0, j))

    def stacked(deep):
        return pl.BlockSpec((2, deep, chunk), lambda j, _: (0, 0, j))

    lefts = [
        pl.BlockSpec((rows, tall), lambda j, spot, i=i: (0, places(spot)[i]))
        for i in range(2)
        for _ in range(2)
    ]

    def sending(spot, x0, x1, y0, y1, a0, a1, *refs):
        out, kept, c0, c1, left, head = refs[2 * half :]

        @pl.when(pl.program_id(0) == 0)
        def _():
            for i, pair in enumerate(((x0, x1), (y0, y1), (a0, a1))):
                here = slice(i * tall, (i + 1) * tall)
                left[here, :rows] = pair[0][...].T
                left[here, rows:] = pair[1][...].T

        for i in range(half):
            here = slice(i * piece, (i + 1) * piece)
            c0[here, :] = refs[i][...]
            c1[here, :] = refs[half + i][...]
        for i in range(2):
            part = mm(left[i * tall : (i + 1) * tall, :rows], c0[...])
            part = part + mm(left[i * tall : (i + 1) * tall, rows:], c1[...])
            out[i, :tall, :] = part.astype(bf16)
        head[...] = mm(left[2 * tall :, :rows], c0[...]) + mm(left[2 * tall :, rows:], c1[...])
        for i in range(2):
            q = 2 * i + spot[1]
            out[i, tall:, :] = head[pl.ds(pl.multiple_of((q ^ 1) * low, low), low), :].astype(bf16)
            kept[i] = head[pl.ds(pl.multiple_of(q * low, low), low), :]

    def keeping(spot, x0, x1, y0, y1, c0, c1, came, kept, sent, own, left):
        @pl.when(pl.program_id(0) == 0)
        def _():
            for i, pair in enumerate(((x0, x1), (y0, y1))):
                here = slice(i * tall, (i + 1) * tall)
                left[here, :rows] = pair[0][...].T
                left[here, rows:] = pair[1][...].T

        for i, out in enumerate((sent, own)):
            x = spot[0] ^ (1 - i)
            here = slice(i * tall, (i + 1) * tall)
            part = mm(left[here, :rows], c0[...]) + mm(left[here, rows:], c1[...])
            out[:tall, :] = (part + came[x, :tall, :].astype(f32)).astype(out.dtype)
            out[tall:, :] = (kept[x] + came[x, tall:, :].astype(f32)).astype(out.dtype)

    grid = (width // chunk,)
    if came is None:
        return call(
            sending,
            grid,
            lefts + [whole(v.shape) for v in att] + [columns(piece)] * len(cot),
            [stacked(tall + low), stacked(low), columns(rows), columns(rows)],
            [((2, tall + low, width), bf16), ((2, low, width), f32)] + [((rows, width), bf16)] * 2,
            [pltpu.VMEM((2 * tall + HEAD, 2 * rows), bf16), pltpu.VMEM((HEAD, chunk), f32)],
            scalars=(spot,),
            args=(*act, *act, *att, *cot),
        )
    return call(
        keeping,
        grid,
        lefts + [columns(rows)] * 2 + [stacked(tall + low), stacked(low)],
        [columns(tall + low)] * 2,
        [((tall + low, width), bf16), ((tall + low, width), f32)],
        [pltpu.VMEM((2 * tall, 2 * rows), bf16)],
        scalars=(spot,),
        args=(*act, *act, *cot, *came),
    )


def columns_gradient(attn_in, dqkv, meta, spot, came=None):
    f32, bf16 = jnp.float32, jnp.bfloat16
    rows, width = attn_in[0].shape
    deep, slots = width // 4, meta.shape[0] - 1
    places = send_places_of if came is None else keep_places_of

    lefts = [
        pl.BlockSpec((rows, deep), lambda s, _, spot, i=i: (0, places(spot)[i]))
        for i in range(2)
        for _ in range(2)
    ]
    kind = pl.BlockSpec((1, rows, HEAD), lambda s, meta, _: (meta[1 + s], 0, 0))
    stacked = pl.BlockSpec((2, deep, HEAD), lambda s, *_: (0, 0, s))
    columns = pl.BlockSpec((deep, HEAD), lambda s, *_: (0, s))

    def kernel(meta, spot, x0, x1, y0, y1, d0, d1, *rest):
        left = rest[-1]

        @pl.when(pl.program_id(0) == 0)
        def _():
            for i, pair in enumerate(((x0, x1), (y0, y1))):
                here = slice(i * deep, (i + 1) * deep)
                left[here, :rows] = pair[0][...].T
                left[here, rows:] = pair[1][...].T

        for i in range(2):
            here = slice(i * deep, (i + 1) * deep)
            part = mm(left[here, :rows], d0[0]) + mm(left[here, rows:], d1[0])
            if came is None:
                rest[0][i] = part.astype(bf16)
            else:
                part = part + rest[0][spot[0] ^ (1 - i)].astype(f32)
                rest[1 + i][...] = part.astype(rest[1 + i].dtype)

    if came is None:
        specs, outs, extra = [stacked], [((2, deep, slots * HEAD), bf16)], ()
    else:
        specs, extra = [columns] * 2, (came,)
        outs = [((deep, slots * HEAD), bf16), ((deep, slots * HEAD), f32)]
    return call(
        kernel,
        (slots,),
        lefts + [kind] * 2 + [stacked] * len(extra),
        specs,
        outs,
        [pltpu.VMEM((2 * deep, 2 * rows), bf16)],
        scalars=(meta, spot),
        args=(*attn_in, *attn_in, *dqkv, *extra),
    )


def pack_sums(norm_sums, head_sums, cot_sums, unit_sums, spot):
    f32 = jnp.float32
    width, units = cot_sums[0].shape[1], unit_sums[0].shape[1]
    members = HEADS
    cols = width // members
    begin = 4 * cols + 3 * HEAD
    total = begin + cols + units

    def kernel(spot, n0, n1, h0, h1, c0, c1, u0, u1, mine, sent, rows):
        rows[...] = jnp.zeros_like(rows)
        place = spot[2]
        own = pl.ds(place, 1)
        for m in range(members):
            for i in range(4):
                there = slice(m * cols, (m + 1) * cols)
                rows[m : m + 1, i * cols : (i + 1) * cols] = (
                    n0[i : i + 1, there] + n1[i : i + 1, there]
                )
        for kind in range(3):
            block = kind * HEADS + place
            lanes = pl.ds(pl.multiple_of(4 * cols + block % 3 * HEAD, HEAD), HEAD)
            rows[pl.ds(block // 3, 1), lanes] = h0[kind : kind + 1, :] + h1[kind : kind + 1, :]
        lanes = pl.ds(pl.multiple_of(place * cols, cols), cols)
        rows[own, begin : begin + cols] = c0[:, lanes] + c1[:, lanes]
        rows[own, begin + cols :] = u0[...] + u1[...]
        for z in range(members // 2):
            mine[z : z + 1, :] = rows[pl.ds(2 * z + spot[3], 1), :]
            sent[z : z + 1, :] = rows[pl.ds(2 * z + 1 - spot[3], 1), :]

    args = (*norm_sums, *head_sums, *cot_sums, *unit_sums)
    return call(
        kernel,
        (1,),
        [whole(v.shape) for v in args],
        [whole((members // 2, total))] * 2,
        [((members // 2, total), f32)] * 2,
        [pltpu.VMEM((members, total), f32)],
        scalars=(spot,),
        args=args,
    )


def fold_blocks(partial, arrived, blocks, passing=()):
    f32, bf16 = jnp.float32, jnp.bfloat16
    rows, width = partial.shape
    deep = rows // 4

    def kernel(a, b, *refs):
        more, outs = refs[: len(passing)], refs[len(passing) :]
        for i, (r, out) in enumerate(zip(blocks, outs)):
            here = slice(r * deep, (r + 1) * deep)
            block = a[here, :].astype(f32) + b[here, :].astype(f32)
            if more:
                block = block + more[i][...].astype(f32)
            out[...] = block.astype(out.dtype)

    return call(
        kernel,
        (1,),
        [whole(v.shape) for v in (partial, arrived, *passing)],
        [whole((deep, width))] * len(blocks),
        [((deep, width), bf16 if r else f32) for r in blocks],
        args=(partial, arrived, *passing),
    )


def member_at(spot, k, sign=1):
    return (spot[4] + sign * (k // 2) + HEADS) % (HEADS // 2) * 2 + (spot[3] ^ (k % 2))


def fold_rows(kept, arrived, spot):
    deep, width = kept.shape
    cols = width // HEADS

    def kernel(spot, a, b, *outs):
        for k, out in enumerate(outs):
            here = pl.ds(pl.multiple_of(member_at(spot, k) * cols, cols), cols)
            out[...] = (a[:, here] + b[:, here].astype(jnp.float32)).astype(jnp.bfloat16)

    return call(
        kernel,
        (1,),
        [whole(kept.shape)] * 2,
        [whole((deep, cols))] * HEADS,
        [((deep, cols), jnp.bfloat16)] * HEADS,
        scalars=(spot,),
        args=(kept, arrived),
    )


def pick_rows(w_fc2, w_out, spot):
    cols = w_fc2.shape[1]
    tall, low = w_fc2.shape[0] // HEADS // 4, w_out.shape[0] // HEADS // 4

    def kernel(spot, a, b, *outs):
        for k, out in enumerate(outs):

            @pl.when(pl.program_id(0) == k)
            def _(out=out):
                out[:tall, :] = a[...]
                out[tall:, :] = b[...]

    def block(deep):
        return pl.BlockSpec(
            (deep, cols), lambda k, spot: (4 * member_at(spot, k) + 2 * spot[0] + spot[1], 0)
        )

    return call(
        kernel,
        (HEADS,),
        [block(tall), block(low)],
        [whole((tall + low, cols))] * HEADS,
        [((tall + low, cols), w_fc2.dtype)] * HEADS,
        scalars=(spot,),
        args=(w_fc2, w_out),
    )


def stack_members(pieces, spot):
    shape = pieces[0].shape

    def kernel(spot, *refs):
        for k, ref in enumerate(refs[:-1]):
            refs[-1][member_at(spot, k, -1)] = ref[...]

    return call(
        kernel,
        (1,),
        [whole(shape)] * HEADS,
        [whole((HEADS, *shape))],
        [((HEADS, *shape), pieces[0].dtype)],
        scalars=(spot,),
        args=pieces,
    )[0]


def to_members(pieces):
    ring = lax.axis_size(CTX)
    came = [pieces[0]]
    for k in range(1, len(pieces)):
        route = [
            (2 * z + y, (z + k // 2) % ring * 2 + (y ^ (k % 2))) for z in range(ring) for y in range(2)
        ]
        came.append(lax.ppermute(pieces[k], GROUP, route))
    return came


def fold_slots(kept, arrived, slots):
    deep, width = kept.shape
    cols = width // slots

    def kernel(a, b, *outs):
        for s, out in enumerate(outs):
            here = slice(s * cols, (s + 1) * cols)
            out[...] = (a[:, here] + b[:, here].astype(jnp.float32)).astype(jnp.bfloat16)

    return call(
        kernel,
        (1,),
        [whole(kept.shape)] * 2,
        [whole((deep, cols))] * slots,
        [((deep, cols), jnp.bfloat16)] * slots,
        args=(kept, arrived),
    )


def sum_side(mine, came, spot):
    ring, total = mine.shape

    def kernel(spot, a, b, *refs):
        refs[-1][...] = a[...] + b[...]
        for r, out in enumerate(refs[:-1]):
            out[...] = refs[-1][pl.ds((spot[4] + r) % ring, 1), :]

    return call(
        kernel,
        (1,),
        [whole(mine.shape)] * 2,
        [whole((1, total))] * ring,
        [((1, total), jnp.float32)] * ring,
        [pltpu.VMEM((ring, total), jnp.float32)],
        scalars=(spot,),
        args=(mine, came),
    )


def sum_vectors(mine, sent, spot):
    came = rotated(sent, FSDP, 1)
    total, *rows = sum_side(mine, came, spot)
    for r, row in enumerate(rows, 1):
        total = total + rotated(row, CTX, r)
    total = total + rotated(total, CORE, 1)
    return (total + rotated(total, X, 1))[0]


def spread_columns(pieces, meta):
    deep, wide = pieces[0].shape

    def kernel(meta, p0, p1, p2, p3, out):
        for d, p in enumerate((p0, p1, p2, p3)):

            @pl.when(pl.program_id(0) == d)
            def _(p=p):
                out[...] = p[...].astype(jnp.float32)

    return call(
        kernel,
        (4,),
        [whole((deep, wide))] * 4,
        [pl.BlockSpec((deep, wide), lambda d, meta: (meta[0] ^ d, 0))],
        [((4 * deep, wide), jnp.float32)],
        scalars=(meta,),
        args=pieces,
    )[0]


def spread_rows(pieces, meta):
    members, deep, cols = pieces[0].shape
    low = HEAD // 4
    tall = deep - low

    def kernel(meta, p0, p1, p2, p3, fc2, out):
        for d, p in enumerate((p0, p1, p2, p3)):

            @pl.when(pl.program_id(0) == d)
            def _(p=p):
                for m in range(members):
                    fc2[m, 0] = p[m, :tall, :].astype(jnp.float32)
                    out[m, 0] = p[m, tall:, :].astype(jnp.float32)

    fc2, out = call(
        kernel,
        (4,),
        [whole(pieces[0].shape)] * 4,
        [
            pl.BlockSpec((members, 1, tall, cols), lambda d, meta: (0, meta[0] ^ d, 0, 0)),
            pl.BlockSpec((members, 1, low, cols), lambda d, meta: (0, meta[0] ^ d, 0, 0)),
        ],
        [((members, 4, tall, cols), jnp.float32), ((members, 4, low, cols), jnp.float32)],
        scalars=(meta,),
        args=pieces,
    )
    return fc2.reshape(-1, cols), out.reshape(-1, cols)


def spread_halves(own, twin, spot):
    deep, wide = own[0].shape
    steps = 2

    def kernel(spot, a, b, c, d, out):
        @pl.when(pl.program_id(0) == 0)
        def _():
            out[...] = a[...].astype(jnp.float32) + b[...].astype(jnp.float32)

        @pl.when(pl.program_id(0) == 1)
        def _():
            out[...] = c[...].astype(jnp.float32) + d[...].astype(jnp.float32)

    block = (deep // steps, wide)
    mine = pl.BlockSpec(block, lambda h, j, _: (jnp.where(h == 0, j, steps - 1), 0))
    theirs = pl.BlockSpec(block, lambda h, j, _: (jnp.where(h == 0, 0, j), 0))
    return call(
        kernel,
        (2, steps),
        [mine, mine, theirs, theirs],
        [pl.BlockSpec(block, lambda h, j, spot: ((spot[1] ^ h) * steps + j, 0))],
        [((2 * deep, wide), jnp.float32)],
        scalars=(spot,),
        args=(*own, *twin),
    )[0]


def tensor_layer(*args):
    return group_layer(*args)


def group_layer(
    hidden,
    cotangent,
    ln1_gain,
    ln1_bias,
    ln2_gain,
    ln2_bias,
    w_qkv,
    b_qkv,
    w_out,
    b_out,
    w_fc1,
    b_fc1,
    w_fc2,
    b_fc2,
):
    f32, bf16 = jnp.float32, jnp.bfloat16
    ring = lax.axis_size(CTX)
    members = ring * lax.axis_size(FSDP)
    ctx_at, side = lax.axis_index(CTX), lax.axis_index(FSDP)
    x_at, core_at = lax.axis_index(X), lax.axis_index(CORE)
    place, replica = lax.axis_index(GROUP), lax.axis_index(REPLICAS)
    inputs, upstream_own = hidden[0], cotangent[0]
    row_count, width = inputs.shape
    length = ring * row_count
    cols = width // members
    slots = w_qkv.shape[1] // HEAD

    def quarter(array, dim):
        size = array.shape[dim] // 4
        return lax.dynamic_slice_in_dim(array, replica * size, size, dim)

    hid = gather_line(inputs)
    hid_other = gather_side(hid)
    cot = gather_line(upstream_own)
    cot_other = gather_side(cot)

    kind_of = [[0] * slots for _ in range(members)]
    for block in range(slots * members):
        kind_of[block % members][block % slots] = block // HEADS
    kinds = jnp.asarray(kind_of, jnp.int32)[place]
    meta = jnp.concatenate([replica[None], kinds]).astype(jnp.int32)
    spot = jnp.stack([x_at, core_at, place, side, ctx_at]).astype(jnp.int32)
    token_pos = (
        ((ctx_at - jnp.arange(ring)) % ring)[:, None] * row_count + jnp.arange(row_count)[None]
    ).reshape(length)
    cosine, sine_table = (t[:, 0] for t in rotary_tables(token_pos.astype(f32), ROT))
    rest = ((0, 0), (0, ROPE_LANES - ROT))
    tables = (
        jnp.pad(jnp.concatenate([cosine, cosine], axis=1), rest, constant_values=1.0),
        jnp.pad(jnp.concatenate([-sine_table, sine_table], axis=1), rest),
    )
    positions = (token_pos[:, None], token_pos[None, :])
    b_fc1 = b_fc1.astype(f32)[None]
    twin_core, own_core = (1 - core_at)[None], core_at[None]
    vector = (ln1_gain, ln1_bias, ln2_gain, ln2_bias, b_out, b_fc2, b_qkv)
    vector, meta, spot, tables, positions, b_fc1, twin_core, own_core = lax.optimization_barrier(
        (vector, meta, spot, tables, positions, b_fc1, twin_core, own_core)
    )
    vector = pack_columns([v[None] for v in vector])[0]
    vectors = [vector]
    for r in range(1, ring):
        vectors.append(rotated(vector, CTX, r))
    vectors = jnp.stack(vectors)
    came = rotated(vectors, FSDP, 1)
    both = jnp.stack([vectors, came])
    both = both[jnp.arange(2) ^ side]
    small = jnp.transpose(both[:, (ctx_at - jnp.arange(ring)) % ring], (1, 0, 2))
    small = small.reshape(members, -1).astype(f32)
    gain_one, shift_one, gain_two, shift_two, full_bout, full_bfc2 = (
        small[:, i * cols : (i + 1) * cols].reshape(width) for i in range(6)
    )
    params = jnp.stack([gain_one, shift_one, gain_two, shift_two])
    bias_qkv = small[:, 6 * cols :].reshape(3, HEADS, HEAD)
    bias_qkv = lax.dynamic_slice_in_dim(bias_qkv, place, 1, 1)

    qkv_quarter = quarter(w_qkv, 0)
    moved_columns = []
    for s in range(slots):
        moved_columns.append(
            lax.ppermute(
                qkv_quarter[:, s * HEAD : (s + 1) * HEAD],
                GROUP,
                [(i, (slots * i + s) % members) for i in range(members)],
            )
        )
    moved_columns = pack_columns(moved_columns)

    def replicas(own):
        over_x = rotated(own, X, 1)
        twin = rotated(own, CORE, 1)
        return [own, twin, over_x, rotated(over_x, CORE, 1)]

    head_columns = replicas(moved_columns)
    picked = pick_rows(w_fc2, w_out, spot)
    picked = to_members(picked)
    moved_rows = stack_members(picked, spot)
    row_pieces = replicas(moved_rows)

    rows = (hid, hid_other)
    normed = []
    for i in range(2):
        normed.append(norm_fc1(rows[i], params, w_fc1, b_fc1))
    attn_in, mlp_in, centre, scale, act, slope = zip(*normed)
    head_qkv, *first = head_attention(attn_in[0], head_columns, bias_qkv, tables, positions, meta)
    second = head_attention(attn_in[1], [head_qkv], bias_qkv, tables, positions, meta)
    qkv, attended, log_total = zip(first, second)

    def send_places(partial, arrived):
        own, far = fold_blocks(partial, arrived, (0, 2))
        up = lax.ppermute(far, CTX, [(0, 1), (1, 2)])
        down = lax.ppermute(far, CTX, [(2, 1), (3, 2)])
        low, high = fold_blocks(partial, arrived, (1, 3), (down, up))
        low = rotated(low, CTX, -1)
        high = rotated(high, CTX, -3)
        return [own, low, high]

    row_weights, branch_other = project_other(row_pieces, act[1], attended[1], meta)
    out_y = gather_side([branch_other])[0]
    branch = project_own(row_weights, act[0], attended[0])
    out_z = send_places(branch, out_y)

    row_part, row_kept, *upstream = rows_gradient(act, attended, cot + cot_other, spot)
    backs, inner = [None, None], [None, None]
    for i in (1, 0):
        backs[i] = backward(
            upstream[i], row_weights, slope[i], attended[i], qkv[i], log_total[i], tables, positions
        )
        inner[i] = input_side(
            rows[i],
            backs[i][0],
            backs[i][1],
            w_fc1,
            head_qkv,
            centre[i],
            scale[i],
            params,
        )
    d_preact, d_qkv, sum_fc1, sum_qkv, sum_cot = zip(*backs)
    u_y = gather_side(inner[1][1:])[0]
    u_z = send_places(inner[0][1], u_y)

    row_part = rotated(row_part, CORE, 1)
    row_sent, row_keep = rows_gradient(act, None, upstream, spot, (row_part, row_kept))
    row_sent = rotated(row_sent, X, 1)
    col_part = columns_gradient(attn_in, d_qkv, meta, spot)[0]
    col_part = rotated(col_part, CORE, 1)
    col_sent, col_keep = columns_gradient(attn_in, d_qkv, meta, spot, col_part)
    col_sent = rotated(col_sent, X, 1)
    fc1_part = fc1_gradient(mlp_in, d_preact, twin_core)
    fc1_part = rotated(fc1_part, CORE, 1)
    fc1_half = fc1_gradient(mlp_in, d_preact, own_core, fc1_part)
    fc1_sent = rotated(fc1_half, X, 1)
    fc1_twin = rotated(fc1_half, CORE, 1)
    fc1_both = rotated(fc1_sent, CORE, 1)

    vectors = pack_sums((inner[0][0], inner[1][0]), sum_qkv, sum_cot, sum_fc1, spot)
    vectors = sum_vectors(*vectors, spot)
    g1, s1, g2, s2 = (vectors[i * cols : (i + 1) * cols] for i in range(4))
    bqkv_grad, bout_grad, bfc1_grad = jnp.split(
        vectors[4 * cols :], (slots * HEAD, slots * HEAD + cols)
    )

    col_part = fold_slots(col_keep, col_sent, slots)
    col_back = []
    for s in range(slots):
        col_back.append(
            lax.ppermute(
                col_part[s],
                GROUP,
                [((slots * i + s) % members, i) for i in range(members)],
            )
        )
    row_part = fold_rows(row_keep, row_sent, spot)
    row_part = to_members(row_part)
    row_back = stack_members(row_part, spot)
    fc1_grad = spread_halves((fc1_half, fc1_sent), (fc1_twin, fc1_both), spot)
    col_back = pack_columns(col_back)
    col_back = replicas(col_back)
    qkv_grad = spread_columns(col_back, meta)
    row_back = replicas(row_back)
    fc2_grad, out_grad = spread_rows(row_back, meta)

    own_f = inputs.astype(f32)
    branch = sum(v.astype(f32) for v in out_z)
    output = (own_f + (branch + full_bout + full_bfc2)).astype(bf16)
    merged = sum(v.astype(f32) for v in u_z)
    own_normed, own_std = normalize(own_f)
    input_grad = (
        upstream_own.astype(f32) + norm_backward(merged, own_normed, own_std)
    ).astype(bf16)

    return (
        output[None],
        input_grad[None],
        g1,
        s1,
        g2,
        s2,
        qkv_grad,
        bqkv_grad,
        out_grad,
        bout_grad,
        fc1_grad,
        bfc1_grad,
        fc2_grad,
        bout_grad,
    )


def solution(mesh):
    sizes = dict(mesh.shape)
    fits = (sizes[CTX], sizes[FSDP], sizes[DP]) == (HEADS // 2, 2, 4)
    if fits:
        mesh = Mesh(
            mesh.devices.reshape(2, 2, sizes[CTX], sizes[FSDP]),
            (X, CORE, CTX, FSDP),
        )
    rows = P((*(REPLICAS if fits else (DP,)), FSDP), CTX, None)
    vector, matrix = P(GROUP), P(None, GROUP)
    params = (vector,) * 4 + (matrix, vector) * 4
    return jax.shard_map(
        tensor_layer if fits else plain_layer,
        mesh=mesh,
        in_specs=(rows, rows, *params),
        out_specs=(rows, rows, *params),
        check_vma=False,
    )
```

time: 3060 us -> 551 us (0.18)
  waiting for transfers between devices: 2400 us -> 211 us
  blocking collectives: 286 us -> 0 us
  matrix products: 162 us -> 0 us
  Pallas kernels: 0 us -> 112 us
  starting transfers between devices: 127 us -> 178 us
    all_gather x9 -> x0, waiting for transfers between devices: 1510 us -> none  [the longest x1 505 us: body(): lax.all_gather(w_fc1, ('ctx', 'fsdp'), axis=1, tiled=True)]
    psum x1 -> x0, waiting for transfers between devices: 410 us -> none  [body(): lax.psum((owned[0], owned[1], owned[2], owned[3], owned[4], owned[5], own...]
    all_gather x8 -> x0, blocking collectives: 274 us -> none  [the longest x1 75 us: body(): lax.all_gather(b_fc1, ('ctx', 'fsdp'), axis=0, tiled=True)]
    dot_general x34 -> x0, matrix products: 162 us -> none  [the longest x4 57 us: contract_cols(): lax.dot_general(left, right, (((1,), (1,)), ((), ())), preferred_element_...]
    ppermute x14 -> x76, waiting for transfers between devices: 356 us -> 211 us  [the longest x48 191 us: rotated(): lax.ppermute(value, axis, [(i, (i + steps) % count) for i in range(count)])]
    all_to_all x3 -> x0, waiting for transfers between devices: 113 us -> none  [the longest x1 65 us: body(): lax.all_to_all(d_preact_bf, ('ctx', 'fsdp'), split_axis=1, concat_axis=0,...]
    pallas_call x0 -> x33, Pallas kernels: none -> 112 us  [call(): pl.pallas_call(kernel, grid_spec=pltpu.PrefetchScalarGridSpec(num_scalar_...]
    ppermute x14 -> x76, starting transfers between devices: 88.3 us -> 178 us  [the longest x48 81.7 us: rotated(): lax.ppermute(value, axis, [(i, (i + steps) % count) for i in range(count)])]
  transfers between devices with their start and end apart: 28 -> 76, of which waited for: 23 -> 23; matrix products, arithmetic and copies ran while one was open for 7% -> 2% of each run, Pallas kernels for 0% -> 20%
where the time goes in v2:
time: 551 us; the launch traced here: 545 us
  waiting for transfers between devices  211 us (38%)
  starting transfers between devices  178 us (32%)
  Pallas kernels  112 us (20%)
  local copies, waits for them, and re-layouts  34.1 us (6%)
  other arithmetic  7.43 us (1%)
    ppermute x48, waiting for transfers between devices, rotated(): lax.ppermute(value, axis, [(i, (i + steps) % count) for i in range(count)])  191 us
    pallas_call x33, Pallas kernels, call(): pl.pallas_call(kernel, grid_spec=pltpu.PrefetchScalarGridSpec(num_scalar_...  112 us
    ppermute x48, starting transfers between devices, rotated(): lax.ppermute(value, axis, [(i, (i + steps) % count) for i in range(count)])  81.7 us
    ppermute x14, starting transfers between devices, to_members(): came.append(lax.ppermute(pieces[k], GROUP, route))  67 us
    unnamed x138, local copies, waits for them, and re-layouts  28.9 us
  transfers between devices with their start and end apart: 76, of which 23 were waited for; matrix products, arithmetic and copies ran while one was open for 2% of the time, Pallas kernels for 20%

profile of v2, /device:TPU:0, one launch (start us, length us, event | category | flops | bytes accessed | tf_op | source)
XLA Modules:
  0.0 544.7 jit_solution(13922784768758835062)
XLA Ops:
  3.9 5.1 collective-permute-start.20
  10.0 2.2 copy-done.11
  12.2 1.9 shard_map.254
  17.7 2.5 collective-permute-start.1
  22.4 1.9 collective-permute-done.21
  25.2 3.0 collective-permute-start.4
  30.1 6.3 %collective-permute-start.24 = (bf16[512,256]{1,0:T(8,128)(2,1)S(1)}, bf16[512,256]{1,0:T(8,128)(2,1)S(1)}, u32[]{:S(2)}, u32[]{:S(2)}) collective-permute-start(bf16[512,256]{1,0:T(8,128)(2,1)S(1)} %get-tuple-element.204), channel_id=1, source_target_pairs={{0,2},{1,5},{2,0},{3,3},{4,6},{5,1},{6,4},{7,7},{8,10},{9,13},{10,... | collective-permute-start | bytes 786440 | tf_op jit(solution)/shard_map/ppermute | solution.py:1215
  38.8 15.2 %collective-permute-start.6 = (bf16[320,256]{1,0:T(8,128)(2,1)S(1)}, bf16[320,256]{1,0:T(8,128)(2,1)S(1)}, u32[]{:S(2)}, u32[]{:S(2)}) collective-permute-start(bf16[320,256]{1,0:T(8,128)(2,1)S(1)} %get-tuple-element.117), channel_id=1, source_target_pairs={{0,7},{1,6},{2,1},{3,0},{4,3},{5,2},{6,5},{7,4},{8,15},{9,14},{10,... | collective-permute-start | bytes 491528 | tf_op jit(solution)/shard_map/ppermute | solution.py:1002
  57.7 4.9 collective-permute-start.35
  62.7 3.0 collective-permute-done.23.refs_1_
  67.2 19.3 %collective-permute-start.11 = (bf16[128,2048]{1,0:T(8,128)(2,1)S(1)}, bf16[128,2048]{1,0:T(8,128)(2,1)S(1)}, u32[]{:S(2)}, u32[]{:S(2)}) collective-permute-start(bf16[128,2048]{1,0:T(8,128)(2,1)S(1)} %bitcast.64), channel_id=1, source_target_pairs={{0,2},{2,4},{4,6},{6,0},{1,3},{3,5},{5,7},{7,1},{8,10},{10,12},{12... | collective-permute-start | bytes 1572872 | tf_op jit(solution)/shard_map/ppermute | solution.py:349
  88.0 6.1 %collective-permute-done.33.refs_1_ = bf16[128,2048]{1,0:T(8,128)(2,1)} collective-permute-done((bf16[128,2048]{1,0:T(8,128)(2,1)S(1)}, bf16[128,2048]{1,0:T(8,128)(2,1)}, u32[]{:S(2)}, u32[]{:S(2)}) %collective-permute-start.33) | collective-permute-done | bytes 524320 | tf_op jit(solution)/shard_map/ppermute | solution.py:349
  99.2 14.0 %collective-permute-done.11.refs_1_ = bf16[128,2048]{1,0:T(8,128)(2,1)S(1)} collective-permute-done((bf16[128,2048]{1,0:T(8,128)(2,1)S(1)}, bf16[128,2048]{1,0:T(8,128)(2,1)S(1)}, u32[]{:S(2)}, u32[]{:S(2)}) %collective-permute-start.11) | collective-permute-done | bytes 524320 | tf_op jit(solution)/shard_map/ppermute | solution.py:349
  123.3 1.7 shard_map.255.p0
  129.5 4.6 collective-permute-start.12
  135.5 2.4 collective-permute-done.17.refs_3_
  139.0 10.0 %collective-permute-done.12.refs_1_ = bf16[128,2048]{1,0:T(8,128)(2,1)S(1)} collective-permute-done((bf16[128,2048]{1,0:T(8,128)(2,1)S(1)}, bf16[128,2048]{1,0:T(8,128)(2,1)S(1)}, u32[]{:S(2)}, u32[]{:S(2)}) %collective-permute-start.12) | collective-permute-done | bytes 524320 | tf_op jit(solution)/shard_map/ppermute | solution.py:349
  149.0 2.0 collective-permute-start.38
  152.6 1.8 collective-permute-start.39
  154.4 5.8 %collective-permute-done.16.refs_2_ = bf16[128,2048]{1,0:T(8,128)(2,1)S(1)} collective-permute-done((bf16[128,2048]{1,0:T(8,128)(2,1)S(1)}, bf16[128,2048]{1,0:T(8,128)(2,1)S(1)}, u32[]{:S(2)}, u32[]{:S(2)}) %collective-permute-start.16) | collective-permute-done | bytes 524320 | tf_op jit(solution)/shard_map/ppermute | solution.py:349
  160.9 2.2 copy-done
  163.1 7.6 %shard_map.258 = (bf16[512,2048]{1,0:T(8,128)(2,1)S(1)}, bf16[512,2048]{1,0:T(8,128)(2,1)S(1)}, f32[512,1]{1,0:T(8,128)S(1)}, f32[512,1]{1,0:T(8,128)S(1)}, bf16...) custom-call(bf16[128,2048]{1,0:T(8,128)(2,1)S(1)} %bitcast.66, bf16[128,2048]{1,0:T(8,128)(2,1)S(1)} %collective-permute-done.11.refs_1_, ...), custom_call_target="tpu_custom_call" | custom-call | tf_op jit(solution)/shard_map/pallas_call | solution.py:385
  171.5 8.4 %shard_map.257 = (bf16[512,2048]{1,0:T(8,128)(2,1)S(1)}, bf16[512,2048]{1,0:T(8,128)(2,1)S(1)}, f32[512,1]{1,0:T(8,128)S(1)}, f32[512,1]{1,0:T(8,128)S(1)}, bf16...) custom-call(bf16[128,2048]{1,0:T(8,128)(2,1)} %collective-permute-done.10.refs_0_, ...), custom_call_target="tpu_custom_call" | custom-call | tf_op jit(solution)/shard_map/pallas_call | solution.py:385
  179.8 5.5 %shard_map.260 = (bf16[3,2048,256]{2,1,0:T(8,128)(2,1)S(1)}, bf16[3,512,256]{2,1,0:T(8,128)(2,1)S(1)}, bf16[512,256]{1,0:T(8,128)(2,1)S(1)}, f32[512,1]{1,0:T(8,128)S(1)}) custom-call(s32[4]{0:T(128)S(1)} %pad_add_fusion.meta, bf16[512,2048]{1,0:T(8,128)(2,1)S(1)} %get-tuple-element.128.x.x0.y0, bf16[512,768]{1,0:T(8,128)(2,1)S(1)} %copy-done.13, ...), custom_call_target="tpu_custom_call" | custom-call | tf_op jit(solution)/shard_map/pallas_call | solution.py:385
  186.2 4.1 shard_map.261
  190.4 2.4 collective-permute-done.39.refs_6_
  192.8 7.8 %shard_map.266 = (bf16[2,320,2048]{2,1,0:T(8,128)(2,1)}, f32[2,64,2048]{2,1,0:T(8,128)S(1)}, bf16[512,2048]{1,0:T(8,128)(2,1)S(1)}, bf16[512,2048]{1,0:T(8,128)(2,1)S(1)}) custom-call(s32[5]{0:T(128)S(1)} %stack.47.spot, bf16[512,1024]{1,0:T(8,128)(2,1)S(1)} %get-tuple-element.136.act.x0.y0, bf16[512,1024]{1,0:T(8,128)(2,1)S(1)} %get-tuple-element.126.act.x1.y1, ...), custom_call_target="tpu_custom_call" | custom-call | tf_op jit(solution)/shard_map/pallas_call | solution.py:385
  204.0 7.1 %shard_map.262 = (bf16[1280,2048]{1,0:T(8,128)(2,1)S(1)}, bf16[512,2048]{1,0:T(8,128)(2,1)}) custom-call(s32[4]{0:T(128)S(1)} %pad_add_fusion.meta, bf16[8,320,256]{2,1,0:T(8,128)(2,1)} %shard_map.255.p0, bf16[8,320,256]{2,1,0:T(8,128)(2,1)S(1)} %collective-permute-done.7.p1, bf16[8,320,256]{2,1,0:T(8,128)(2,1)} %collective-permute-done.8.p2, ...), custom_call_target="tpu_custom_call" | custom-call | tf_op jit(solution)/shard_map/pallas_call | solution.py:385
  211.2 5.1 shard_map.269
  219.1 5.1 shard_map.267
  224.2 4.6 shard_map.275
  229.2 4.4 shard_map.284
  234.3 7.4 %shard_map.270 = (f32[8,2048]{1,0:T(8,128)S(1)}, bf16[512,2048]{1,0:T(8,128)(2,1)}) custom-call(bf16[128,2048]{1,0:T(8,128)(2,1)} %collective-permute-done.10.refs_0_, bf16[128,2048]{1,0:T(8,128)(2,1)S(1)} %collective-permute-done.12.refs_1_, bf16[128,2048]{1,0:T(8,128)(2,1)S(1)} %copy-done.22, bf16[128,2048]{1,0:T(8,128)(2,1)} %collective-permute-done.17.refs_3_, ...), custom_call_target="tpu_custom_call" | custom-call | tf_op jit(solution)/shard_map/pallas_call | solution.py:385
  241.7 5.8 %shard_map.268 = (f32[8,2048]{1,0:T(8,128)S(1)}, bf16[512,2048]{1,0:T(8,128)(2,1)S(1)}) custom-call(bf16[128,2048]{1,0:T(8,128)(2,1)S(1)} %bitcast.67, bf16[128,2048]{1,0:T(8,128)(2,1)S(1)} %copy-done.20, bf16[128,2048]{1,0:T(8,128)(2,1)S(1)} %broadcast_select_fusion.1.refs_2_, bf16[128,2048]{1,0:T(8,128)(2,1)S(1)} %copy-done.18, ...), custom_call_target="tpu_custom_call" | custom-call | tf_op jit(solution)/shard_map/pallas_call | solution.py:385
  249.6 33.3 %collective-permute-done.46.b = f32[4,3072]{1,0:T(4,128)S(1)} collective-permute-done((f32[4,3072]{1,0:T(4,128)S(1)}, f32[4,3072]{1,0:T(4,128)S(1)}, u32[]{:S(2)}, u32[]{:S(2)}) %collective-permute-start.46) | collective-permute-done | bytes 49184 | tf_op jit(solution)/shard_map/ppermute | solution.py:349
  283.5 5.2 collective-permute-start.47
  290.4 3.3 collective-permute-start.48
  295.0 3.9 shard_map.276
  299.0 5.8 %shard_map.280 = (bf16[320,2048]{1,0:T(8,128)(2,1)S(1)}, f32[320,2048]{1,0:T(8,128)S(1)}) custom-call(s32[5]{0:T(128)S(1)} %stack.47.spot, bf16[512,1024]{1,0:T(8,128)(2,1)S(1)} %get-tuple-element.136.act.x0.y0, bf16[512,1024]{1,0:T(8,128)(2,1)S(1)} %get-tuple-element.126.act.x1.y1, bf16[512,1024]{1,0:T(8,128)(2,1)S(1)} %get-tuple-element.136.act.x0.y0, ...), custom_call_target="tpu_custom_call" | custom-call | tf_op jit(solution)/shard_map/pallas_call | solution.py:385
  307.0 4.7 shard_map.285.a
  313.8 4.0 shard_map.263.a
  318.1 77.2 %collective-permute-done.51 = f32[1,3072]{1,0:T(1,128)S(1)} collective-permute-done((f32[1,3072]{1,0:T(1,128)S(1)}, f32[1,3072]{1,0:T(1,128)S(1)}, u32[]{:S(2)}, u32[]{:S(2)}) %collective-permute-start.51) | collective-permute-done | bytes 12320 | tf_op jit(solution)/shard_map/ppermute | solution.py:349
  395.3 2.8 collective-permute-start.30
  399.1 2.8 collective-permute-start.43
  401.9 8.5 %collective-permute-done.30.refs_1_ = bf16[128,2048]{1,0:T(8,128)(2,1)S(1)} collective-permute-done((bf16[128,2048]{1,0:T(8,128)(2,1)S(1)}, bf16[128,2048]{1,0:T(8,128)(2,1)S(1)}, u32[]{:S(2)}, u32[]{:S(2)}) %collective-permute-start.30) | collective-permute-done | bytes 524320 | tf_op jit(solution)/shard_map/ppermute | solution.py:1245
  412.0 7.7 %collective-permute-start.55 = (bf16[512,256]{1,0:T(8,128)(2,1)S(1)}, bf16[512,256]{1,0:T(8,128)(2,1)S(1)}, u32[]{:S(2)}, u32[]{:S(2)}) collective-permute-start(bf16[512,256]{1,0:T(8,128)(2,1)S(1)} %get-tuple-element.182), channel_id=1, source_target_pairs={{1,0},{4,1},{7,2},{2,3},{5,4},{0,5},{3,6},{6,7},{9,8},{12,9},{15,1... | collective-permute-start | bytes 786440 | tf_op jit(solution)/shard_map/ppermute | solution.py:1302
  420.6 4.0 collective-permute-start.62
  424.5 8.9 %collective-permute-start.63 = (bf16[320,256]{1,0:T(8,128)(2,1)S(1)}, bf16[320,256]{1,0:T(8,128)(2,1)S(1)}, u32[]{:S(2)}, u32[]{:S(2)}) collective-permute-start(bf16[320,256]{1,0:T(8,128)(2,1)S(1)} %get-tuple-element.190), channel_id=1, source_target_pairs={{0,2},{1,3},{2,4},{3,5},{4,6},{5,7},{6,0},{7,1},{8,10},{9,11},{10,... | collective-permute-start | bytes 491528 | tf_op jit(solution)/shard_map/ppermute | solution.py:1002
  433.4 14.7 %collective-permute-start.65 = (bf16[320,256]{1,0:T(8,128)(2,1)S(1)}, bf16[320,256]{1,0:T(8,128)(2,1)S(1)}, u32[]{:S(2)}, u32[]{:S(2)}) collective-permute-start(bf16[320,256]{1,0:T(8,128)(2,1)S(1)} %get-tuple-element.192), channel_id=1, source_target_pairs={{0,4},{1,5},{2,6},{3,7},{4,0},{5,1},{6,2},{7,3},{8,12},{9,13},{10,... | collective-permute-start | bytes 491528 | tf_op jit(solution)/shard_map/ppermute | solution.py:1002
  448.1 1.9 collective-permute-start.56
  450.1 5.1 collective-permute-done.64.refs_3_
  456.2 15.2 %collective-permute-start.68 = (bf16[320,256]{1,0:T(8,128)(2,1)S(1)}, bf16[320,256]{1,0:T(8,128)(2,1)S(1)}, u32[]{:S(2)}, u32[]{:S(2)}) collective-permute-start(bf16[320,256]{1,0:T(8,128)(2,1)S(1)} %get-tuple-element.195), channel_id=1, source_target_pairs={{0,7},{1,6},{2,1},{3,0},{4,3},{5,2},{6,5},{7,4},{8,15},{9,14},{10,... | collective-permute-start | bytes 491528 | tf_op jit(solution)/shard_map/ppermute | solution.py:1002
  473.6 12.6 %collective-permute-start.31 = (bf16[128,2048]{1,0:T(8,128)(2,1)S(1)}, bf16[128,2048]{1,0:T(8,128)(2,1)S(1)}, u32[]{:S(2)}, u32[]{:S(2)}) collective-permute-start(bf16[128,2048]{1,0:T(8,128)(2,1)S(1)} %get-tuple-element.141), channel_id=1, source_target_pairs={{0,6},{2,0},{4,2},{6,4},{1,7},{3,1},{5,3},{7,5},{8,14},{10,8},{12,... | collective-permute-start | bytes 1572872 | tf_op jit(solution)/shard_map/ppermute | solution.py:349
  486.2 3.8 collective-permute-start.44
  491.0 1.9 collective-permute-done.31
  492.9 10.0 %collective-permute-done.32 = bf16[128,2048]{1,0:T(8,128)(2,1)S(1)} collective-permute-done((bf16[128,2048]{1,0:T(8,128)(2,1)S(1)}, bf16[128,2048]{1,0:T(8,128)(2,1)S(1)}, u32[]{:S(2)}, u32[]{:S(2)}) %collective-permute-start.32) | collective-permute-done | bytes 524320 | tf_op jit(solution)/shard_map/ppermute | solution.py:349
  502.9 6.8 %collective-permute-done.44 = bf16[128,2048]{1,0:T(8,128)(2,1)S(1)} collective-permute-done((bf16[128,2048]{1,0:T(8,128)(2,1)S(1)}, bf16[128,2048]{1,0:T(8,128)(2,1)S(1)}, u32[]{:S(2)}, u32[]{:S(2)}) %collective-permute-start.44) | collective-permute-done | bytes 524320 | tf_op jit(solution)/shard_map/ppermute | solution.py:349
  510.4 11.0 %collective-permute-done.45 = bf16[128,2048]{1,0:T(8,128)(2,1)S(1)} collective-permute-done((bf16[128,2048]{1,0:T(8,128)(2,1)S(1)}, bf16[128,2048]{1,0:T(8,128)(2,1)S(1)}, u32[]{:S(2)}, u32[]{:S(2)}) %collective-permute-start.45) | collective-permute-done | bytes 524320 | tf_op jit(solution)/shard_map/ppermute | solution.py:349
  522.0 3.2 collective-permute-done.58.p2
  527.5 1.9 fusion.12
  529.4 1.9 collective-permute-done.59.p3
  531.2 3.6 shard_map.279
  534.8 4.7 shard_map.283
  539.5 4.3 shard_map.286
  (312 shorter events, 76.7 us)
Async XLA Ops:
  3.9 16.2 %collective-permute-start.20 = (bf16[2304]{0:T(1024)(128)(2,1)S(1)}, bf16[2304]{0:T(1024)(128)(2,1)S(1)}, u32[]{:S(2)}, u32[]{:S(2)}) collective-permute-start(bf16[2304]{0:T(1024)(128)(2,1)S(1)} %reduce), channel_id=1, source_target_pairs={{0,6},{2,0},{4,2},{6,4},{1,7},{3,1},{5,3},{7,5},{8,14},{10,8},{12,... | collective-permute-start | bytes 13832 | tf_op jit(solution)/shard_map/ppermute | solution.py:349
  17.7 11.8 %collective-permute-start.1 = (bf16[320,256]{1,0:T(8,128)(2,1)}, bf16[320,256]{1,0:T(8,128)(2,1)S(1)}, u32[]{:S(2)}, u32[]{:S(2)}) collective-permute-start(bf16[320,256]{1,0:T(8,128)(2,1)} %get-tuple-element.112), channel_id=1, source_target_pairs={{0,2},{1,3},{2,4},{3,5},{4,6},{5,7},{6,0},{7,1},{8,10},{9,11},{10,... | collective-permute-start | bytes 491528 | tf_op jit(solution)/shard_map/ppermute | solution.py:1002
  20.8 65.7 %collective-permute-start.37 = (bf16[128,2048]{1,0:T(8,128)(2,1)S(1)}, bf16[128,2048]{1,0:T(8,128)(2,1)}, u32[]{:S(2)}, u32[]{:S(2)}) collective-permute-start(bf16[128,2048]{1,0:T(8,128)(2,1)S(1)} %bitcast.68), channel_id=1, source_target_pairs={{0,1},{1,0},{2,3},{3,2},{4,5},{5,4},{6,7},{7,6},{8,9},{9,8},{10,11... | collective-permute-start | bytes 1572872 | tf_op jit(solution)/shard_map/ppermute | solution.py:349
  22.4 14.0 %collective-permute-start.2 = (bf16[320,256]{1,0:T(8,128)(2,1)}, bf16[320,256]{1,0:T(8,128)(2,1)S(1)}, u32[]{:S(2)}, u32[]{:S(2)}) collective-permute-start(bf16[320,256]{1,0:T(8,128)(2,1)} %get-tuple-element.113), channel_id=1, source_target_pairs={{0,3},{1,2},{2,5},{3,4},{4,7},{5,6},{6,1},{7,0},{8,11},{9,10},{10,... | collective-permute-start | bytes 491528 | tf_op jit(solution)/shard_map/ppermute | solution.py:1002
  24.3 13.9 %collective-permute-start.3 = (bf16[320,256]{1,0:T(8,128)(2,1)}, bf16[320,256]{1,0:T(8,128)(2,1)S(1)}, u32[]{:S(2)}, u32[]{:S(2)}) collective-permute-start(bf16[320,256]{1,0:T(8,128)(2,1)} %copy-done.56), channel_id=1, source_target_pairs={{0,4},{1,5},{2,6},{3,7},{4,0},{5,1},{6,2},{7,3},{8,12},{9,13},{10,... | collective-permute-start | bytes 491528 | tf_op jit(solution)/shard_map/ppermute | solution.py:1002
  25.2 28.8 %collective-permute-start.4 = (bf16[320,256]{1,0:T(8,128)(2,1)}, bf16[320,256]{1,0:T(8,128)(2,1)S(1)}, u32[]{:S(2)}, u32[]{:S(2)}) collective-permute-start(bf16[320,256]{1,0:T(8,128)(2,1)} %copy-done.55), channel_id=1, source_target_pairs={{0,5},{1,4},{2,7},{3,6},{4,1},{5,0},{6,3},{7,2},{8,13},{9,12},{10,... | collective-permute-start | bytes 491528 | tf_op jit(solution)/shard_map/ppermute | solution.py:1002
  30.1 32.5 %collective-permute-start.24 = (bf16[512,256]{1,0:T(8,128)(2,1)S(1)}, bf16[512,256]{1,0:T(8,128)(2,1)S(1)}, u32[]{:S(2)}, u32[]{:S(2)}) collective-permute-start(bf16[512,256]{1,0:T(8,128)(2,1)S(1)} %get-tuple-element.204), channel_id=1, source_target_pairs={{0,2},{1,5},{2,0},{3,3},{4,6},{5,1},{6,4},{7,7},{8,10},{9,13},{10,... | collective-permute-start | bytes 786440 | tf_op jit(solution)/shard_map/ppermute | solution.py:1215
  37.1 17.6 %collective-permute-start.5 = (bf16[320,256]{1,0:T(8,128)(2,1)}, bf16[320,256]{1,0:T(8,128)(2,1)S(1)}, u32[]{:S(2)}, u32[]{:S(2)}) collective-permute-start(bf16[320,256]{1,0:T(8,128)(2,1)} %copy-done.54), channel_id=1, source_target_pairs={{0,6},{1,7},{2,0},{3,1},{4,2},{5,3},{6,4},{7,5},{8,14},{9,15},{10,... | collective-permute-start | bytes 491528 | tf_op jit(solution)/shard_map/ppermute | solution.py:1002
  38.8 18.2 %collective-permute-start.6 = (bf16[320,256]{1,0:T(8,128)(2,1)S(1)}, bf16[320,256]{1,0:T(8,128)(2,1)S(1)}, u32[]{:S(2)}, u32[]{:S(2)}) collective-permute-start(bf16[320,256]{1,0:T(8,128)(2,1)S(1)} %get-tuple-element.117), channel_id=1, source_target_pairs={{0,7},{1,6},{2,1},{3,0},{4,3},{5,2},{6,5},{7,4},{8,15},{9,14},{10,... | collective-permute-start | bytes 491528 | tf_op jit(solution)/shard_map/ppermute | solution.py:1002
  55.4 11.2 %collective-permute-start.22 = (bf16[512,256]{1,0:T(8,128)(2,1)S(1)}, bf16[512,256]{1,0:T(8,128)(2,1)S(1)}, u32[]{:S(2)}, u32[]{:S(2)}) collective-permute-start(bf16[512,256]{1,0:T(8,128)(2,1)S(1)} %get-tuple-element.206), channel_id=1, source_target_pairs={{0,0},{1,3},{2,6},{3,1},{4,4},{5,7},{6,2},{7,5},{8,8},{9,11},{10,1... | collective-permute-start | bytes 786440 | tf_op jit(solution)/shard_map/ppermute | solution.py:1215
  57.7 29.0 %collective-permute-start.35 = (bf16[128,2048]{1,0:T(8,128)(2,1)S(1)}, bf16[128,2048]{1,0:T(8,128)(2,1)}, u32[]{:S(2)}, u32[]{:S(2)}) collective-permute-start(bf16[128,2048]{1,0:T(8,128)(2,1)S(1)} %bitcast.69), channel_id=1, source_target_pairs={{0,6},{2,0},{4,2},{6,4},{1,7},{3,1},{5,3},{7,5},{8,14},{10,8},{12,... | collective-permute-start | bytes 1572872 | tf_op jit(solution)/shard_map/ppermute | solution.py:349
  62.6 31.5 %collective-permute-start.33 = (bf16[128,2048]{1,0:T(8,128)(2,1)S(1)}, bf16[128,2048]{1,0:T(8,128)(2,1)}, u32[]{:S(2)}, u32[]{:S(2)}) collective-permute-start(bf16[128,2048]{1,0:T(8,128)(2,1)S(1)} %bitcast.70), channel_id=1, source_target_pairs={{0,2},{2,4},{4,6},{6,0},{1,3},{3,5},{5,7},{7,1},{8,10},{10,12},{12... | collective-permute-start | bytes 1572872 | tf_op jit(solution)/shard_map/ppermute | solution.py:349
  65.7 31.9 %collective-permute-start.14 = (bf16[128,2048]{1,0:T(8,128)(2,1)S(1)}, bf16[128,2048]{1,0:T(8,128)(2,1)S(1)}, u32[]{:S(2)}, u32[]{:S(2)}) collective-permute-start(bf16[128,2048]{1,0:T(8,128)(2,1)S(1)} %bitcast.63), channel_id=1, source_target_pairs={{0,6},{2,0},{4,2},{6,4},{1,7},{3,1},{5,3},{7,5},{8,14},{10,8},{12,... | collective-permute-start | bytes 1572872 | tf_op jit(solution)/shard_map/ppermute | solution.py:349
  67.2 45.9 %collective-permute-start.11 = (bf16[128,2048]{1,0:T(8,128)(2,1)S(1)}, bf16[128,2048]{1,0:T(8,128)(2,1)S(1)}, u32[]{:S(2)}, u32[]{:S(2)}) collective-permute-start(bf16[128,2048]{1,0:T(8,128)(2,1)S(1)} %bitcast.64), channel_id=1, source_target_pairs={{0,2},{2,4},{4,6},{6,0},{1,3},{3,5},{5,7},{7,1},{8,10},{10,12},{12... | collective-permute-start | bytes 1572872 | tf_op jit(solution)/shard_map/ppermute | solution.py:349
  86.5 27.9 %collective-permute-start.10 = (bf16[128,2048]{1,0:T(8,128)(2,1)S(1)}, bf16[128,2048]{1,0:T(8,128)(2,1)}, u32[]{:S(2)}, u32[]{:S(2)}) collective-permute-start(bf16[128,2048]{1,0:T(8,128)(2,1)S(1)} %bitcast.65), channel_id=1, source_target_pairs={{0,1},{1,0},{2,3},{3,2},{4,5},{5,4},{6,7},{7,6},{8,9},{9,8},{10,11... | collective-permute-start | bytes 1572872 | tf_op jit(solution)/shard_map/ppermute | solution.py:349
  86.7 38.3 %collective-permute-start.36 = (bf16[128,2048]{1,0:T(8,128)(2,1)}, bf16[128,2048]{1,0:T(8,128)(2,1)}, u32[]{:S(2)}, u32[]{:S(2)}) collective-permute-start(bf16[128,2048]{1,0:T(8,128)(2,1)} %collective-permute-done.35.refs_3_), channel_id=1, source_target_pairs={{4,2},{2,0},{5,3},{3,1},{12,10},{10,8},{13,11},{11,9},{20,18},{18,... | collective-permute-start | bytes 1572872 | tf_op jit(solution)/shard_map/ppermute | solution.py:357
  94.1 32.3 %collective-permute-start.34 = (bf16[128,2048]{1,0:T(8,128)(2,1)}, bf16[128,2048]{1,0:T(8,128)(2,1)}, u32[]{:S(2)}, u32[]{:S(2)}) collective-permute-start(bf16[128,2048]{1,0:T(8,128)(2,1)} %collective-permute-done.33.refs_1_), channel_id=1, source_target_pairs={{2,4},{4,6},{3,5},{5,7},{10,12},{12,14},{11,13},{13,15},{18,20},{2... | collective-permute-start | bytes 1572872 | tf_op jit(solution)/shard_map/ppermute | solution.py:356
  97.6 36.5 %collective-permute-start.26 = (bf16[512,768]{1,0:T(8,128)(2,1)S(1)}, bf16[512,768]{1,0:T(8,128)(2,1)}, u32[]{:S(2)}, u32[]{:S(2)}) collective-permute-start(bf16[512,768]{1,0:T(8,128)(2,1)S(1)} %shard_map.259.refs_0_), channel_id=1, source_target_pairs={{0,16},{16,0},{1,17},{17,1},{2,18},{18,2},{3,19},{19,3},{4,20},{20... | collective-permute-start | bytes 2359304 | tf_op jit(solution)/shard_map/ppermute | solution.py:349
  113.2 16.3 %collective-permute-start.15 = (bf16[128,2048]{1,0:T(8,128)(2,1)S(1)}, bf16[128,2048]{1,0:T(8,128)(2,1)}, u32[]{:S(2)}, u32[]{:S(2)}) collective-permute-start(bf16[128,2048]{1,0:T(8,128)(2,1)S(1)} %collective-permute-done.14.refs_3_), channel_id=1, source_target_pairs={{4,2},{2,0},{5,3},{3,1},{12,10},{10,8},{13,11},{11,9},{20,18},{18,... | collective-permute-start | bytes 1572872 | tf_op jit(solution)/shard_map/ppermute | solution.py:357
  114.5 15.1 %collective-permute-start.13 = (bf16[128,2048]{1,0:T(8,128)(2,1)S(1)}, bf16[128,2048]{1,0:T(8,128)(2,1)}, u32[]{:S(2)}, u32[]{:S(2)}) collective-permute-start(bf16[128,2048]{1,0:T(8,128)(2,1)S(1)} %collective-permute-done.11.refs_1_), channel_id=1, source_target_pairs={{2,4},{4,6},{3,5},{5,7},{10,12},{12,14},{11,13},{13,15},{18,20},{2... | collective-permute-start | bytes 1572872 | tf_op jit(solution)/shard_map/ppermute | solution.py:356
  125.0 27.6 %collective-permute-start.8 = (bf16[8,320,256]{2,1,0:T(8,128)(2,1)}, bf16[8,320,256]{2,1,0:T(8,128)(2,1)}, u32[]{:S(2)}, u32[]{:S(2)}) collective-permute-start(bf16[8,320,256]{2,1,0:T(8,128)(2,1)} %shard_map.255.p0), channel_id=1, source_target_pairs={{0,16},{16,0},{1,17},{17,1},{2,18},{18,2},{3,19},{19,3},{4,20},{20... | collective-permute-start | bytes 3932168 | tf_op jit(solution)/shard_map/ppermute | solution.py:349
  126.5 11.4 %collective-permute-start.17 = (bf16[128,2048]{1,0:T(8,128)(2,1)S(1)}, bf16[128,2048]{1,0:T(8,128)(2,1)}, u32[]{:S(2)}, u32[]{:S(2)}) collective-permute-start(bf16[128,2048]{1,0:T(8,128)(2,1)S(1)} %collective-permute-done.14.refs_3_), channel_id=1, source_target_pairs={{0,1},{1,0},{2,3},{3,2},{4,5},{5,4},{6,7},{7,6},{8,9},{9,8},{10,11... | collective-permute-start | bytes 1572872 | tf_op jit(solution)/shard_map/ppermute | solution.py:349
  129.5 19.6 %collective-permute-start.25 = (bf16[512,768]{1,0:T(8,128)(2,1)S(1)}, bf16[512,768]{1,0:T(8,128)(2,1)S(1)}, u32[]{:S(2)}, u32[]{:S(2)}) collective-permute-start(bf16[512,768]{1,0:T(8,128)(2,1)S(1)} %shard_map.259.refs_0_), channel_id=1, source_target_pairs={{0,8},{8,0},{1,9},{9,1},{2,10},{10,2},{3,11},{11,3},{4,12},{12,4},... | collective-permute-start | bytes 2359304 | tf_op jit(solution)/shard_map/ppermute | solution.py:349
  129.5 19.5 %collective-permute-start.12 = (bf16[128,2048]{1,0:T(8,128)(2,1)S(1)}, bf16[128,2048]{1,0:T(8,128)(2,1)S(1)}, u32[]{:S(2)}, u32[]{:S(2)}) collective-permute-start(bf16[128,2048]{1,0:T(8,128)(2,1)S(1)} %collective-permute-done.11.refs_1_), channel_id=1, source_target_pairs={{0,1},{1,0},{2,3},{3,2},{4,5},{5,4},{6,7},{7,6},{8,9},{9,8},{10,11... | collective-permute-start | bytes 1572872 | tf_op jit(solution)/shard_map/ppermute | solution.py:349
  134.1 26.1 %collective-permute-start.27 = (bf16[512,768]{1,0:T(8,128)(2,1)}, bf16[512,768]{1,0:T(8,128)(2,1)S(1)}, u32[]{:S(2)}, u32[]{:S(2)}) collective-permute-start(bf16[512,768]{1,0:T(8,128)(2,1)} %collective-permute-done.26.refs_2_), channel_id=1, source_target_pairs={{0,8},{8,0},{1,9},{9,1},{2,10},{10,2},{3,11},{11,3},{4,12},{12,4},... | collective-permute-start | bytes 2359304 | tf_op jit(solution)/shard_map/ppermute | solution.py:349
  137.9 22.4 %collective-permute-start.16 = (bf16[128,2048]{1,0:T(8,128)(2,1)S(1)}, bf16[128,2048]{1,0:T(8,128)(2,1)S(1)}, u32[]{:S(2)}, u32[]{:S(2)}) collective-permute-start(bf16[128,2048]{1,0:T(8,128)(2,1)S(1)} %broadcast_select_fusion.1.refs_2_), channel_id=1, source_target_pairs={{0,1},{1,0},{2,3},{3,2},{4,5},{5,4},{6,7},{7,6},{8,9},{9,8},{10,11... | collective-permute-start | bytes 1572872 | tf_op jit(solution)/shard_map/ppermute | solution.py:349
  149.0 41.4 %collective-permute-start.40 = (bf16[128,2048]{1,0:T(8,128)(2,1)}, bf16[128,2048]{1,0:T(8,128)(2,1)S(1)}, u32[]{:S(2)}, u32[]{:S(2)}) collective-permute-start(bf16[128,2048]{1,0:T(8,128)(2,1)} %collective-permute-done.35.refs_3_), channel_id=1, source_target_pairs={{0,1},{1,0},{2,3},{3,2},{4,5},{5,4},{6,7},{7,6},{8,9},{9,8},{10,11... | collective-permute-start | bytes 1572872 | tf_op jit(solution)/shard_map/ppermute | solution.py:349
  149.0 41.4 %collective-permute-start.38 = (bf16[128,2048]{1,0:T(8,128)(2,1)}, bf16[128,2048]{1,0:T(8,128)(2,1)S(1)}, u32[]{:S(2)}, u32[]{:S(2)}) collective-permute-start(bf16[128,2048]{1,0:T(8,128)(2,1)} %collective-permute-done.33.refs_1_), channel_id=1, source_target_pairs={{0,1},{1,0},{2,3},{3,2},{4,5},{5,4},{6,7},{7,6},{8,9},{9,8},{10,11... | collective-permute-start | bytes 1572872 | tf_op jit(solution)/shard_map/ppermute | solution.py:349
  152.6 40.2 %collective-permute-start.39 = (bf16[128,2048]{1,0:T(8,128)(2,1)S(1)}, bf16[128,2048]{1,0:T(8,128)(2,1)S(1)}, u32[]{:S(2)}, u32[]{:S(2)}) collective-permute-start(bf16[128,2048]{1,0:T(8,128)(2,1)S(1)} %broadcast_select_fusion.refs_2_), channel_id=1, source_target_pairs={{0,1},{1,0},{2,3},{3,2},{4,5},{5,4},{6,7},{7,6},{8,9},{9,8},{10,11... | collective-permute-start | bytes 1572872 | tf_op jit(solution)/shard_map/ppermute | solution.py:349
  160.2 41.3 %collective-permute-start.7 = (bf16[8,320,256]{2,1,0:T(8,128)(2,1)}, bf16[8,320,256]{2,1,0:T(8,128)(2,1)S(1)}, u32[]{:S(2)}, u32[]{:S(2)}) collective-permute-start(bf16[8,320,256]{2,1,0:T(8,128)(2,1)} %shard_map.255.p0), channel_id=1, source_target_pairs={{0,8},{8,0},{1,9},{9,1},{2,10},{10,2},{3,11},{11,3},{4,12},{12,4},... | collective-permute-start | bytes 3932168 | tf_op jit(solution)/shard_map/ppermute | solution.py:349
  160.3 41.3 %collective-permute-start.9 = (bf16[8,320,256]{2,1,0:T(8,128)(2,1)}, bf16[8,320,256]{2,1,0:T(8,128)(2,1)S(1)}, u32[]{:S(2)}, u32[]{:S(2)}) collective-permute-start(bf16[8,320,256]{2,1,0:T(8,128)(2,1)} %collective-permute-done.8.p2), channel_id=1, source_target_pairs={{0,8},{8,0},{1,9},{9,1},{2,10},{10,2},{3,11},{11,3},{4,12},{12,4},... | collective-permute-start | bytes 3932168 | tf_op jit(solution)/shard_map/ppermute | solution.py:349
  201.6 92.1 %collective-permute-start.60 = (bf16[2,320,2048]{2,1,0:T(8,128)(2,1)}, bf16[2,320,2048]{2,1,0:T(8,128)(2,1)}, u32[]{:S(2)}, u32[]{:S(2)}) collective-permute-start(bf16[2,320,2048]{2,1,0:T(8,128)(2,1)} %get-tuple-element.184), channel_id=1, source_target_pairs={{0,8},{8,0},{1,9},{9,1},{2,10},{10,2},{3,11},{11,3},{4,12},{12,4},... | collective-permute-start | bytes 7864328 | tf_op jit(solution)/shard_map/ppermute | solution.py:349
  228.8 61.6 %collective-permute-start.52 = (bf16[2,512,768]{2,1,0:T(8,128)(2,1)}, bf16[2,512,768]{2,1,0:T(8,128)(2,1)S(1)}, u32[]{:S(2)}, u32[]{:S(2)}) collective-permute-start(bf16[2,512,768]{2,1,0:T(8,128)(2,1)} %shard_map.275), channel_id=1, source_target_pairs={{0,8},{8,0},{1,9},{9,1},{2,10},{10,2},{3,11},{11,3},{4,12},{12,4},... | collective-permute-start | bytes 4718600 | tf_op jit(solution)/shard_map/ppermute | solution.py:349
  233.6 73.3 %collective-permute-start.72 = (bf16[1024,1024]{1,0:T(8,128)(2,1)}, bf16[1024,1024]{1,0:T(8,128)(2,1)}, u32[]{:S(2)}, u32[]{:S(2)}) collective-permute-start(bf16[1024,1024]{1,0:T(8,128)(2,1)} %shard_map.284), channel_id=1, source_target_pairs={{0,8},{8,0},{1,9},{9,1},{2,10},{10,2},{3,11},{11,3},{4,12},{12,4},... | collective-permute-start | bytes 6291464 | tf_op jit(solution)/shard_map/ppermute | solution.py:349
  233.7 79.6 %collective-permute-start.28 = (bf16[512,2048]{1,0:T(8,128)(2,1)}, bf16[512,2048]{1,0:T(8,128)(2,1)S(1)}, u32[]{:S(2)}, u32[]{:S(2)}) collective-permute-start(bf16[512,2048]{1,0:T(8,128)(2,1)} %get-tuple-element.138), channel_id=1, source_target_pairs={{0,1},{1,0},{2,3},{3,2},{4,5},{5,4},{6,7},{7,6},{8,9},{9,8},{10,11... | collective-permute-start | bytes 6291464 | tf_op jit(solution)/shard_map/ppermute | solution.py:349
  248.2 34.7 %collective-permute-start.46 = (f32[4,3072]{1,0:T(4,128)S(1)}, f32[4,3072]{1,0:T(4,128)S(1)}, u32[]{:S(2)}, u32[]{:S(2)}) collective-permute-start(f32[4,3072]{1,0:T(4,128)S(1)} %get-tuple-element.174), channel_id=1, source_target_pairs={{0,1},{1,0},{2,3},{3,2},{4,5},{5,4},{6,7},{7,6},{8,9},{9,8},{10,11... | collective-permute-start | bytes 147464 | tf_op jit(solution)/shard_map/ppermute | solution.py:349
  290.1 108.0 %collective-permute-start.41 = (bf16[512,2048]{1,0:T(8,128)(2,1)}, bf16[512,2048]{1,0:T(8,128)(2,1)S(1)}, u32[]{:S(2)}, u32[]{:S(2)}) collective-permute-start(bf16[512,2048]{1,0:T(8,128)(2,1)} %get-tuple-element.160), channel_id=1, source_target_pairs={{0,1},{1,0},{2,3},{3,2},{4,5},{5,4},{6,7},{7,6},{8,9},{9,8},{10,11... | collective-permute-start | bytes 6291464 | tf_op jit(solution)/shard_map/ppermute | solution.py:349
  290.4 14.4 %collective-permute-start.48 = (f32[1,3072]{1,0:T(1,128)S(1)}, f32[1,3072]{1,0:T(1,128)S(1)}, u32[]{:S(2)}, u32[]{:S(2)}) collective-permute-start(f32[1,3072]{1,0:T(1,128)S(1)} %get-tuple-element.177), channel_id=1, source_target_pairs={{0,4},{2,6},{4,0},{6,2},{1,5},{3,7},{5,1},{7,3},{8,12},{10,14},{12... | collective-permute-start | bytes 36872 | tf_op jit(solution)/shard_map/ppermute | solution.py:349
  293.7 12.7 %collective-permute-start.49 = (f32[1,3072]{1,0:T(1,128)S(1)}, f32[1,3072]{1,0:T(1,128)S(1)}, u32[]{:S(2)}, u32[]{:S(2)}) collective-permute-start(f32[1,3072]{1,0:T(1,128)S(1)} %get-tuple-element.178), channel_id=1, source_target_pairs={{0,6},{2,0},{4,2},{6,4},{1,7},{3,1},{5,3},{7,5},{8,14},{10,8},{12,... | collective-permute-start | bytes 36872 | tf_op jit(solution)/shard_map/ppermute | solution.py:349
  304.8 94.3 %collective-permute-start.53 = (bf16[512,768]{1,0:T(8,128)(2,1)S(1)}, bf16[512,768]{1,0:T(8,128)(2,1)S(1)}, u32[]{:S(2)}, u32[]{:S(2)}) collective-permute-start(bf16[512,768]{1,0:T(8,128)(2,1)S(1)} %get-tuple-element.180), channel_id=1, source_target_pairs={{0,16},{16,0},{1,17},{17,1},{2,18},{18,2},{3,19},{19,3},{4,20},{20... | collective-permute-start | bytes 2359304 | tf_op jit(solution)/shard_map/ppermute | solution.py:349
  306.3 105.6 %collective-permute-start.61 = (bf16[320,2048]{1,0:T(8,128)(2,1)S(1)}, bf16[320,2048]{1,0:T(8,128)(2,1)S(1)}, u32[]{:S(2)}, u32[]{:S(2)}) collective-permute-start(bf16[320,2048]{1,0:T(8,128)(2,1)S(1)} %get-tuple-element.187), channel_id=1, source_target_pairs={{0,16},{16,0},{1,17},{17,1},{2,18},{18,2},{3,19},{19,3},{4,20},{20... | collective-permute-start | bytes 3932168 | tf_op jit(solution)/shard_map/ppermute | solution.py:349
  311.7 198.3 %collective-permute-start.73 = (bf16[1024,1024]{1,0:T(8,128)(2,1)S(1)}, bf16[1024,1024]{1,0:T(8,128)(2,1)S(1)}, u32[]{:S(2)}, u32[]{:S(2)}) collective-permute-start(bf16[1024,1024]{1,0:T(8,128)(2,1)S(1)} %shard_map.285.a), channel_id=1, source_target_pairs={{0,16},{16,0},{1,17},{17,1},{2,18},{18,2},{3,19},{19,3},{4,20},{20... | collective-permute-start | bytes 6291464 | tf_op jit(solution)/shard_map/ppermute | solution.py:349
  313.3 82.1 %collective-permute-start.51 = (f32[1,3072]{1,0:T(1,128)S(1)}, f32[1,3072]{1,0:T(1,128)S(1)}, u32[]{:S(2)}, u32[]{:S(2)}) collective-permute-start(f32[1,3072]{1,0:T(1,128)S(1)} %add.189), channel_id=1, source_target_pairs={{0,16},{16,0},{1,17},{17,1},{2,18},{18,2},{3,19},{19,3},{4,20},{20... | collective-permute-start | bytes 36872 | tf_op jit(solution)/shard_map/ppermute | solution.py:349
  395.3 15.0 %collective-permute-start.30 = (bf16[128,2048]{1,0:T(8,128)(2,1)S(1)}, bf16[128,2048]{1,0:T(8,128)(2,1)S(1)}, u32[]{:S(2)}, u32[]{:S(2)}) collective-permute-start(bf16[128,2048]{1,0:T(8,128)(2,1)S(1)} %get-tuple-element.140), channel_id=1, source_target_pairs={{0,2},{2,4},{1,3},{3,5},{8,10},{10,12},{9,11},{11,13},{16,18},{18,... | collective-permute-start | bytes 1572872 | tf_op jit(solution)/shard_map/ppermute | solution.py:1245
  398.1 13.1 %collective-permute-start.29 = (bf16[128,2048]{1,0:T(8,128)(2,1)S(1)}, bf16[128,2048]{1,0:T(8,128)(2,1)S(1)}, u32[]{:S(2)}, u32[]{:S(2)}) collective-permute-start(bf16[128,2048]{1,0:T(8,128)(2,1)S(1)} %get-tuple-element.140), channel_id=1, source_target_pairs={{4,2},{6,4},{5,3},{7,5},{12,10},{14,12},{13,11},{15,13},{20,18},{2... | collective-permute-start | bytes 1572872 | tf_op jit(solution)/shard_map/ppermute | solution.py:1246
  399.1 34.3 %collective-permute-start.43 = (bf16[128,2048]{1,0:T(8,128)(2,1)S(1)}, bf16[128,2048]{1,0:T(8,128)(2,1)S(1)}, u32[]{:S(2)}, u32[]{:S(2)}) collective-permute-start(bf16[128,2048]{1,0:T(8,128)(2,1)S(1)} %get-tuple-element.162), channel_id=1, source_target_pairs={{0,2},{2,4},{1,3},{3,5},{8,10},{10,12},{9,11},{11,13},{16,18},{18,... | collective-permute-start | bytes 1572872 | tf_op jit(solution)/shard_map/ppermute | solution.py:1245
  410.4 23.0 %collective-permute-start.42 = (bf16[128,2048]{1,0:T(8,128)(2,1)S(1)}, bf16[128,2048]{1,0:T(8,128)(2,1)S(1)}, u32[]{:S(2)}, u32[]{:S(2)}) collective-permute-start(bf16[128,2048]{1,0:T(8,128)(2,1)S(1)} %get-tuple-element.162), channel_id=1, source_target_pairs={{4,2},{6,4},{5,3},{7,5},{12,10},{14,12},{13,11},{15,13},{20,18},{2... | collective-permute-start | bytes 1572872 | tf_op jit(solution)/shard_map/ppermute | solution.py:1246
  412.0 12.6 %collective-permute-start.55 = (bf16[512,256]{1,0:T(8,128)(2,1)S(1)}, bf16[512,256]{1,0:T(8,128)(2,1)S(1)}, u32[]{:S(2)}, u32[]{:S(2)}) collective-permute-start(bf16[512,256]{1,0:T(8,128)(2,1)S(1)} %get-tuple-element.182), channel_id=1, source_target_pairs={{1,0},{4,1},{7,2},{2,3},{5,4},{0,5},{3,6},{6,7},{9,8},{12,9},{15,1... | collective-permute-start | bytes 786440 | tf_op jit(solution)/shard_map/ppermute | solution.py:1302
  420.6 27.6 %collective-permute-start.62 = (bf16[320,256]{1,0:T(8,128)(2,1)S(1)}, bf16[320,256]{1,0:T(8,128)(2,1)S(1)}, u32[]{:S(2)}, u32[]{:S(2)}) collective-permute-start(bf16[320,256]{1,0:T(8,128)(2,1)S(1)} %get-tuple-element.189), channel_id=1, source_target_pairs={{0,1},{1,0},{2,3},{3,2},{4,5},{5,4},{6,7},{7,6},{8,9},{9,8},{10,11... | collective-permute-start | bytes 491528 | tf_op jit(solution)/shard_map/ppermute | solution.py:1002
  424.5 25.5 %collective-permute-start.63 = (bf16[320,256]{1,0:T(8,128)(2,1)S(1)}, bf16[320,256]{1,0:T(8,128)(2,1)S(1)}, u32[]{:S(2)}, u32[]{:S(2)}) collective-permute-start(bf16[320,256]{1,0:T(8,128)(2,1)S(1)} %get-tuple-element.190), channel_id=1, source_target_pairs={{0,2},{1,3},{2,4},{3,5},{4,6},{5,7},{6,0},{7,1},{8,10},{9,11},{10,... | collective-permute-start | bytes 491528 | tf_op jit(solution)/shard_map/ppermute | solution.py:1002
  433.4 21.8 %collective-permute-start.64 = (bf16[320,256]{1,0:T(8,128)(2,1)S(1)}, bf16[320,256]{1,0:T(8,128)(2,1)S(1)}, u32[]{:S(2)}, u32[]{:S(2)}) collective-permute-start(bf16[320,256]{1,0:T(8,128)(2,1)S(1)} %get-tuple-element.191), channel_id=1, source_target_pairs={{0,3},{1,2},{2,5},{3,4},{4,7},{5,6},{6,1},{7,0},{8,11},{9,10},{10,... | collective-permute-start | bytes 491528 | tf_op jit(solution)/shard_map/ppermute | solution.py:1002
  433.4 22.8 %collective-permute-start.65 = (bf16[320,256]{1,0:T(8,128)(2,1)S(1)}, bf16[320,256]{1,0:T(8,128)(2,1)S(1)}, u32[]{:S(2)}, u32[]{:S(2)}) collective-permute-start(bf16[320,256]{1,0:T(8,128)(2,1)S(1)} %get-tuple-element.192), channel_id=1, source_target_pairs={{0,4},{1,5},{2,6},{3,7},{4,0},{5,1},{6,2},{7,3},{8,12},{9,13},{10,... | collective-permute-start | bytes 491528 | tf_op jit(solution)/shard_map/ppermute | solution.py:1002
  448.1 42.5 %collective-permute-start.56 = (bf16[512,256]{1,0:T(8,128)(2,1)S(1)}, bf16[512,256]{1,0:T(8,128)(2,1)S(1)}, u32[]{:S(2)}, u32[]{:S(2)}) collective-permute-start(bf16[512,256]{1,0:T(8,128)(2,1)S(1)} %get-tuple-element.183), channel_id=1, source_target_pairs={{2,0},{5,1},{0,2},{3,3},{6,4},{1,5},{4,6},{7,7},{10,8},{13,9},{8,1... | collective-permute-start | bytes 786440 | tf_op jit(solution)/shard_map/ppermute | solution.py:1302
  450.1 23.5 %collective-permute-start.66 = (bf16[320,256]{1,0:T(8,128)(2,1)S(1)}, bf16[320,256]{1,0:T(8,128)(2,1)S(1)}, u32[]{:S(2)}, u32[]{:S(2)}) collective-permute-start(bf16[320,256]{1,0:T(8,128)(2,1)S(1)} %get-tuple-element.193), channel_id=1, source_target_pairs={{0,5},{1,4},{2,7},{3,6},{4,1},{5,0},{6,3},{7,2},{8,13},{9,12},{10,... | collective-permute-start | bytes 491528 | tf_op jit(solution)/shard_map/ppermute | solution.py:1002
  455.2 31.0 %collective-permute-start.67 = (bf16[320,256]{1,0:T(8,128)(2,1)S(1)}, bf16[320,256]{1,0:T(8,128)(2,1)S(1)}, u32[]{:S(2)}, u32[]{:S(2)}) collective-permute-start(bf16[320,256]{1,0:T(8,128)(2,1)S(1)} %get-tuple-element.194), channel_id=1, source_target_pairs={{0,6},{1,7},{2,0},{3,1},{4,2},{5,3},{6,4},{7,5},{8,14},{9,15},{10,... | collective-permute-start | bytes 491528 | tf_op jit(solution)/shard_map/ppermute | solution.py:1002
  456.2 30.0 %collective-permute-start.68 = (bf16[320,256]{1,0:T(8,128)(2,1)S(1)}, bf16[320,256]{1,0:T(8,128)(2,1)S(1)}, u32[]{:S(2)}, u32[]{:S(2)}) collective-permute-start(bf16[320,256]{1,0:T(8,128)(2,1)S(1)} %get-tuple-element.195), channel_id=1, source_target_pairs={{0,7},{1,6},{2,1},{3,0},{4,3},{5,2},{6,5},{7,4},{8,15},{9,14},{10,... | collective-permute-start | bytes 491528 | tf_op jit(solution)/shard_map/ppermute | solution.py:1002
  473.6 19.3 %collective-permute-start.31 = (bf16[128,2048]{1,0:T(8,128)(2,1)S(1)}, bf16[128,2048]{1,0:T(8,128)(2,1)S(1)}, u32[]{:S(2)}, u32[]{:S(2)}) collective-permute-start(bf16[128,2048]{1,0:T(8,128)(2,1)S(1)} %get-tuple-element.141), channel_id=1, source_target_pairs={{0,6},{2,0},{4,2},{6,4},{1,7},{3,1},{5,3},{7,5},{8,14},{10,8},{12,... | collective-permute-start | bytes 1572872 | tf_op jit(solution)/shard_map/ppermute | solution.py:349
  486.2 16.7 %collective-permute-start.32 = (bf16[128,2048]{1,0:T(8,128)(2,1)S(1)}, bf16[128,2048]{1,0:T(8,128)(2,1)S(1)}, u32[]{:S(2)}, u32[]{:S(2)}) collective-permute-start(bf16[128,2048]{1,0:T(8,128)(2,1)S(1)} %get-tuple-element.142), channel_id=1, source_target_pairs={{0,2},{2,4},{4,6},{6,0},{1,3},{3,5},{5,7},{7,1},{8,10},{10,12},{12... | collective-permute-start | bytes 1572872 | tf_op jit(solution)/shard_map/ppermute | solution.py:349
  486.2 23.5 %collective-permute-start.44 = (bf16[128,2048]{1,0:T(8,128)(2,1)S(1)}, bf16[128,2048]{1,0:T(8,128)(2,1)S(1)}, u32[]{:S(2)}, u32[]{:S(2)}) collective-permute-start(bf16[128,2048]{1,0:T(8,128)(2,1)S(1)} %get-tuple-element.163), channel_id=1, source_target_pairs={{0,6},{2,0},{4,2},{6,4},{1,7},{3,1},{5,3},{7,5},{8,14},{10,8},{12,... | collective-permute-start | bytes 1572872 | tf_op jit(solution)/shard_map/ppermute | solution.py:349
  490.7 34.5 %collective-permute-start.70 = (bf16[8,320,256]{2,1,0:T(8,128)(2,1)S(1)}, bf16[8,320,256]{2,1,0:T(8,128)(2,1)S(1)}, u32[]{:S(2)}, u32[]{:S(2)}) collective-permute-start(bf16[8,320,256]{2,1,0:T(8,128)(2,1)S(1)} %shard_map.282.p0), channel_id=1, source_target_pairs={{0,16},{16,0},{1,17},{17,1},{2,18},{18,2},{3,19},{19,3},{4,20},{20... | collective-permute-start | bytes 3932168 | tf_op jit(solution)/shard_map/ppermute | solution.py:349
  492.9 46.7 %collective-permute-start.74 = (bf16[1024,1024]{1,0:T(8,128)(2,1)S(1)}, bf16[1024,1024]{1,0:T(8,128)(2,1)S(1)}, u32[]{:S(2)}, u32[]{:S(2)}) collective-permute-start(bf16[1024,1024]{1,0:T(8,128)(2,1)S(1)} %shard_map.285.a), channel_id=1, source_target_pairs={{0,8},{8,0},{1,9},{9,1},{2,10},{10,2},{3,11},{11,3},{4,12},{12,4},... | collective-permute-start | bytes 6291464 | tf_op jit(solution)/shard_map/ppermute | solution.py:349
  502.9 22.3 %collective-permute-start.58 = (bf16[512,768]{1,0:T(8,128)(2,1)S(1)}, bf16[512,768]{1,0:T(8,128)(2,1)S(1)}, u32[]{:S(2)}, u32[]{:S(2)}) collective-permute-start(bf16[512,768]{1,0:T(8,128)(2,1)S(1)} %shard_map.278.p0), channel_id=1, source_target_pairs={{0,16},{16,0},{1,17},{17,1},{2,18},{18,2},{3,19},{19,3},{4,20},{20... | collective-permute-start | bytes 2359304 | tf_op jit(solution)/shard_map/ppermute | solution.py:349
  509.7 11.7 %collective-permute-start.45 = (bf16[128,2048]{1,0:T(8,128)(2,1)S(1)}, bf16[128,2048]{1,0:T(8,128)(2,1)S(1)}, u32[]{:S(2)}, u32[]{:S(2)}) collective-permute-start(bf16[128,2048]{1,0:T(8,128)(2,1)S(1)} %get-tuple-element.164), channel_id=1, source_target_pairs={{0,2},{2,4},{4,6},{6,0},{1,3},{3,5},{5,7},{7,1},{8,10},{10,12},{12... | collective-permute-start | bytes 1572872 | tf_op jit(solution)/shard_map/ppermute | solution.py:349
  510.0 29.6 %collective-permute-start.75 = (bf16[1024,1024]{1,0:T(8,128)(2,1)S(1)}, bf16[1024,1024]{1,0:T(8,128)(2,1)S(1)}, u32[]{:S(2)}, u32[]{:S(2)}) collective-permute-start(bf16[1024,1024]{1,0:T(8,128)(2,1)S(1)} %collective-permute-done.73.b), channel_id=1, source_target_pairs={{0,8},{8,0},{1,9},{9,1},{2,10},{10,2},{3,11},{11,3},{4,12},{12,4},... | collective-permute-start | bytes 6291464 | tf_op jit(solution)/shard_map/ppermute | solution.py:349
  (77 other events, 1159.1 us)

commit v3 on v2

--- a/solution.py
+++ b/solution.py
@@ -480,48 +480,69 @@
     return jnp.concatenate([first * cosine + swapped * sine, tensor[:, ROPE_LANES:]], axis=1)
 
 
-def head_attention(attn_in, weights, bias, tables, positions, meta):
+def seen_by(spot, block, rows, length):
+    ring = length // rows
+    first = (spot[4] - block + ring) % ring * rows
+    lane = lax.broadcasted_iota(jnp.int32, (1, length), 1)
+    keys = (spot[4] - lane // rows + ring) % ring * rows + lane % rows
+    return first + lax.broadcasted_iota(jnp.int32, (rows, 1), 0) >= keys
+
+
+def join_columns(pieces, meta):
+    deep, slots = pieces[0].shape[0], pieces[0].shape[1] // HEAD
+
+    def kernel(meta, p0, p1, p2, p3, w):
+        for d, p in enumerate((p0, p1, p2, p3)):
+            here = pl.ds(pl.multiple_of((meta[0] ^ d) * deep, deep), deep)
+            for s in range(slots):
+                w[meta[1 + s], here, :] = p[:, s * HEAD : (s + 1) * HEAD]
+
+    shape = (slots, 4 * deep, HEAD)
+    return call(
+        kernel,
+        (1,),
+        [whole(p.shape) for p in pieces],
+        [whole(shape)],
+        [(shape, pieces[0].dtype)],
+        scalars=(meta,),
+        args=pieces,
+    )[0]
+
+
+def head_attention(attn_in, weights, bias, tables, spot):
     f32, bf16 = jnp.float32, jnp.bfloat16
-    length, width = attn_in.shape
-    chunk, slots = length // 4, 3
-    joins = len(weights) > 1
-
-    def kernel(meta, x, *refs):
-        pieces, (b, cosine, sine, down, along) = refs[: len(weights)], refs[len(weights) :][:5]
-        qkv, att, log_total = refs[-3:]
-        w = refs[-4] if joins else pieces[0]
-        if joins:
-            deep = pieces[0].shape[0]
-            for d, p in enumerate(pieces):
-                here = pl.ds(pl.multiple_of((meta[0] ^ d) * deep, deep), deep)
-                for s in range(slots):
-                    w[meta[1 + s], here, :] = p[:, s * HEAD : (s + 1) * HEAD]
+    length = attn_in.shape[0]
+    chunk = length // 4
+
+    def kernel(spot, x, w, b, cosine, sine, qkv, att, log_total):
         for kind in range(3):
             t = mm(x[...], w[kind]) + b[kind]
             if kind < 2:
                 t = turn(t, cosine[...], sine[...])
             qkv[kind] = t.astype(bf16)
-        for c in range(4):
-            here = slice(c * chunk, (c + 1) * chunk)
-            seen = down[here, :] >= along[...]
+
+        def attend(c, _):
+            here = pl.ds(pl.multiple_of(c * chunk, chunk), chunk)
+            seen = seen_by(spot, c, chunk, length)
             scores = jnp.where(seen, mm(qkv[0, here, :], qkv[1], NT) * HEAD**-0.5, MASKED)
             top = jnp.max(scores, axis=-1, keepdims=True)
             powers = jnp.where(seen, jnp.exp(scores - top), 0.0)
             total = jnp.sum(powers, axis=-1, keepdims=True)
             att[here, :] = (mm(powers.astype(bf16), qkv[2]) / total).astype(bf16)
             log_total[here, :] = top + jnp.log(total)
-
-    args = (attn_in, *weights, bias, *tables, *positions)
+            return 0
+
+        lax.fori_loop(0, spot[5], attend, 0)
+
+    args = (attn_in, weights, bias, *tables)
     outs = [((3, length, HEAD), bf16), ((length, HEAD), bf16), ((length, 1), f32)]
-    if joins:
-        outs = [((3, width, HEAD), bf16)] + outs
     return call(
         kernel,
         (1,),
         [whole(v.shape) for v in args],
         [whole(shape) for shape, _ in outs],
         outs,
-        scalars=(meta,),
+        scalars=(spot,),
         args=args,
     )
 
@@ -541,10 +562,14 @@
             for m in range(members):
                 w[upper, m * cols : (m + 1) * cols] = p[m, :tall, :]
                 w[lower, m * cols : (m + 1) * cols] = p[m, tall:, :]
-        for m in range(members):
-            here = slice(m * cols, (m + 1) * cols)
+
+        def columns(m, _):
+            here = pl.ds(pl.multiple_of(m * 2 * cols, 2 * cols), 2 * cols)
             part = mm(act[...], w[:units, here]) + mm(att[...], w[units:, here])
             out[:, here] = part.astype(bf16)
+            return 0
+
+        lax.fori_loop(0, members // 2, columns, 0)
 
     args = (*pieces, act, att)
     return call(
@@ -581,19 +606,22 @@
     )[0]
 
 
-def backward(cot, w, slope, att, qkv, log_total, tables, positions):
+def backward(cot, w, slope, att, qkv, log_total, tables, spot):
     f32, bf16 = jnp.float32, jnp.bfloat16
     length, units = slope.shape
     width, chunk, wide = cot.shape[1], length // 4, 256
 
-    def kernel(*refs):
-        (cot, w, slope, att, qkv, log_total, cosine, sine, down, along) = refs[:10]
-        (dpre, dqkv, sum_fc1, sum_qkv, sum_cot, datt, dk, dv) = refs[10:]
-        total = jnp.zeros((1, width), f32)
-        for c in range(4):
-            block = cot[c * chunk : (c + 1) * chunk, :].astype(f32)
-            total = total + jnp.sum(block, axis=0, keepdims=True)
-        sum_cot[...] = total
+    def kernel(spot, *refs):
+        (cot, w, slope, att, qkv, log_total, cosine, sine) = refs[:8]
+        (dpre, dqkv, sum_fc1, sum_qkv, sum_cot, datt, dk, dv) = refs[8:]
+        sum_cot[...] = jnp.zeros_like(sum_cot)
+
+        def count(c, _):
+            here = pl.ds(pl.multiple_of(c * chunk, chunk), chunk)
+            sum_cot[...] += jnp.sum(cot[here, :].astype(f32), axis=0, keepdims=True)
+            return 0
+
+        lax.fori_loop(0, spot[5], count, 0)
         datt[...] = mm(cot[...], w[units:, :], NT).astype(bf16)
         for n in range(units // wide):
             here = slice(n * wide, (n + 1) * wide)
@@ -606,7 +634,7 @@
         for c in range(4):
             here = slice(c * chunk, (c + 1) * chunk)
             queries, grad = qkv[0, here, :], datt[here, :]
-            seen = down[here, :] >= along[...]
+            seen = seen_by(spot, c, chunk, length)
             scores = mm(queries, qkv[1], NT) * HEAD**-0.5
             prob = jnp.where(seen, jnp.exp(jnp.where(seen, scores, MASKED) - log_total[here, :]), 0.0)
             dot = jnp.sum(grad.astype(f32) * att[here, :].astype(f32), axis=-1, keepdims=True)
@@ -622,7 +650,7 @@
         dqkv[1] = turned.astype(bf16)
         dqkv[2] = dv[...].astype(bf16)
 
-    args = (cot, w, slope, att, qkv, log_total, *tables, *positions)
+    args = (cot, w, slope, att, qkv, log_total, *tables)
     outs = [
         ((length, units), bf16),
         ((3, length, HEAD), bf16),
@@ -641,6 +669,7 @@
             pltpu.VMEM((length, HEAD), f32),
             pltpu.VMEM((length, HEAD), f32),
         ],
+        scalars=(spot,),
         args=args,
     )
 
@@ -1174,7 +1203,7 @@
         kind_of[block % members][block % slots] = block // HEADS
     kinds = jnp.asarray(kind_of, jnp.int32)[place]
     meta = jnp.concatenate([replica[None], kinds]).astype(jnp.int32)
-    spot = jnp.stack([x_at, core_at, place, side, ctx_at]).astype(jnp.int32)
+    spot = jnp.stack([x_at, core_at, place, side, ctx_at, jnp.int32(4)]).astype(jnp.int32)
     token_pos = (
         ((ctx_at - jnp.arange(ring)) % ring)[:, None] * row_count + jnp.arange(row_count)[None]
     ).reshape(length)
@@ -1184,12 +1213,11 @@
         jnp.pad(jnp.concatenate([cosine, cosine], axis=1), rest, constant_values=1.0),
         jnp.pad(jnp.concatenate([-sine_table, sine_table], axis=1), rest),
     )
-    positions = (token_pos[:, None], token_pos[None, :])
     b_fc1 = b_fc1.astype(f32)[None]
     twin_core, own_core = (1 - core_at)[None], core_at[None]
     vector = (ln1_gain, ln1_bias, ln2_gain, ln2_bias, b_out, b_fc2, b_qkv)
-    vector, meta, spot, tables, positions, b_fc1, twin_core, own_core = lax.optimization_barrier(
-        (vector, meta, spot, tables, positions, b_fc1, twin_core, own_core)
+    vector, meta, spot, tables, b_fc1, twin_core, own_core = lax.optimization_barrier(
+        (vector, meta, spot, tables, b_fc1, twin_core, own_core)
     )
     vector = pack_columns([v[None] for v in vector])[0]
     vectors = [vector]
@@ -1236,8 +1264,9 @@
     for i in range(2):
         normed.append(norm_fc1(rows[i], params, w_fc1, b_fc1))
     attn_in, mlp_in, centre, scale, act, slope = zip(*normed)
-    head_qkv, *first = head_attention(attn_in[0], head_columns, bias_qkv, tables, positions, meta)
-    second = head_attention(attn_in[1], [head_qkv], bias_qkv, tables, positions, meta)
+    head_qkv = join_columns(head_columns, meta)
+    first = head_attention(attn_in[0], head_qkv, bias_qkv, tables, spot)
+    second = head_attention(attn_in[1], head_qkv, bias_qkv, tables, spot)
     qkv, attended, log_total = zip(first, second)
 
     def send_places(partial, arrived):
@@ -1258,7 +1287,7 @@
     backs, inner = [None, None], [None, None]
     for i in (1, 0):
         backs[i] = backward(
-            upstream[i], row_weights, slope[i], attended[i], qkv[i], log_total[i], tables, positions
+            upstream[i], row_weights, slope[i], attended[i], qkv[i], log_total[i], tables, spot
         )
         inner[i] = input_side(
             rows[i],

time: 551 us -> 556 us (level)
    unnamed x138 -> x140, local copies, waits for them, and re-layouts: 28.9 us -> 26.3 us
    pallas_call x33 -> x34, Pallas kernels: 112 us -> 114 us  [call(): pl.pallas_call(kernel, grid_spec=pltpu.PrefetchScalarGridSpec(num_scalar_...]
where the time goes in v3:
time: 556 us; the launch traced here: 547 us
  waiting for transfers between devices  214 us (38%)
  starting transfers between devices  177 us (32%)
  Pallas kernels  114 us (21%)
  local copies, waits for them, and re-layouts  31.6 us (6%)
  other arithmetic  7.57 us (1%)
    ppermute x48, waiting for transfers between devices, rotated(): lax.ppermute(value, axis, [(i, (i + steps) % count) for i in range(count)])  192 us
    pallas_call x34, Pallas kernels, call(): pl.pallas_call(kernel, grid_spec=pltpu.PrefetchScalarGridSpec(num_scalar_...  114 us
    ppermute x48, starting transfers between devices, rotated(): lax.ppermute(value, axis, [(i, (i + steps) % count) for i in range(count)])  83.6 us
    ppermute x14, starting transfers between devices, to_members(): came.append(lax.ppermute(pieces[k], GROUP, route))  65.4 us
    unnamed x140, local copies, waits for them, and re-layouts  26.3 us
  transfers between devices with their start and end apart: 76, of which 23 were waited for; matrix products, arithmetic and copies ran while one was open for 2% of the time, Pallas kernels for 20%

profile of v3, /device:TPU:0, one launch (start us, length us, event | category | flops | bytes accessed | tf_op | source)
XLA Modules:
  0.0 546.6 jit_solution(9509803706477537913)
XLA Ops:
  3.9 5.1 collective-permute-start.20
  10.1 2.2 copy-done.9
  12.2 2.1 shard_map.254
  16.5 2.5 collective-permute-start.1
  21.2 1.9 collective-permute-done.21
  24.0 3.0 collective-permute-start.4
  28.9 6.3 %collective-permute-start.24 = (bf16[512,256]{1,0:T(8,128)(2,1)S(1)}, bf16[512,256]{1,0:T(8,128)(2,1)S(1)}, u32[]{:S(2)}, u32[]{:S(2)}) collective-permute-start(bf16[512,256]{1,0:T(8,128)(2,1)S(1)} %get-tuple-element.198), channel_id=1, source_target_pairs={{0,2},{1,5},{2,0},{3,3},{4,6},{5,1},{6,4},{7,7},{8,10},{9,13},{10,... | collective-permute-start | bytes 786440 | tf_op jit(solution)/shard_map/ppermute | solution.py:1243
  37.6 15.2 %collective-permute-start.6 = (bf16[320,256]{1,0:T(8,128)(2,1)}, bf16[320,256]{1,0:T(8,128)(2,1)S(1)}, u32[]{:S(2)}, u32[]{:S(2)}) collective-permute-start(bf16[320,256]{1,0:T(8,128)(2,1)} %get-tuple-element.114), channel_id=1, source_target_pairs={{0,7},{1,6},{2,1},{3,0},{4,3},{5,2},{6,5},{7,4},{8,15},{9,14},{10,... | collective-permute-start | bytes 491528 | tf_op jit(solution)/shard_map/ppermute | solution.py:1031
  57.0 4.6 collective-permute-start.35
  61.7 2.8 collective-permute-done.23.refs_1_
  66.2 19.1 %collective-permute-start.11 = (bf16[128,2048]{1,0:T(8,128)(2,1)S(1)}, bf16[128,2048]{1,0:T(8,128)(2,1)S(1)}, u32[]{:S(2)}, u32[]{:S(2)}) collective-permute-start(bf16[128,2048]{1,0:T(8,128)(2,1)S(1)} %bitcast.62), channel_id=1, source_target_pairs={{0,2},{2,4},{4,6},{6,0},{1,3},{3,5},{5,7},{7,1},{8,10},{10,12},{12... | collective-permute-start | bytes 1572872 | tf_op jit(solution)/shard_map/ppermute | solution.py:349
  87.3 5.7 %collective-permute-done.33.refs_1_ = bf16[128,2048]{1,0:T(8,128)(2,1)} collective-permute-done((bf16[128,2048]{1,0:T(8,128)(2,1)S(1)}, bf16[128,2048]{1,0:T(8,128)(2,1)}, u32[]{:S(2)}, u32[]{:S(2)}) %collective-permute-start.33) | collective-permute-done | bytes 524320 | tf_op jit(solution)/shard_map/ppermute | solution.py:349
  97.5 14.5 %collective-permute-done.11.refs_1_ = bf16[128,2048]{1,0:T(8,128)(2,1)S(1)} collective-permute-done((bf16[128,2048]{1,0:T(8,128)(2,1)S(1)}, bf16[128,2048]{1,0:T(8,128)(2,1)S(1)}, u32[]{:S(2)}, u32[]{:S(2)}) %collective-permute-start.11) | collective-permute-done | bytes 524320 | tf_op jit(solution)/shard_map/ppermute | solution.py:349
  126.1 2.4 collective-permute-start.17
  130.3 2.7 collective-permute-start.12
  134.3 4.0 collective-permute-done.17.refs_3_
  139.6 9.9 %collective-permute-done.12.refs_1_ = bf16[128,2048]{1,0:T(8,128)(2,1)S(1)} collective-permute-done((bf16[128,2048]{1,0:T(8,128)(2,1)S(1)}, bf16[128,2048]{1,0:T(8,128)(2,1)S(1)}, u32[]{:S(2)}, u32[]{:S(2)}) %collective-permute-start.12) | collective-permute-done | bytes 524320 | tf_op jit(solution)/shard_map/ppermute | solution.py:349
  153.2 7.5 %collective-permute-done.16.refs_2_ = bf16[128,2048]{1,0:T(8,128)(2,1)S(1)} collective-permute-done((bf16[128,2048]{1,0:T(8,128)(2,1)S(1)}, bf16[128,2048]{1,0:T(8,128)(2,1)S(1)}, u32[]{:S(2)}, u32[]{:S(2)}) %collective-permute-start.16) | collective-permute-done | bytes 524320 | tf_op jit(solution)/shard_map/ppermute | solution.py:349
  161.4 2.2 copy-done
  163.6 7.1 %shard_map.262 = (bf16[512,2048]{1,0:T(8,128)(2,1)S(1)}, bf16[512,2048]{1,0:T(8,128)(2,1)S(1)}, f32[512,1]{1,0:T(8,128)S(1)}, f32[512,1]{1,0:T(8,128)S(1)}, bf16...) custom-call(bf16[128,2048]{1,0:T(8,128)(2,1)S(1)} %bitcast.64, bf16[128,2048]{1,0:T(8,128)(2,1)S(1)} %collective-permute-done.11.refs_1_, ...), custom_call_target="tpu_custom_call" | custom-call | tf_op jit(solution)/shard_map/pallas_call | solution.py:385
  172.2 8.3 %shard_map.257 = (bf16[512,2048]{1,0:T(8,128)(2,1)S(1)}, bf16[512,2048]{1,0:T(8,128)(2,1)S(1)}, f32[512,1]{1,0:T(8,128)S(1)}, f32[512,1]{1,0:T(8,128)S(1)}, bf16...) custom-call(bf16[128,2048]{1,0:T(8,128)(2,1)} %collective-permute-done.10.refs_0_, ...), custom_call_target="tpu_custom_call" | custom-call | tf_op jit(solution)/shard_map/pallas_call | solution.py:385
  180.5 1.9 shard_map.259.w.refs_7_
  182.4 4.7 shard_map.263
  187.1 4.3 shard_map.260
  192.5 7.6 %shard_map.267 = (bf16[2,320,2048]{2,1,0:T(8,128)(2,1)}, f32[2,64,2048]{2,1,0:T(8,128)S(1)}, bf16[512,2048]{1,0:T(8,128)(2,1)S(1)}, bf16[512,2048]{1,0:T(8,128)(2,1)S(1)}) custom-call(s32[6]{0:T(128)S(1)} %stack.47.spot, bf16[512,1024]{1,0:T(8,128)(2,1)S(1)} %get-tuple-element.129.act.x0.y0, bf16[512,1024]{1,0:T(8,128)(2,1)S(1)} %get-tuple-element.123.act.x1.y1, ...), custom_call_target="tpu_custom_call" | custom-call | tf_op jit(solution)/shard_map/pallas_call | solution.py:385
  203.5 7.7 %shard_map.261 = (bf16[1280,2048]{1,0:T(8,128)(2,1)S(1)}, bf16[512,2048]{1,0:T(8,128)(2,1)}) custom-call(s32[4]{0:T(128)S(1)} %pad_add_fusion.meta, bf16[8,320,256]{2,1,0:T(8,128)(2,1)} %shard_map.255.p0, bf16[8,320,256]{2,1,0:T(8,128)(2,1)S(1)} %collective-permute-done.7.p1, bf16[8,320,256]{2,1,0:T(8,128)(2,1)} %collective-permute-done.8.p2, ...), custom_call_target="tpu_custom_call" | custom-call | tf_op jit(solution)/shard_map/pallas_call | solution.py:385
  211.2 5.7 %shard_map.270 = (bf16[512,1024]{1,0:T(8,128)(2,1)S(1)}, bf16[3,512,256]{2,1,0:T(8,128)(2,1)S(1)}, f32[1,1024]{1,0:T(1,128)S(1)}, f32[8,256]{1,0:T(8,128)S(1)}, f32[1,2048]{1,0:T(1,128)S(1)}) custom-call(s32[6]{0:T(128)S(1)} %stack.47.spot, bf16[512,2048]{1,0:T(8,128)(2,1)S(1)} %get-tuple-element.146.refs_0_.c1, ...), custom_call_target="tpu_custom_call" | custom-call | tf_op jit(solution)/shard_map/pallas_call | solution.py:385
  218.8 5.8 %shard_map.268 = (bf16[512,1024]{1,0:T(8,128)(2,1)S(1)}, bf16[3,512,256]{2,1,0:T(8,128)(2,1)S(1)}, f32[1,1024]{1,0:T(1,128)S(1)}, f32[8,256]{1,0:T(8,128)S(1)}, f32[1,2048]{1,0:T(1,128)S(1)}) custom-call(s32[6]{0:T(128)S(1)} %stack.47.spot, bf16[512,2048]{1,0:T(8,128)(2,1)S(1)} %get-tuple-element.137.refs_0_.c0, ...), custom_call_target="tpu_custom_call" | custom-call | tf_op jit(solution)/shard_map/pallas_call | solution.py:385
  224.7 4.6 shard_map.276
  229.7 4.2 shard_map.285
  235.5 7.4 %shard_map.271 = (f32[8,2048]{1,0:T(8,128)S(1)}, bf16[512,2048]{1,0:T(8,128)(2,1)}) custom-call(bf16[128,2048]{1,0:T(8,128)(2,1)} %collective-permute-done.10.refs_0_, bf16[128,2048]{1,0:T(8,128)(2,1)S(1)} %collective-permute-done.12.refs_1_, bf16[128,2048]{1,0:T(8,128)(2,1)S(1)} %copy-done.20, bf16[128,2048]{1,0:T(8,128)(2,1)} %collective-permute-done.17.refs_3_, ...), custom_call_target="tpu_custom_call" | custom-call | tf_op jit(solution)/shard_map/pallas_call | solution.py:385
  242.9 5.9 %shard_map.269 = (f32[8,2048]{1,0:T(8,128)S(1)}, bf16[512,2048]{1,0:T(8,128)(2,1)S(1)}) custom-call(bf16[128,2048]{1,0:T(8,128)(2,1)S(1)} %bitcast.65, bf16[128,2048]{1,0:T(8,128)(2,1)S(1)} %copy-done.18, bf16[128,2048]{1,0:T(8,128)(2,1)S(1)} %broadcast_select_fusion.1.refs_2_, bf16[128,2048]{1,0:T(8,128)(2,1)S(1)} %copy-done.16, ...), custom_call_target="tpu_custom_call" | custom-call | tf_op jit(solution)/shard_map/pallas_call | solution.py:385
  250.0 33.2 %collective-permute-done.46.b = f32[4,3072]{1,0:T(4,128)S(1)} collective-permute-done((f32[4,3072]{1,0:T(4,128)S(1)}, f32[4,3072]{1,0:T(4,128)S(1)}, u32[]{:S(2)}, u32[]{:S(2)}) %collective-permute-start.46) | collective-permute-done | bytes 49184 | tf_op jit(solution)/shard_map/ppermute | solution.py:349
  283.7 7.4 %collective-permute-start.47 = (f32[1,3072]{1,0:T(1,128)S(1)}, f32[1,3072]{1,0:T(1,128)S(1)}, u32[]{:S(2)}, u32[]{:S(2)}) collective-permute-start(f32[1,3072]{1,0:T(1,128)S(1)} %get-tuple-element.170), channel_id=1, source_target_pairs={{0,2},{2,4},{4,6},{6,0},{1,3},{3,5},{5,7},{7,1},{8,10},{10,12},{12... | collective-permute-start | bytes 36872 | tf_op jit(solution)/shard_map/ppermute | solution.py:349
  292.8 2.4 collective-permute-start.48
  295.3 2.4 collective-permute-start.49
  297.7 3.9 shard_map.277
  301.6 5.8 %shard_map.281 = (bf16[320,2048]{1,0:T(8,128)(2,1)S(1)}, f32[320,2048]{1,0:T(8,128)S(1)}) custom-call(s32[6]{0:T(128)S(1)} %stack.47.spot, bf16[512,1024]{1,0:T(8,128)(2,1)S(1)} %get-tuple-element.129.act.x0.y0, bf16[512,1024]{1,0:T(8,128)(2,1)S(1)} %get-tuple-element.123.act.x1.y1, bf16[512,1024]{1,0:T(8,128)(2,1)S(1)} %get-tuple-element.129.act.x0.y0, ...), custom_call_target="tpu_custom_call" | custom-call | tf_op jit(solution)/shard_map/pallas_call | solution.py:385
  309.6 4.6 shard_map.286.a
  316.5 4.0 shard_map.264.a
  320.7 77.4 %collective-permute-done.51 = f32[1,3072]{1,0:T(1,128)S(1)} collective-permute-done((f32[1,3072]{1,0:T(1,128)S(1)}, f32[1,3072]{1,0:T(1,128)S(1)}, u32[]{:S(2)}, u32[]{:S(2)}) %collective-permute-start.51) | collective-permute-done | bytes 12320 | tf_op jit(solution)/shard_map/ppermute | solution.py:349
  398.1 1.7 collective-permute-start.30
  400.9 2.8 collective-permute-start.43
  403.7 8.4 %collective-permute-done.30.refs_1_ = bf16[128,2048]{1,0:T(8,128)(2,1)S(1)} collective-permute-done((bf16[128,2048]{1,0:T(8,128)(2,1)S(1)}, bf16[128,2048]{1,0:T(8,128)(2,1)S(1)}, u32[]{:S(2)}, u32[]{:S(2)}) %collective-permute-start.30) | collective-permute-done | bytes 524320 | tf_op jit(solution)/shard_map/ppermute | solution.py:1274
  413.7 7.7 %collective-permute-start.55 = (bf16[512,256]{1,0:T(8,128)(2,1)S(1)}, bf16[512,256]{1,0:T(8,128)(2,1)S(1)}, u32[]{:S(2)}, u32[]{:S(2)}) collective-permute-start(bf16[512,256]{1,0:T(8,128)(2,1)S(1)} %get-tuple-element.176), channel_id=1, source_target_pairs={{1,0},{4,1},{7,2},{2,3},{5,4},{0,5},{3,6},{6,7},{9,8},{12,9},{15,1... | collective-permute-start | bytes 786440 | tf_op jit(solution)/shard_map/ppermute | solution.py:1331
  422.3 4.0 collective-permute-start.62
  426.3 8.9 %collective-permute-start.63 = (bf16[320,256]{1,0:T(8,128)(2,1)S(1)}, bf16[320,256]{1,0:T(8,128)(2,1)S(1)}, u32[]{:S(2)}, u32[]{:S(2)}) collective-permute-start(bf16[320,256]{1,0:T(8,128)(2,1)S(1)} %get-tuple-element.184), channel_id=1, source_target_pairs={{0,2},{1,3},{2,4},{3,5},{4,6},{5,7},{6,0},{7,1},{8,10},{9,11},{10,... | collective-permute-start | bytes 491528 | tf_op jit(solution)/shard_map/ppermute | solution.py:1031
  435.2 14.6 %collective-permute-start.65 = (bf16[320,256]{1,0:T(8,128)(2,1)S(1)}, bf16[320,256]{1,0:T(8,128)(2,1)S(1)}, u32[]{:S(2)}, u32[]{:S(2)}) collective-permute-start(bf16[320,256]{1,0:T(8,128)(2,1)S(1)} %get-tuple-element.186), channel_id=1, source_target_pairs={{0,4},{1,5},{2,6},{3,7},{4,0},{5,1},{6,2},{7,3},{8,12},{9,13},{10,... | collective-permute-start | bytes 491528 | tf_op jit(solution)/shard_map/ppermute | solution.py:1031
  449.8 1.9 collective-permute-start.56
  451.8 5.0 collective-permute-done.64.refs_3_
  456.8 2.9 collective-permute-done.65.refs_4_
  459.6 13.7 %collective-permute-start.68 = (bf16[320,256]{1,0:T(8,128)(2,1)S(1)}, bf16[320,256]{1,0:T(8,128)(2,1)S(1)}, u32[]{:S(2)}, u32[]{:S(2)}) collective-permute-start(bf16[320,256]{1,0:T(8,128)(2,1)S(1)} %get-tuple-element.189), channel_id=1, source_target_pairs={{0,7},{1,6},{2,1},{3,0},{4,3},{5,2},{6,5},{7,4},{8,15},{9,14},{10,... | collective-permute-start | bytes 491528 | tf_op jit(solution)/shard_map/ppermute | solution.py:1031
  475.2 12.9 %collective-permute-start.31 = (bf16[128,2048]{1,0:T(8,128)(2,1)S(1)}, bf16[128,2048]{1,0:T(8,128)(2,1)S(1)}, u32[]{:S(2)}, u32[]{:S(2)}) collective-permute-start(bf16[128,2048]{1,0:T(8,128)(2,1)S(1)} %get-tuple-element.135), channel_id=1, source_target_pairs={{0,6},{2,0},{4,2},{6,4},{1,7},{3,1},{5,3},{7,5},{8,14},{10,8},{12,... | collective-permute-start | bytes 1572872 | tf_op jit(solution)/shard_map/ppermute | solution.py:349
  488.1 3.8 collective-permute-start.44
  492.9 1.9 collective-permute-done.31
  494.8 10.3 %collective-permute-done.32 = bf16[128,2048]{1,0:T(8,128)(2,1)S(1)} collective-permute-done((bf16[128,2048]{1,0:T(8,128)(2,1)S(1)}, bf16[128,2048]{1,0:T(8,128)(2,1)S(1)}, u32[]{:S(2)}, u32[]{:S(2)}) %collective-permute-start.32) | collective-permute-done | bytes 524320 | tf_op jit(solution)/shard_map/ppermute | solution.py:349
  505.0 6.6 %collective-permute-done.44 = bf16[128,2048]{1,0:T(8,128)(2,1)S(1)} collective-permute-done((bf16[128,2048]{1,0:T(8,128)(2,1)S(1)}, bf16[128,2048]{1,0:T(8,128)(2,1)S(1)}, u32[]{:S(2)}, u32[]{:S(2)}) %collective-permute-start.44) | collective-permute-done | bytes 524320 | tf_op jit(solution)/shard_map/ppermute | solution.py:349
  512.0 11.1 %collective-permute-done.45 = bf16[128,2048]{1,0:T(8,128)(2,1)S(1)} collective-permute-done((bf16[128,2048]{1,0:T(8,128)(2,1)S(1)}, bf16[128,2048]{1,0:T(8,128)(2,1)S(1)}, u32[]{:S(2)}, u32[]{:S(2)}) %collective-permute-start.45) | collective-permute-done | bytes 524320 | tf_op jit(solution)/shard_map/ppermute | solution.py:349
  523.6 3.4 collective-permute-done.58.p2
  529.3 1.9 fusion.12
  531.3 1.9 collective-permute-done.59.p3
  533.1 3.6 shard_map.280
  536.7 4.7 shard_map.284
  541.4 4.3 shard_map.287
  (314 shorter events, 76.4 us)
Async XLA Ops:
  3.9 15.1 %collective-permute-start.20 = (bf16[2304]{0:T(1024)(128)(2,1)S(1)}, bf16[2304]{0:T(1024)(128)(2,1)S(1)}, u32[]{:S(2)}, u32[]{:S(2)}) collective-permute-start(bf16[2304]{0:T(1024)(128)(2,1)S(1)} %reduce), channel_id=1, source_target_pairs={{0,6},{2,0},{4,2},{6,4},{1,7},{3,1},{5,3},{7,5},{8,14},{10,8},{12,... | collective-permute-start | bytes 13832 | tf_op jit(solution)/shard_map/ppermute | solution.py:349
  16.5 11.8 %collective-permute-start.1 = (bf16[320,256]{1,0:T(8,128)(2,1)}, bf16[320,256]{1,0:T(8,128)(2,1)S(1)}, u32[]{:S(2)}, u32[]{:S(2)}) collective-permute-start(bf16[320,256]{1,0:T(8,128)(2,1)} %get-tuple-element.109), channel_id=1, source_target_pairs={{0,2},{1,3},{2,4},{3,5},{4,6},{5,7},{6,0},{7,1},{8,10},{9,11},{10,... | collective-permute-start | bytes 491528 | tf_op jit(solution)/shard_map/ppermute | solution.py:1031
  19.7 65.7 %collective-permute-start.37 = (bf16[128,2048]{1,0:T(8,128)(2,1)S(1)}, bf16[128,2048]{1,0:T(8,128)(2,1)}, u32[]{:S(2)}, u32[]{:S(2)}) collective-permute-start(bf16[128,2048]{1,0:T(8,128)(2,1)S(1)} %bitcast.66), channel_id=1, source_target_pairs={{0,1},{1,0},{2,3},{3,2},{4,5},{5,4},{6,7},{7,6},{8,9},{9,8},{10,11... | collective-permute-start | bytes 1572872 | tf_op jit(solution)/shard_map/ppermute | solution.py:349
  21.2 14.0 %collective-permute-start.2 = (bf16[320,256]{1,0:T(8,128)(2,1)}, bf16[320,256]{1,0:T(8,128)(2,1)S(1)}, u32[]{:S(2)}, u32[]{:S(2)}) collective-permute-start(bf16[320,256]{1,0:T(8,128)(2,1)} %get-tuple-element.110), channel_id=1, source_target_pairs={{0,3},{1,2},{2,5},{3,4},{4,7},{5,6},{6,1},{7,0},{8,11},{9,10},{10,... | collective-permute-start | bytes 491528 | tf_op jit(solution)/shard_map/ppermute | solution.py:1031
  23.1 13.9 %collective-permute-start.3 = (bf16[320,256]{1,0:T(8,128)(2,1)}, bf16[320,256]{1,0:T(8,128)(2,1)S(1)}, u32[]{:S(2)}, u32[]{:S(2)}) collective-permute-start(bf16[320,256]{1,0:T(8,128)(2,1)} %copy-done.54), channel_id=1, source_target_pairs={{0,4},{1,5},{2,6},{3,7},{4,0},{5,1},{6,2},{7,3},{8,12},{9,13},{10,... | collective-permute-start | bytes 491528 | tf_op jit(solution)/shard_map/ppermute | solution.py:1031
  24.0 28.8 %collective-permute-start.4 = (bf16[320,256]{1,0:T(8,128)(2,1)S(1)}, bf16[320,256]{1,0:T(8,128)(2,1)S(1)}, u32[]{:S(2)}, u32[]{:S(2)}) collective-permute-start(bf16[320,256]{1,0:T(8,128)(2,1)S(1)} %get-tuple-element.112), channel_id=1, source_target_pairs={{0,5},{1,4},{2,7},{3,6},{4,1},{5,0},{6,3},{7,2},{8,13},{9,12},{10,... | collective-permute-start | bytes 491528 | tf_op jit(solution)/shard_map/ppermute | solution.py:1031
  28.9 32.7 %collective-permute-start.24 = (bf16[512,256]{1,0:T(8,128)(2,1)S(1)}, bf16[512,256]{1,0:T(8,128)(2,1)S(1)}, u32[]{:S(2)}, u32[]{:S(2)}) collective-permute-start(bf16[512,256]{1,0:T(8,128)(2,1)S(1)} %get-tuple-element.198), channel_id=1, source_target_pairs={{0,2},{1,5},{2,0},{3,3},{4,6},{5,1},{6,4},{7,7},{8,10},{9,13},{10,... | collective-permute-start | bytes 786440 | tf_op jit(solution)/shard_map/ppermute | solution.py:1243
  35.9 17.6 %collective-permute-start.5 = (bf16[320,256]{1,0:T(8,128)(2,1)}, bf16[320,256]{1,0:T(8,128)(2,1)S(1)}, u32[]{:S(2)}, u32[]{:S(2)}) collective-permute-start(bf16[320,256]{1,0:T(8,128)(2,1)} %get-tuple-element.113), channel_id=1, source_target_pairs={{0,6},{1,7},{2,0},{3,1},{4,2},{5,3},{6,4},{7,5},{8,14},{9,15},{10,... | collective-permute-start | bytes 491528 | tf_op jit(solution)/shard_map/ppermute | solution.py:1031
  37.6 18.7 %collective-permute-start.6 = (bf16[320,256]{1,0:T(8,128)(2,1)}, bf16[320,256]{1,0:T(8,128)(2,1)S(1)}, u32[]{:S(2)}, u32[]{:S(2)}) collective-permute-start(bf16[320,256]{1,0:T(8,128)(2,1)} %get-tuple-element.114), channel_id=1, source_target_pairs={{0,7},{1,6},{2,1},{3,0},{4,3},{5,2},{6,5},{7,4},{8,15},{9,14},{10,... | collective-permute-start | bytes 491528 | tf_op jit(solution)/shard_map/ppermute | solution.py:1031
  54.2 11.3 %collective-permute-start.22 = (bf16[512,256]{1,0:T(8,128)(2,1)S(1)}, bf16[512,256]{1,0:T(8,128)(2,1)S(1)}, u32[]{:S(2)}, u32[]{:S(2)}) collective-permute-start(bf16[512,256]{1,0:T(8,128)(2,1)S(1)} %get-tuple-element.200), channel_id=1, source_target_pairs={{0,0},{1,3},{2,6},{3,1},{4,4},{5,7},{6,2},{7,5},{8,8},{9,11},{10,1... | collective-permute-start | bytes 786440 | tf_op jit(solution)/shard_map/ppermute | solution.py:1243
  57.0 28.9 %collective-permute-start.35 = (bf16[128,2048]{1,0:T(8,128)(2,1)S(1)}, bf16[128,2048]{1,0:T(8,128)(2,1)}, u32[]{:S(2)}, u32[]{:S(2)}) collective-permute-start(bf16[128,2048]{1,0:T(8,128)(2,1)S(1)} %bitcast.67), channel_id=1, source_target_pairs={{0,6},{2,0},{4,2},{6,4},{1,7},{3,1},{5,3},{7,5},{8,14},{10,8},{12,... | collective-permute-start | bytes 1572872 | tf_op jit(solution)/shard_map/ppermute | solution.py:349
  61.7 31.3 %collective-permute-start.33 = (bf16[128,2048]{1,0:T(8,128)(2,1)S(1)}, bf16[128,2048]{1,0:T(8,128)(2,1)}, u32[]{:S(2)}, u32[]{:S(2)}) collective-permute-start(bf16[128,2048]{1,0:T(8,128)(2,1)S(1)} %bitcast.68), channel_id=1, source_target_pairs={{0,2},{2,4},{4,6},{6,0},{1,3},{3,5},{5,7},{7,1},{8,10},{10,12},{12... | collective-permute-start | bytes 1572872 | tf_op jit(solution)/shard_map/ppermute | solution.py:349
  64.5 30.9 %collective-permute-start.14 = (bf16[128,2048]{1,0:T(8,128)(2,1)S(1)}, bf16[128,2048]{1,0:T(8,128)(2,1)S(1)}, u32[]{:S(2)}, u32[]{:S(2)}) collective-permute-start(bf16[128,2048]{1,0:T(8,128)(2,1)S(1)} %bitcast.61), channel_id=1, source_target_pairs={{0,6},{2,0},{4,2},{6,4},{1,7},{3,1},{5,3},{7,5},{8,14},{10,8},{12,... | collective-permute-start | bytes 1572872 | tf_op jit(solution)/shard_map/ppermute | solution.py:349
  66.2 45.8 %collective-permute-start.11 = (bf16[128,2048]{1,0:T(8,128)(2,1)S(1)}, bf16[128,2048]{1,0:T(8,128)(2,1)S(1)}, u32[]{:S(2)}, u32[]{:S(2)}) collective-permute-start(bf16[128,2048]{1,0:T(8,128)(2,1)S(1)} %bitcast.62), channel_id=1, source_target_pairs={{0,2},{2,4},{4,6},{6,0},{1,3},{3,5},{5,7},{7,1},{8,10},{10,12},{12... | collective-permute-start | bytes 1572872 | tf_op jit(solution)/shard_map/ppermute | solution.py:349
  85.3 27.9 %collective-permute-start.10 = (bf16[128,2048]{1,0:T(8,128)(2,1)S(1)}, bf16[128,2048]{1,0:T(8,128)(2,1)}, u32[]{:S(2)}, u32[]{:S(2)}) collective-permute-start(bf16[128,2048]{1,0:T(8,128)(2,1)S(1)} %bitcast.63), channel_id=1, source_target_pairs={{0,1},{1,0},{2,3},{3,2},{4,5},{5,4},{6,7},{7,6},{8,9},{9,8},{10,11... | collective-permute-start | bytes 1572872 | tf_op jit(solution)/shard_map/ppermute | solution.py:349
  86.0 37.9 %collective-permute-start.36 = (bf16[128,2048]{1,0:T(8,128)(2,1)}, bf16[128,2048]{1,0:T(8,128)(2,1)S(1)}, u32[]{:S(2)}, u32[]{:S(2)}) collective-permute-start(bf16[128,2048]{1,0:T(8,128)(2,1)} %collective-permute-done.35.refs_3_), channel_id=1, source_target_pairs={{4,2},{2,0},{5,3},{3,1},{12,10},{10,8},{13,11},{11,9},{20,18},{18,... | collective-permute-start | bytes 1572872 | tf_op jit(solution)/shard_map/ppermute | solution.py:357
  93.0 32.4 %collective-permute-start.34 = (bf16[128,2048]{1,0:T(8,128)(2,1)}, bf16[128,2048]{1,0:T(8,128)(2,1)S(1)}, u32[]{:S(2)}, u32[]{:S(2)}) collective-permute-start(bf16[128,2048]{1,0:T(8,128)(2,1)} %collective-permute-done.33.refs_1_), channel_id=1, source_target_pairs={{2,4},{4,6},{3,5},{5,7},{10,12},{12,14},{11,13},{13,15},{18,20},{2... | collective-permute-start | bytes 1572872 | tf_op jit(solution)/shard_map/ppermute | solution.py:356
  95.4 37.6 %collective-permute-start.26 = (bf16[512,768]{1,0:T(8,128)(2,1)S(1)}, bf16[512,768]{1,0:T(8,128)(2,1)}, u32[]{:S(2)}, u32[]{:S(2)}) collective-permute-start(bf16[512,768]{1,0:T(8,128)(2,1)S(1)} %shard_map.258.p0), channel_id=1, source_target_pairs={{0,16},{16,0},{1,17},{17,1},{2,18},{18,2},{3,19},{19,3},{4,20},{20... | collective-permute-start | bytes 2359304 | tf_op jit(solution)/shard_map/ppermute | solution.py:349
  112.0 18.2 %collective-permute-start.15 = (bf16[128,2048]{1,0:T(8,128)(2,1)S(1)}, bf16[128,2048]{1,0:T(8,128)(2,1)}, u32[]{:S(2)}, u32[]{:S(2)}) collective-permute-start(bf16[128,2048]{1,0:T(8,128)(2,1)S(1)} %collective-permute-done.14.refs_3_), channel_id=1, source_target_pairs={{4,2},{2,0},{5,3},{3,1},{12,10},{10,8},{13,11},{11,9},{20,18},{18,... | collective-permute-start | bytes 1572872 | tf_op jit(solution)/shard_map/ppermute | solution.py:357
  113.3 17.0 %collective-permute-start.13 = (bf16[128,2048]{1,0:T(8,128)(2,1)S(1)}, bf16[128,2048]{1,0:T(8,128)(2,1)}, u32[]{:S(2)}, u32[]{:S(2)}) collective-permute-start(bf16[128,2048]{1,0:T(8,128)(2,1)S(1)} %collective-permute-done.11.refs_1_), channel_id=1, source_target_pairs={{2,4},{4,6},{3,5},{5,7},{10,12},{12,14},{11,13},{13,15},{18,20},{2... | collective-permute-start | bytes 1572872 | tf_op jit(solution)/shard_map/ppermute | solution.py:356
  123.9 27.7 %collective-permute-start.8 = (bf16[8,320,256]{2,1,0:T(8,128)(2,1)}, bf16[8,320,256]{2,1,0:T(8,128)(2,1)}, u32[]{:S(2)}, u32[]{:S(2)}) collective-permute-start(bf16[8,320,256]{2,1,0:T(8,128)(2,1)} %shard_map.255.p0), channel_id=1, source_target_pairs={{0,16},{16,0},{1,17},{17,1},{2,18},{18,2},{3,19},{19,3},{4,20},{20... | collective-permute-start | bytes 3932168 | tf_op jit(solution)/shard_map/ppermute | solution.py:349
  126.1 12.2 %collective-permute-start.17 = (bf16[128,2048]{1,0:T(8,128)(2,1)S(1)}, bf16[128,2048]{1,0:T(8,128)(2,1)}, u32[]{:S(2)}, u32[]{:S(2)}) collective-permute-start(bf16[128,2048]{1,0:T(8,128)(2,1)S(1)} %collective-permute-done.14.refs_3_), channel_id=1, source_target_pairs={{0,1},{1,0},{2,3},{3,2},{4,5},{5,4},{6,7},{7,6},{8,9},{9,8},{10,11... | collective-permute-start | bytes 1572872 | tf_op jit(solution)/shard_map/ppermute | solution.py:349
  130.2 20.5 %collective-permute-start.25 = (bf16[512,768]{1,0:T(8,128)(2,1)S(1)}, bf16[512,768]{1,0:T(8,128)(2,1)S(1)}, u32[]{:S(2)}, u32[]{:S(2)}) collective-permute-start(bf16[512,768]{1,0:T(8,128)(2,1)S(1)} %shard_map.258.p0), channel_id=1, source_target_pairs={{0,8},{8,0},{1,9},{9,1},{2,10},{10,2},{3,11},{11,3},{4,12},{12,4},... | collective-permute-start | bytes 2359304 | tf_op jit(solution)/shard_map/ppermute | solution.py:349
  130.3 19.2 %collective-permute-start.12 = (bf16[128,2048]{1,0:T(8,128)(2,1)S(1)}, bf16[128,2048]{1,0:T(8,128)(2,1)S(1)}, u32[]{:S(2)}, u32[]{:S(2)}) collective-permute-start(bf16[128,2048]{1,0:T(8,128)(2,1)S(1)} %collective-permute-done.11.refs_1_), channel_id=1, source_target_pairs={{0,1},{1,0},{2,3},{3,2},{4,5},{5,4},{6,7},{7,6},{8,9},{9,8},{10,11... | collective-permute-start | bytes 1572872 | tf_op jit(solution)/shard_map/ppermute | solution.py:349
  133.0 27.8 %collective-permute-start.27 = (bf16[512,768]{1,0:T(8,128)(2,1)}, bf16[512,768]{1,0:T(8,128)(2,1)S(1)}, u32[]{:S(2)}, u32[]{:S(2)}) collective-permute-start(bf16[512,768]{1,0:T(8,128)(2,1)} %collective-permute-done.26.p2), channel_id=1, source_target_pairs={{0,8},{8,0},{1,9},{9,1},{2,10},{10,2},{3,11},{11,3},{4,12},{12,4},... | collective-permute-start | bytes 2359304 | tf_op jit(solution)/shard_map/ppermute | solution.py:349
  138.4 22.4 %collective-permute-start.16 = (bf16[128,2048]{1,0:T(8,128)(2,1)S(1)}, bf16[128,2048]{1,0:T(8,128)(2,1)S(1)}, u32[]{:S(2)}, u32[]{:S(2)}) collective-permute-start(bf16[128,2048]{1,0:T(8,128)(2,1)S(1)} %broadcast_select_fusion.1.refs_2_), channel_id=1, source_target_pairs={{0,1},{1,0},{2,3},{3,2},{4,5},{5,4},{6,7},{7,6},{8,9},{9,8},{10,11... | collective-permute-start | bytes 1572872 | tf_op jit(solution)/shard_map/ppermute | solution.py:349
  149.5 41.9 %collective-permute-start.40 = (bf16[128,2048]{1,0:T(8,128)(2,1)}, bf16[128,2048]{1,0:T(8,128)(2,1)S(1)}, u32[]{:S(2)}, u32[]{:S(2)}) collective-permute-start(bf16[128,2048]{1,0:T(8,128)(2,1)} %collective-permute-done.35.refs_3_), channel_id=1, source_target_pairs={{0,1},{1,0},{2,3},{3,2},{4,5},{5,4},{6,7},{7,6},{8,9},{9,8},{10,11... | collective-permute-start | bytes 1572872 | tf_op jit(solution)/shard_map/ppermute | solution.py:349
  150.7 40.7 %collective-permute-start.38 = (bf16[128,2048]{1,0:T(8,128)(2,1)}, bf16[128,2048]{1,0:T(8,128)(2,1)S(1)}, u32[]{:S(2)}, u32[]{:S(2)}) collective-permute-start(bf16[128,2048]{1,0:T(8,128)(2,1)} %collective-permute-done.33.refs_1_), channel_id=1, source_target_pairs={{0,1},{1,0},{2,3},{3,2},{4,5},{5,4},{6,7},{7,6},{8,9},{9,8},{10,11... | collective-permute-start | bytes 1572872 | tf_op jit(solution)/shard_map/ppermute | solution.py:349
  151.5 40.9 %collective-permute-start.39 = (bf16[128,2048]{1,0:T(8,128)(2,1)S(1)}, bf16[128,2048]{1,0:T(8,128)(2,1)S(1)}, u32[]{:S(2)}, u32[]{:S(2)}) collective-permute-start(bf16[128,2048]{1,0:T(8,128)(2,1)S(1)} %broadcast_select_fusion.refs_2_), channel_id=1, source_target_pairs={{0,1},{1,0},{2,3},{3,2},{4,5},{5,4},{6,7},{7,6},{8,9},{9,8},{10,11... | collective-permute-start | bytes 1572872 | tf_op jit(solution)/shard_map/ppermute | solution.py:349
  160.7 40.4 %collective-permute-start.7 = (bf16[8,320,256]{2,1,0:T(8,128)(2,1)}, bf16[8,320,256]{2,1,0:T(8,128)(2,1)S(1)}, u32[]{:S(2)}, u32[]{:S(2)}) collective-permute-start(bf16[8,320,256]{2,1,0:T(8,128)(2,1)} %shard_map.255.p0), channel_id=1, source_target_pairs={{0,8},{8,0},{1,9},{9,1},{2,10},{10,2},{3,11},{11,3},{4,12},{12,4},... | collective-permute-start | bytes 3932168 | tf_op jit(solution)/shard_map/ppermute | solution.py:349
  160.7 40.4 %collective-permute-start.9 = (bf16[8,320,256]{2,1,0:T(8,128)(2,1)}, bf16[8,320,256]{2,1,0:T(8,128)(2,1)S(1)}, u32[]{:S(2)}, u32[]{:S(2)}) collective-permute-start(bf16[8,320,256]{2,1,0:T(8,128)(2,1)} %collective-permute-done.8.p2), channel_id=1, source_target_pairs={{0,8},{8,0},{1,9},{9,1},{2,10},{10,2},{3,11},{11,3},{4,12},{12,4},... | collective-permute-start | bytes 3932168 | tf_op jit(solution)/shard_map/ppermute | solution.py:349
  201.1 94.2 %collective-permute-start.60 = (bf16[2,320,2048]{2,1,0:T(8,128)(2,1)}, bf16[2,320,2048]{2,1,0:T(8,128)(2,1)}, u32[]{:S(2)}, u32[]{:S(2)}) collective-permute-start(bf16[2,320,2048]{2,1,0:T(8,128)(2,1)} %get-tuple-element.178), channel_id=1, source_target_pairs={{0,8},{8,0},{1,9},{9,1},{2,10},{10,2},{3,11},{11,3},{4,12},{12,4},... | collective-permute-start | bytes 7864328 | tf_op jit(solution)/shard_map/ppermute | solution.py:349
  229.3 63.6 %collective-permute-start.52 = (bf16[2,512,768]{2,1,0:T(8,128)(2,1)}, bf16[2,512,768]{2,1,0:T(8,128)(2,1)S(1)}, u32[]{:S(2)}, u32[]{:S(2)}) collective-permute-start(bf16[2,512,768]{2,1,0:T(8,128)(2,1)} %shard_map.276), channel_id=1, source_target_pairs={{0,8},{8,0},{1,9},{9,1},{2,10},{10,2},{3,11},{11,3},{4,12},{12,4},... | collective-permute-start | bytes 4718600 | tf_op jit(solution)/shard_map/ppermute | solution.py:349
  233.8 75.7 %collective-permute-start.72 = (bf16[1024,1024]{1,0:T(8,128)(2,1)}, bf16[1024,1024]{1,0:T(8,128)(2,1)}, u32[]{:S(2)}, u32[]{:S(2)}) collective-permute-start(bf16[1024,1024]{1,0:T(8,128)(2,1)} %shard_map.285), channel_id=1, source_target_pairs={{0,8},{8,0},{1,9},{9,1},{2,10},{10,2},{3,11},{11,3},{4,12},{12,4},... | collective-permute-start | bytes 6291464 | tf_op jit(solution)/shard_map/ppermute | solution.py:349
  233.9 81.7 %collective-permute-start.28 = (bf16[512,2048]{1,0:T(8,128)(2,1)}, bf16[512,2048]{1,0:T(8,128)(2,1)S(1)}, u32[]{:S(2)}, u32[]{:S(2)}) collective-permute-start(bf16[512,2048]{1,0:T(8,128)(2,1)} %get-tuple-element.132), channel_id=1, source_target_pairs={{0,1},{1,0},{2,3},{3,2},{4,5},{5,4},{6,7},{7,6},{8,9},{9,8},{10,11... | collective-permute-start | bytes 6291464 | tf_op jit(solution)/shard_map/ppermute | solution.py:349
  249.4 33.8 %collective-permute-start.46 = (f32[4,3072]{1,0:T(4,128)S(1)}, f32[4,3072]{1,0:T(4,128)S(1)}, u32[]{:S(2)}, u32[]{:S(2)}) collective-permute-start(f32[4,3072]{1,0:T(4,128)S(1)} %get-tuple-element.168), channel_id=1, source_target_pairs={{0,1},{1,0},{2,3},{3,2},{4,5},{5,4},{6,7},{7,6},{8,9},{9,8},{10,11... | collective-permute-start | bytes 147464 | tf_op jit(solution)/shard_map/ppermute | solution.py:349
  292.5 107.3 %collective-permute-start.41 = (bf16[512,2048]{1,0:T(8,128)(2,1)}, bf16[512,2048]{1,0:T(8,128)(2,1)S(1)}, u32[]{:S(2)}, u32[]{:S(2)}) collective-permute-start(bf16[512,2048]{1,0:T(8,128)(2,1)} %get-tuple-element.154), channel_id=1, source_target_pairs={{0,1},{1,0},{2,3},{3,2},{4,5},{5,4},{6,7},{7,6},{8,9},{9,8},{10,11... | collective-permute-start | bytes 6291464 | tf_op jit(solution)/shard_map/ppermute | solution.py:349
  292.8 14.6 %collective-permute-start.48 = (f32[1,3072]{1,0:T(1,128)S(1)}, f32[1,3072]{1,0:T(1,128)S(1)}, u32[]{:S(2)}, u32[]{:S(2)}) collective-permute-start(f32[1,3072]{1,0:T(1,128)S(1)} %get-tuple-element.171), channel_id=1, source_target_pairs={{0,4},{2,6},{4,0},{6,2},{1,5},{3,7},{5,1},{7,3},{8,12},{10,14},{12... | collective-permute-start | bytes 36872 | tf_op jit(solution)/shard_map/ppermute | solution.py:349
  295.3 13.5 %collective-permute-start.49 = (f32[1,3072]{1,0:T(1,128)S(1)}, f32[1,3072]{1,0:T(1,128)S(1)}, u32[]{:S(2)}, u32[]{:S(2)}) collective-permute-start(f32[1,3072]{1,0:T(1,128)S(1)} %get-tuple-element.172), channel_id=1, source_target_pairs={{0,6},{2,0},{4,2},{6,4},{1,7},{3,1},{5,3},{7,5},{8,14},{10,8},{12,... | collective-permute-start | bytes 36872 | tf_op jit(solution)/shard_map/ppermute | solution.py:349
  307.4 93.4 %collective-permute-start.53 = (bf16[512,768]{1,0:T(8,128)(2,1)S(1)}, bf16[512,768]{1,0:T(8,128)(2,1)S(1)}, u32[]{:S(2)}, u32[]{:S(2)}) collective-permute-start(bf16[512,768]{1,0:T(8,128)(2,1)S(1)} %get-tuple-element.174), channel_id=1, source_target_pairs={{0,16},{16,0},{1,17},{17,1},{2,18},{18,2},{3,19},{19,3},{4,20},{20... | collective-permute-start | bytes 2359304 | tf_op jit(solution)/shard_map/ppermute | solution.py:349
  308.7 104.9 %collective-permute-start.61 = (bf16[320,2048]{1,0:T(8,128)(2,1)S(1)}, bf16[320,2048]{1,0:T(8,128)(2,1)S(1)}, u32[]{:S(2)}, u32[]{:S(2)}) collective-permute-start(bf16[320,2048]{1,0:T(8,128)(2,1)S(1)} %get-tuple-element.181), channel_id=1, source_target_pairs={{0,16},{16,0},{1,17},{17,1},{2,18},{18,2},{3,19},{19,3},{4,20},{20... | collective-permute-start | bytes 3932168 | tf_op jit(solution)/shard_map/ppermute | solution.py:349
  314.3 197.3 %collective-permute-start.73 = (bf16[1024,1024]{1,0:T(8,128)(2,1)S(1)}, bf16[1024,1024]{1,0:T(8,128)(2,1)S(1)}, u32[]{:S(2)}, u32[]{:S(2)}) collective-permute-start(bf16[1024,1024]{1,0:T(8,128)(2,1)S(1)} %shard_map.286.a), channel_id=1, source_target_pairs={{0,16},{16,0},{1,17},{17,1},{2,18},{18,2},{3,19},{19,3},{4,20},{20... | collective-permute-start | bytes 6291464 | tf_op jit(solution)/shard_map/ppermute | solution.py:349
  315.6 82.5 %collective-permute-start.51 = (f32[1,3072]{1,0:T(1,128)S(1)}, f32[1,3072]{1,0:T(1,128)S(1)}, u32[]{:S(2)}, u32[]{:S(2)}) collective-permute-start(f32[1,3072]{1,0:T(1,128)S(1)} %add.168), channel_id=1, source_target_pairs={{0,16},{16,0},{1,17},{17,1},{2,18},{18,2},{3,19},{19,3},{4,20},{20... | collective-permute-start | bytes 36872 | tf_op jit(solution)/shard_map/ppermute | solution.py:349
  398.1 14.0 %collective-permute-start.30 = (bf16[128,2048]{1,0:T(8,128)(2,1)S(1)}, bf16[128,2048]{1,0:T(8,128)(2,1)S(1)}, u32[]{:S(2)}, u32[]{:S(2)}) collective-permute-start(bf16[128,2048]{1,0:T(8,128)(2,1)S(1)} %get-tuple-element.134), channel_id=1, source_target_pairs={{0,2},{2,4},{1,3},{3,5},{8,10},{10,12},{9,11},{11,13},{16,18},{18,... | collective-permute-start | bytes 1572872 | tf_op jit(solution)/shard_map/ppermute | solution.py:1274
  399.9 13.1 %collective-permute-start.29 = (bf16[128,2048]{1,0:T(8,128)(2,1)S(1)}, bf16[128,2048]{1,0:T(8,128)(2,1)S(1)}, u32[]{:S(2)}, u32[]{:S(2)}) collective-permute-start(bf16[128,2048]{1,0:T(8,128)(2,1)S(1)} %get-tuple-element.134), channel_id=1, source_target_pairs={{4,2},{6,4},{5,3},{7,5},{12,10},{14,12},{13,11},{15,13},{20,18},{2... | collective-permute-start | bytes 1572872 | tf_op jit(solution)/shard_map/ppermute | solution.py:1275
  400.9 34.3 %collective-permute-start.43 = (bf16[128,2048]{1,0:T(8,128)(2,1)S(1)}, bf16[128,2048]{1,0:T(8,128)(2,1)S(1)}, u32[]{:S(2)}, u32[]{:S(2)}) collective-permute-start(bf16[128,2048]{1,0:T(8,128)(2,1)S(1)} %get-tuple-element.156), channel_id=1, source_target_pairs={{0,2},{2,4},{1,3},{3,5},{8,10},{10,12},{9,11},{11,13},{16,18},{18,... | collective-permute-start | bytes 1572872 | tf_op jit(solution)/shard_map/ppermute | solution.py:1274
  412.1 23.0 %collective-permute-start.42 = (bf16[128,2048]{1,0:T(8,128)(2,1)S(1)}, bf16[128,2048]{1,0:T(8,128)(2,1)S(1)}, u32[]{:S(2)}, u32[]{:S(2)}) collective-permute-start(bf16[128,2048]{1,0:T(8,128)(2,1)S(1)} %get-tuple-element.156), channel_id=1, source_target_pairs={{4,2},{6,4},{5,3},{7,5},{12,10},{14,12},{13,11},{15,13},{20,18},{2... | collective-permute-start | bytes 1572872 | tf_op jit(solution)/shard_map/ppermute | solution.py:1275
  413.7 12.6 %collective-permute-start.55 = (bf16[512,256]{1,0:T(8,128)(2,1)S(1)}, bf16[512,256]{1,0:T(8,128)(2,1)S(1)}, u32[]{:S(2)}, u32[]{:S(2)}) collective-permute-start(bf16[512,256]{1,0:T(8,128)(2,1)S(1)} %get-tuple-element.176), channel_id=1, source_target_pairs={{1,0},{4,1},{7,2},{2,3},{5,4},{0,5},{3,6},{6,7},{9,8},{12,9},{15,1... | collective-permute-start | bytes 786440 | tf_op jit(solution)/shard_map/ppermute | solution.py:1331
  422.3 27.5 %collective-permute-start.62 = (bf16[320,256]{1,0:T(8,128)(2,1)S(1)}, bf16[320,256]{1,0:T(8,128)(2,1)S(1)}, u32[]{:S(2)}, u32[]{:S(2)}) collective-permute-start(bf16[320,256]{1,0:T(8,128)(2,1)S(1)} %get-tuple-element.183), channel_id=1, source_target_pairs={{0,1},{1,0},{2,3},{3,2},{4,5},{5,4},{6,7},{7,6},{8,9},{9,8},{10,11... | collective-permute-start | bytes 491528 | tf_op jit(solution)/shard_map/ppermute | solution.py:1031
  426.3 25.4 %collective-permute-start.63 = (bf16[320,256]{1,0:T(8,128)(2,1)S(1)}, bf16[320,256]{1,0:T(8,128)(2,1)S(1)}, u32[]{:S(2)}, u32[]{:S(2)}) collective-permute-start(bf16[320,256]{1,0:T(8,128)(2,1)S(1)} %get-tuple-element.184), channel_id=1, source_target_pairs={{0,2},{1,3},{2,4},{3,5},{4,6},{5,7},{6,0},{7,1},{8,10},{9,11},{10,... | collective-permute-start | bytes 491528 | tf_op jit(solution)/shard_map/ppermute | solution.py:1031
  435.2 21.6 %collective-permute-start.64 = (bf16[320,256]{1,0:T(8,128)(2,1)S(1)}, bf16[320,256]{1,0:T(8,128)(2,1)S(1)}, u32[]{:S(2)}, u32[]{:S(2)}) collective-permute-start(bf16[320,256]{1,0:T(8,128)(2,1)S(1)} %get-tuple-element.185), channel_id=1, source_target_pairs={{0,3},{1,2},{2,5},{3,4},{4,7},{5,6},{6,1},{7,0},{8,11},{9,10},{10,... | collective-permute-start | bytes 491528 | tf_op jit(solution)/shard_map/ppermute | solution.py:1031
  435.2 24.5 %collective-permute-start.65 = (bf16[320,256]{1,0:T(8,128)(2,1)S(1)}, bf16[320,256]{1,0:T(8,128)(2,1)S(1)}, u32[]{:S(2)}, u32[]{:S(2)}) collective-permute-start(bf16[320,256]{1,0:T(8,128)(2,1)S(1)} %get-tuple-element.186), channel_id=1, source_target_pairs={{0,4},{1,5},{2,6},{3,7},{4,0},{5,1},{6,2},{7,3},{8,12},{9,13},{10,... | collective-permute-start | bytes 491528 | tf_op jit(solution)/shard_map/ppermute | solution.py:1031
  449.8 42.8 %collective-permute-start.56 = (bf16[512,256]{1,0:T(8,128)(2,1)S(1)}, bf16[512,256]{1,0:T(8,128)(2,1)S(1)}, u32[]{:S(2)}, u32[]{:S(2)}) collective-permute-start(bf16[512,256]{1,0:T(8,128)(2,1)S(1)} %get-tuple-element.177), channel_id=1, source_target_pairs={{2,0},{5,1},{0,2},{3,3},{6,4},{1,5},{4,6},{7,7},{10,8},{13,9},{8,1... | collective-permute-start | bytes 786440 | tf_op jit(solution)/shard_map/ppermute | solution.py:1331
  451.7 23.5 %collective-permute-start.66 = (bf16[320,256]{1,0:T(8,128)(2,1)S(1)}, bf16[320,256]{1,0:T(8,128)(2,1)S(1)}, u32[]{:S(2)}, u32[]{:S(2)}) collective-permute-start(bf16[320,256]{1,0:T(8,128)(2,1)S(1)} %get-tuple-element.187), channel_id=1, source_target_pairs={{0,5},{1,4},{2,7},{3,6},{4,1},{5,0},{6,3},{7,2},{8,13},{9,12},{10,... | collective-permute-start | bytes 491528 | tf_op jit(solution)/shard_map/ppermute | solution.py:1031
  456.8 31.3 %collective-permute-start.67 = (bf16[320,256]{1,0:T(8,128)(2,1)S(1)}, bf16[320,256]{1,0:T(8,128)(2,1)S(1)}, u32[]{:S(2)}, u32[]{:S(2)}) collective-permute-start(bf16[320,256]{1,0:T(8,128)(2,1)S(1)} %get-tuple-element.188), channel_id=1, source_target_pairs={{0,6},{1,7},{2,0},{3,1},{4,2},{5,3},{6,4},{7,5},{8,14},{9,15},{10,... | collective-permute-start | bytes 491528 | tf_op jit(solution)/shard_map/ppermute | solution.py:1031
  459.6 28.5 %collective-permute-start.68 = (bf16[320,256]{1,0:T(8,128)(2,1)S(1)}, bf16[320,256]{1,0:T(8,128)(2,1)S(1)}, u32[]{:S(2)}, u32[]{:S(2)}) collective-permute-start(bf16[320,256]{1,0:T(8,128)(2,1)S(1)} %get-tuple-element.189), channel_id=1, source_target_pairs={{0,7},{1,6},{2,1},{3,0},{4,3},{5,2},{6,5},{7,4},{8,15},{9,14},{10,... | collective-permute-start | bytes 491528 | tf_op jit(solution)/shard_map/ppermute | solution.py:1031
  475.2 19.6 %collective-permute-start.31 = (bf16[128,2048]{1,0:T(8,128)(2,1)S(1)}, bf16[128,2048]{1,0:T(8,128)(2,1)S(1)}, u32[]{:S(2)}, u32[]{:S(2)}) collective-permute-start(bf16[128,2048]{1,0:T(8,128)(2,1)S(1)} %get-tuple-element.135), channel_id=1, source_target_pairs={{0,6},{2,0},{4,2},{6,4},{1,7},{3,1},{5,3},{7,5},{8,14},{10,8},{12,... | collective-permute-start | bytes 1572872 | tf_op jit(solution)/shard_map/ppermute | solution.py:349
  488.1 17.0 %collective-permute-start.32 = (bf16[128,2048]{1,0:T(8,128)(2,1)S(1)}, bf16[128,2048]{1,0:T(8,128)(2,1)S(1)}, u32[]{:S(2)}, u32[]{:S(2)}) collective-permute-start(bf16[128,2048]{1,0:T(8,128)(2,1)S(1)} %get-tuple-element.136), channel_id=1, source_target_pairs={{0,2},{2,4},{4,6},{6,0},{1,3},{3,5},{5,7},{7,1},{8,10},{10,12},{12... | collective-permute-start | bytes 1572872 | tf_op jit(solution)/shard_map/ppermute | solution.py:349
  488.1 23.5 %collective-permute-start.44 = (bf16[128,2048]{1,0:T(8,128)(2,1)S(1)}, bf16[128,2048]{1,0:T(8,128)(2,1)S(1)}, u32[]{:S(2)}, u32[]{:S(2)}) collective-permute-start(bf16[128,2048]{1,0:T(8,128)(2,1)S(1)} %get-tuple-element.157), channel_id=1, source_target_pairs={{0,6},{2,0},{4,2},{6,4},{1,7},{3,1},{5,3},{7,5},{8,14},{10,8},{12,... | collective-permute-start | bytes 1572872 | tf_op jit(solution)/shard_map/ppermute | solution.py:349
  492.6 34.5 %collective-permute-start.70 = (bf16[8,320,256]{2,1,0:T(8,128)(2,1)S(1)}, bf16[8,320,256]{2,1,0:T(8,128)(2,1)S(1)}, u32[]{:S(2)}, u32[]{:S(2)}) collective-permute-start(bf16[8,320,256]{2,1,0:T(8,128)(2,1)S(1)} %shard_map.283.p0), channel_id=1, source_target_pairs={{0,16},{16,0},{1,17},{17,1},{2,18},{18,2},{3,19},{19,3},{4,20},{20... | collective-permute-start | bytes 3932168 | tf_op jit(solution)/shard_map/ppermute | solution.py:349
  494.8 46.7 %collective-permute-start.74 = (bf16[1024,1024]{1,0:T(8,128)(2,1)S(1)}, bf16[1024,1024]{1,0:T(8,128)(2,1)S(1)}, u32[]{:S(2)}, u32[]{:S(2)}) collective-permute-start(bf16[1024,1024]{1,0:T(8,128)(2,1)S(1)} %shard_map.286.a), channel_id=1, source_target_pairs={{0,8},{8,0},{1,9},{9,1},{2,10},{10,2},{3,11},{11,3},{4,12},{12,4},... | collective-permute-start | bytes 6291464 | tf_op jit(solution)/shard_map/ppermute | solution.py:349
  505.0 22.1 %collective-permute-start.58 = (bf16[512,768]{1,0:T(8,128)(2,1)S(1)}, bf16[512,768]{1,0:T(8,128)(2,1)S(1)}, u32[]{:S(2)}, u32[]{:S(2)}) collective-permute-start(bf16[512,768]{1,0:T(8,128)(2,1)S(1)} %shard_map.279.p0), channel_id=1, source_target_pairs={{0,16},{16,0},{1,17},{17,1},{2,18},{18,2},{3,19},{19,3},{4,20},{20... | collective-permute-start | bytes 2359304 | tf_op jit(solution)/shard_map/ppermute | solution.py:349
  511.6 11.4 %collective-permute-start.45 = (bf16[128,2048]{1,0:T(8,128)(2,1)S(1)}, bf16[128,2048]{1,0:T(8,128)(2,1)S(1)}, u32[]{:S(2)}, u32[]{:S(2)}) collective-permute-start(bf16[128,2048]{1,0:T(8,128)(2,1)S(1)} %get-tuple-element.158), channel_id=1, source_target_pairs={{0,2},{2,4},{4,6},{6,0},{1,3},{3,5},{5,7},{7,1},{8,10},{10,12},{12... | collective-permute-start | bytes 1572872 | tf_op jit(solution)/shard_map/ppermute | solution.py:349
  511.6 29.8 %collective-permute-start.75 = (bf16[1024,1024]{1,0:T(8,128)(2,1)S(1)}, bf16[1024,1024]{1,0:T(8,128)(2,1)S(1)}, u32[]{:S(2)}, u32[]{:S(2)}) collective-permute-start(bf16[1024,1024]{1,0:T(8,128)(2,1)S(1)} %collective-permute-done.73.b), channel_id=1, source_target_pairs={{0,8},{8,0},{1,9},{9,1},{2,10},{10,2},{3,11},{11,3},{4,12},{12,4},... | collective-permute-start | bytes 6291464 | tf_op jit(solution)/shard_map/ppermute | solution.py:349
  (78 other events, 1041.2 us)
